TPU v7x, 512 devices: a whole 4x8x8 slice. The times are simulated.
512 devices in a mesh: dp: 64 (over y, z), factor: 8 (over x, core).
Axes of the slice: x: 4, y: 8, z: 8, core: 2. Of those that a mesh axis runs over, the one named last changes fastest.
Arguments:
- layer_inputs: bfloat16 [65536, 5120], P('dp', 'factor'), may hold values from -64 to 64
- out_grads: bfloat16 [65536, 5120], P('dp', 'factor'), may hold values from -64 to 64
- weight_grad: bfloat16 [5120, 5120], P('dp', 'factor'), may hold values from -32 to 32
- left_inv: float32 [5120, 5120], P('dp', 'factor'), may hold values from -4 to 10, as said below
- right_inv: float32 [5120, 5120], P('factor', 'dp'), may hold values from -4 to 10, as said below
Outputs:
- precond_grad: bfloat16 [5120, 5120], P('dp', 'factor')
- new_left: float32 [5120, 5120], P('dp', 'factor')
- new_right: float32 [5120, 5120], P('factor', 'dp')
Inputs may be any that keep to these rules, and one draw needn't show every extreme that they name: `left_inv`: symmetric and positive definite, every eigenvalue 0.1 or more. `right_inv`: symmetric and positive definite, every eigenvalue 0.1 or more.
All inputs are finite; a program needn't handle non-finite values.
Results may differ from a plain program's by a relative error of at most 0.00275.
The roundings to bfloat16 on the way count: a program that leaves them out, or rounds other values in their place, can miss the bound.
Values may be sent and summed in bfloat16 or wider, within the bound.
No kernel may reach another device: no remote copies, remote signals or barrier semaphores. Data moves between devices by JAX's collectives and lax.ppermute only.
A program may use at most 64 MiB of HBM per device.

v0:
```python
import jax
import jax.numpy as jnp
from jax import lax
from jax.sharding import PartitionSpec as P

decay = 0.9


def coefficient(quadratic):
    return (1.0 - decay) / (decay * decay * (1.0 + (1.0 - decay) / decay * quadratic))


def per_device(layer_inputs, out_grads, weight_grad, left_inv, right_inv):
    highest = lax.Precision.HIGHEST
    token_count = layer_inputs.shape[0] * lax.axis_size("dp")
    act_local = jnp.sum(layer_inputs, axis=0, dtype=jnp.float32)
    grad_local = jnp.sum(out_grads, axis=0, dtype=jnp.float32)
    act_sums, grad_sums = lax.psum((act_local, grad_local), "dp")
    mean_act = act_sums / token_count
    mean_grad = grad_sums / token_count
    whole_act, whole_grad = (
        lax.all_gather(mean_act, "factor", axis=0, tiled=True),
        lax.all_gather(mean_grad, "factor", axis=0, tiled=True),
    )
    left_rows, left_cols = left_inv.shape
    right_rows, right_cols = right_inv.shape
    data_index = lax.axis_index("dp")
    act_rows = lax.dynamic_slice_in_dim(whole_act, data_index * left_rows, left_rows)
    grad_cols = lax.dynamic_slice_in_dim(whole_grad, data_index * right_cols, right_cols)
    row_terms = jnp.dot(left_inv, mean_act, precision=highest)
    col_terms = jnp.dot(mean_grad, right_inv, precision=highest)
    left_image_rows, right_image_cols = lax.psum((row_terms, col_terms), "factor")
    left_partial = jnp.dot(act_rows, left_inv, precision=highest)
    right_partial = jnp.dot(right_inv, grad_cols, precision=highest)
    left_image_cols, right_image_rows = lax.psum((left_partial, right_partial), "dp")
    left_quad, right_quad = lax.psum(
        (jnp.sum(mean_act * left_image_cols), jnp.sum(mean_grad * right_image_rows)), "factor"
    )
    left_coef = coefficient(left_quad)
    right_coef = coefficient(right_quad)
    new_left = left_inv / decay - left_coef * left_image_rows[:, None] * left_image_cols[None, :]
    new_right = (
        right_inv / decay - right_coef * right_image_rows[:, None] * right_image_cols[None, :]
    )
    left_half = new_left.astype(jnp.bfloat16)
    right_half = new_right.astype(jnp.bfloat16)
    left_wide = lax.all_gather(left_half, "factor", axis=1, tiled=True)
    hidden_sum = jnp.dot(
        left_wide,
        lax.all_gather(weight_grad, "dp", axis=0, tiled=True),
        preferred_element_type=jnp.float32,
    )
    hidden = hidden_sum.astype(jnp.bfloat16)
    partial_terms = jnp.dot(
        hidden,
        lax.all_gather(right_half, "dp", axis=1, tiled=True),
        preferred_element_type=jnp.float32,
    )
    precond = lax.psum_scatter(partial_terms, "factor", scatter_dimension=1, tiled=True)
    return (precond.astype(jnp.bfloat16), new_left, new_right)


def solution(mesh):
    in_specs = (
        P("dp", "factor"),
        P("dp", "factor"),
        P("dp", "factor"),
        P("dp", "factor"),
        P("factor", "dp"),
    )
    out_specs = (P("dp", "factor"), P("dp", "factor"), P("factor", "dp"))
    return jax.shard_map(
        per_device, mesh=mesh, in_specs=in_specs, out_specs=out_specs, check_vma=False
    )
```

profile of v0, /device:TPU:1, one launch (start us, length us, event | category | flops | bytes accessed | tf_op | source)
XLA Modules:
  0.0 487.0 jit_solution(5599409717818635755)
XLA Ops:
  7.2 0.0 all-gather.5.cloned.1.call-start
  7.2 0.7 all-gather.5.cloned.1.call-update
  7.9 0.0 all-gather.7.cloned.1.call-start
  7.9 1.6 convert_reduce_fusion.1
  9.5 1.6 convert_reduce_fusion
  11.1 127.9 %all-reduce.1 = (f32[640]{0:T(1024)S(1)}, f32[640]{0:T(1024)S(1)}) all-reduce(f32[640]{0:T(1024)S(1)} %convert_reduce_fusion, f32[640]{0:T(1024)S(1)} %convert_reduce_fusion.1), channel_id=1, replica_groups=mesh['dp'=64,'factor'=8] {'dp'}, use_global_device_ids=true, to_apply=%region_7.0 | all-reduce | flops 1280 | bytes 10240 | tf_op jit(solution)/shard_map/psum | solution.py:18
  139.0 39.9 %all-gather = f32[8,1,640]{2,1,0:T(1,128)S(1)} all-gather(f32[1,1,640]{2,1,0:T(1,128)S(1)} %reshape.12), channel_id=1, replica_groups=mesh['dp'=64,'factor'=8] {'factor'}, dimensions={0}, use_global_device_ids=true | all-gather | bytes 23040 | tf_op jit(solution)/shard_map/all_gather | solution.py:22
  179.0 12.7 %all-gather.1 = f32[8,1,640]{2,1,0:T(1,128)S(1)} all-gather(f32[1,1,640]{2,1,0:T(1,128)S(1)} %reshape.14), channel_id=1, replica_groups=mesh['dp'=64,'factor'=8] {'factor'}, dimensions={0}, use_global_device_ids=true | all-gather | bytes 23040 | tf_op jit(solution)/shard_map/all_gather | solution.py:23
  191.7 1.2 convolution_reduce_fusion.1
  192.9 1.2 convolution_reduce_fusion
  194.1 112.3 %all-reduce = (f32[640]{0:T(1024)S(1)}, f32[640]{0:T(1024)S(1)}) all-reduce(f32[640]{0:T(1024)S(1)} %convolution_reduce_fusion, f32[640]{0:T(1024)S(1)} %convolution_reduce_fusion.1), channel_id=1, replica_groups=mesh['dp'=64,'factor'=8] {'dp'}, use_global_device_ids=true, to_apply=%region_8.0 | all-reduce | flops 1280 | bytes 10240 | tf_op jit(solution)/shard_map/psum | solution.py:35
  306.5 0.6 multiply_reduce_fusion
  307.1 1.2 convolution_bitcast_fusion
  308.2 1.2 convolution_bitcast_fusion.1
  309.5 40.3 %all-reduce.2 = (f32[80]{0:T(128)S(1)}, f32[]{:T(128)}, f32[80]{0:T(128)S(1)}, f32[]{:T(128)}) all-reduce(f32[80]{0:T(128)S(1)} %convolution_bitcast_fusion, f32[]{:T(128)} %get-tuple-element.15, f32[80]{0:T(128)S(1)} %convolution_bitcast_fusion.1, f32[]{:T(128)} %get-tuple-element.16), channel_id=1, replica_groups=mesh['dp'=64,'factor'=8] {'factor'}, use_global_device_ids=true, to_apply=%region_11.0 | all-reduce | flops 162 | bytes 1296 | tf_op jit(solution)/shard_map/psum | solution.py:32
  350.5 1.7 fusion.6
  352.2 0.0 all-gather.7.cloned.1.call-update
  352.2 0.0 reduce-scatter.2.cloned.1.call-start
  353.0 1.7 fusion.5
  354.7 14.2 %all_gather.16 = bf16[80,5120]{1,0:T(8,128)(2,1)S(1)} all-gather(bf16[80,640]{1,0:T(8,128)(2,1)S(1)} %get-tuple-element.11), channel_id=1, replica_groups=mesh['dp'=64,'factor'=8] {'factor'}, dimensions={1}, use_global_device_ids=true | all-gather | bytes 921600 | tf_op jit(solution)/shard_map/all_gather | solution.py:47
  368.8 0.0 all-gather.5.cloned.1.call-done
  368.8 66.5 %all-gather.7.cloned.1.call-done = bf16[640,5120]{0,1:T(8,128)(2,1)} async-done(((bf16[640,80]{0,1:T(8,128)(2,1)}), bf16[640,5120]{0,1:T(8,128)(2,1)}) %all-gather.7.cloned.1.call-update) | async-done | bytes 6553616 | tf_op jit(solution)/shard_map/all_gather | solution.py:56
  435.3 9.1 %fusion = f32[80,5120]{1,0:T(8,128)} fusion(bf16[640,5120]{0,1:T(8,128)(2,1)} %all-gather.7.cloned.1.call-done, bf16[80,5120]{1,0:T(8,128)(2,1)S(1)} %all_gather.16, bf16[5120,640]{1,0:T(8,128)(2,1)} %all-gather.5.cloned.1.call-done), kind=kOutput, calls=%fused_computation.7 | convolution fusion | flops 1048627200 | bytes 15564800 | tf_op jit(solution)/shard_map/dot_general | solution.py:54
  444.4 0.0 reduce-scatter.2.cloned.1.call-update
  444.4 34.4 %reduce-scatter.2.cloned.1.call-done = f32[80,640]{1,0:T(8,128)} async-done(((f32[80,5120]{1,0:T(8,128)}), f32[80,640]{1,0:T(8,128)}) %reduce-scatter.2.cloned.1.call-update) | async-done | bytes 204816 | tf_op jit(solution)/shard_map/reduce_scatter | solution.py:59
  478.9 1.6 convert_element_type.23
  (8 shorter events, 0.0 us)
Async XLA Ops:
  7.2 361.7 %all-gather.5.cloned.1.call-start = ((), (), s32[]{:S(2)}) async-start(), calls=%async_computation.1 | async-start | bytes 6656000 | tf_op jit(solution)/shard_map/all_gather | solution.py:50
  7.9 427.4 %all-gather.7.cloned.1.call-start = ((), (), s32[]{:S(2)}) async-start(), calls=%async_computation.2 | async-start | bytes 6656000 | tf_op jit(solution)/shard_map/all_gather | solution.py:56
  352.2 126.7 %reduce-scatter.2.cloned.1.call-start = ((), (), s32[]{:S(2)}) async-start(), calls=%async_computation.3 | async-start | bytes 1843200 | tf_op jit(solution)/shard_map/reduce_scatter | solution.py:59
Sparse Core Ops, SparseCore 0:
  11.0 97.8 all-gather.4
  352.4 82.9 all-gather.6
  444.6 34.2 reduce-scatter.1
where the time goes:
time: 488 us; the launch traced here: 487 us
  blocking collectives  347 us (71%)
  waiting for transfers between devices  102 us (21%)
  between operations  15.2 us (3%)
  matrix products  13.9 us (3%)
  other arithmetic  8.77 us (2%)
    psum x1, blocking collectives, per_device(): act_sums, grad_sums = lax.psum((act_local, grad_local), 'dp')  128 us
    psum x1, blocking collectives, per_device(): lax.psum((left_partial, right_partial), 'dp')  112 us
    all_gather x1, waiting for transfers between devices, per_device(): lax.all_gather(right_half, 'dp', axis=1, tiled=True)  66.5 us
    psum x1, blocking collectives, per_device(): lax.psum((row_terms, col_terms), 'factor')  40.3 us
    all_gather x1, blocking collectives, per_device(): lax.all_gather(mean_act, 'factor', axis=0, tiled=True)  39.9 us
    reduce_scatter x1, waiting for transfers between devices, per_device(): lax.psum_scatter(partial_terms, 'factor', scatter_dimension=1, tiled=True)  34.4 us
    all_gather x1, blocking collectives, per_device(): left_wide = lax.all_gather(left_half, 'factor', axis=1, tiled=True)  14.2 us
    all_gather x1, blocking collectives, per_device(): lax.all_gather(mean_grad, 'factor', axis=0, tiled=True)  12.7 us
  transfers between devices with their start and end apart: 3, of which 2 were waited for; matrix products, arithmetic and copies ran while one was open for 2% of the time, Pallas kernels for 0%

commit v1 on v0

v1 whole, which is shorter than its diff:
```python
import jax
import jax.numpy as jnp
from jax import lax
from jax.sharding import Mesh, PartitionSpec as P

decay = 0.9
PAD = 104


def coefficient(quadratic):
    return (1.0 - decay) / (decay * decay * (1.0 + (1.0 - decay) / decay * quadratic))


def share(vec, axes, count):
    return lax.all_to_all(jnp.broadcast_to(vec[None], (count,) + vec.shape), axes, 0, 0, tiled=True)


def gather_rows(block, axis, count):
    rows, cols = block.shape
    padded = jnp.pad(block, ((0, PAD - rows), (0, 0)))
    whole = lax.all_gather(padded, axis, axis=0, tiled=False)
    return whole[:, :rows, :].reshape(count * rows, cols)


def per_device(layer_inputs, out_grads, weight_grad, left_inv, right_inv):
    ny, nz, nf = lax.axis_size("y"), lax.axis_size("z"), lax.axis_size("f")
    token_count = layer_inputs.shape[0] * ny * nz
    rows, cols = left_inv.shape
    y, z, f = lax.axis_index("y"), lax.axis_index("z"), lax.axis_index("f")

    left_wide = lax.all_gather(left_inv, "y", axis=0, tiled=True)
    swap = [(a * nf + b, b * nf + a) for a in range(ny) for b in range(nf)]
    weight_piece = lax.ppermute(weight_grad, ("y", "f"), swap)

    act_local = jnp.sum(layer_inputs, axis=0, dtype=jnp.float32)
    grad_local = jnp.sum(out_grads, axis=0, dtype=jnp.float32)
    sums = share(jnp.concatenate([act_local, grad_local]), ("y", "z"), ny * nz)
    means = jnp.sum(sums, axis=0) / token_count
    mean_act, mean_grad = means[:cols], means[cols:]

    weight_piece, means = lax.optimization_barrier((weight_piece, means))
    weight_block = gather_rows(weight_piece, "z", nz)

    left_partial = jnp.sum(left_inv * means[None, :cols], axis=1)
    right_partial = jnp.sum(right_inv * means[cols:, None], axis=0)
    both = share(jnp.concatenate([means, left_partial, right_partial]), "f", nf)
    whole_act = both[:, :cols].reshape(nf * cols)
    whole_grad = both[:, cols : 2 * cols].reshape(nf * cols)
    images = jnp.sum(both[:, 2 * cols :], axis=0)

    all_images = share(images, ("y", "z"), ny * nz)
    left_image = all_images[:, :rows].reshape(ny * nz * rows)
    right_image = all_images[:, rows:].reshape(ny * nz * rows)
    left_coef = coefficient(jnp.sum(whole_act * left_image))
    right_coef = coefficient(jnp.sum(whole_grad * right_image))

    left_cols = lax.dynamic_slice_in_dim(left_image, f * cols, cols)
    right_rows = lax.dynamic_slice_in_dim(right_image, f * cols, cols)
    new_left = left_inv / decay - left_coef * images[:rows, None] * left_cols[None, :]
    new_right = right_inv / decay - right_coef * right_rows[:, None] * images[None, rows:]

    right_block = gather_rows(new_right.astype(jnp.bfloat16).T, "z", nz)

    wide_rows = lax.dynamic_slice_in_dim(left_image.reshape(ny, nz, rows), z, 1, 1).reshape(ny * rows)
    left_block = left_wide / decay - left_coef * wide_rows[:, None] * left_cols[None, :]
    partial = jnp.dot(
        left_block.astype(jnp.bfloat16), weight_block, preferred_element_type=jnp.float32
    )
    pieces = lax.all_to_all(partial.reshape(nf, ny * rows // nf, cols), "f", 0, 0, tiled=True)
    hidden_piece = jnp.sum(pieces, axis=0).astype(jnp.bfloat16)
    hidden = lax.all_gather(hidden_piece, "f", axis=0, tiled=True)

    partial = jnp.dot(hidden, right_block, preferred_element_type=jnp.float32)
    pieces = lax.all_to_all(partial.reshape(ny, rows, cols), "y", 0, 0, tiled=True)
    precond = jnp.sum(pieces, axis=0).astype(jnp.bfloat16)
    return (precond, new_left, new_right)


def solution(mesh):
    cube = Mesh(mesh.devices.reshape(8, 8, 8), ("y", "z", "f"))
    rows, cols = P(("y", "z"), "f"), P("f", ("y", "z"))
    return jax.shard_map(
        per_device,
        mesh=cube,
        in_specs=(rows, rows, rows, rows, cols),
        out_specs=(rows, rows, cols),
        check_vma=False,
    )
```

time: 488 us -> 245 us (0.50)
  blocking collectives: 347 us -> 35.5 us
  starting transfers between devices: 0.12 us -> 42.5 us
  waiting for transfers between devices: 102 us -> 134 us
  matrix products: 13.9 us -> 4.14 us
  local copies, waits for them, and re-layouts: 0.01 us -> 6 us
    psum x3 -> x0, blocking collectives: 281 us -> none  [the longest x1 128 us: per_device(): act_sums, grad_sums = lax.psum((act_local, grad_local), 'dp')]
    all_to_all x0 -> x4, waiting for transfers between devices: none -> 61.9 us  [the longest x1 41.1 us: per_device(): lax.all_to_all(partial.reshape(ny, rows, cols), 'y', 0, 0, tiled=True)]
    all_gather x3 -> x1, blocking collectives: 66.8 us -> 18.7 us  [per_device(): hidden = lax.all_gather(hidden_piece, 'f', axis=0, tiled=True)]
    all_to_all x0 -> x4, starting transfers between devices: none -> 38.3 us  [the longest x2 22.8 us: share(): lax.all_to_all(jnp.broadcast_to(vec[None], (count,) + vec.shape), axes, 0...]
    reduce_scatter x1 -> x0, waiting for transfers between devices: 34.4 us -> none  [per_device(): lax.psum_scatter(partial_terms, 'factor', scatter_dimension=1, tiled=True)]
    all_to_all x0 -> x1, blocking collectives: none -> 16.8 us  [share(): lax.all_to_all(jnp.broadcast_to(vec[None], (count,) + vec.shape), axes, 0...]
    dot_general x5 -> x2, matrix products: 13.9 us -> 4.14 us  [the longest x1 2.08 us: per_device(): jnp.dot(left_block.astype(jnp.bfloat16), weight_block, preferred_element_...]
    all_gather x2 -> x3, waiting for transfers between devices: 66.5 us -> 70.9 us  [the longest x1 41.1 us: per_device(): left_wide = lax.all_gather(left_inv, 'y', axis=0, tiled=True)]
  transfers between devices with their start and end apart: 3 -> 8, of which waited for: 2 -> 5; matrix products, arithmetic and copies ran while one was open for 2% -> 4% of each run, Pallas kernels for 0% -> 0%
where the time goes in v1:
time: 245 us; the launch traced here: 244 us
  waiting for transfers between devices  134 us (55%)
  starting transfers between devices  42.5 us (17%)
  blocking collectives  35.5 us (14%)
  between operations  15.3 us (6%)
  other arithmetic  7.46 us (3%)
  local copies, waits for them, and re-layouts  6 us (2%)
  matrix products  4.14 us (2%)
    all_to_all x1, waiting for transfers between devices, per_device(): lax.all_to_all(partial.reshape(ny, rows, cols), 'y', 0, 0, tiled=True)  41.1 us
    all_gather x1, waiting for transfers between devices, per_device(): left_wide = lax.all_gather(left_inv, 'y', axis=0, tiled=True)  41.1 us
    all_gather x2, waiting for transfers between devices, gather_rows(): whole = lax.all_gather(padded, axis, axis=0, tiled=False)  29.8 us
    all_to_all x2, starting transfers between devices, share(): lax.all_to_all(jnp.broadcast_to(vec[None], (count,) + vec.shape), axes, 0...  22.8 us
    all_to_all x2, waiting for transfers between devices, share(): lax.all_to_all(jnp.broadcast_to(vec[None], (count,) + vec.shape), axes, 0...  20.8 us
    all_gather x1, blocking collectives, per_device(): hidden = lax.all_gather(hidden_piece, 'f', axis=0, tiled=True)  18.7 us
    all_to_all x1, blocking collectives, share(): lax.all_to_all(jnp.broadcast_to(vec[None], (count,) + vec.shape), axes, 0...  16.8 us
    all_to_all x1, starting transfers between devices, per_device(): lax.all_to_all(partial.reshape(nf, ny * rows // nf, cols), 'f', 0, 0, til...  9.13 us
  transfers between devices with their start and end apart: 8, of which 5 were waited for; matrix products, arithmetic and copies ran while one was open for 4% of the time, Pallas kernels for 0%

profile of v1, /device:TPU:1, one launch (start us, length us, event | category | flops | bytes accessed | tf_op | source)
XLA Modules:
  0.0 244.4 jit_solution(15196800060828398383)
XLA Ops:
  7.2 2.2 convert_reduce_fusion
  9.4 0.9 broadcast_in_dim.6
  10.3 17.1 %all-to-all-start = ((f32[64,1,1280]{2,1,0:T(1,128)}), f32[64,1,1280]{2,1,0:T(1,128)S(1)}, u32[]{:S(2)}, u32[]{:S(2)}) async-start(f32[64,1,1280]{2,1,0:T(1,128)} %broadcast_in_dim.6), calls=%async_computation | async-start | bytes 655360 | tf_op jit(solution)/shard_map/all_to_all | solution.py:15
  27.4 0.0 all-gather.8.cloned.1.call-start
  27.4 4.0 %collective-permute-start = (bf16[80,640]{1,0:T(8,128)(2,1)S(1)}, bf16[80,640]{1,0:T(8,128)(2,1)S(1)}, u32[]{:S(2)}, u32[]{:S(2)}) collective-permute-start(bf16[80,640]{1,0:T(8,128)(2,1)S(1)} %copy-done.2), channel_id=1, source_target_pairs={{0,0},{1,64},{2,128},{3,192},{4,256},{5,320},{6,384},{7,448},{64,1... | collective-permute-start | bytes 307208 | tf_op jit(solution)/shard_map/ppermute | solution.py:33
  31.5 9.7 %all-to-all-done = f32[64,1,1280]{2,1,0:T(1,128)S(1)} async-done(((f32[64,1,1280]{2,1,0:T(1,128)}), f32[64,1,1280]{2,1,0:T(1,128)S(1)}, u32[]{:S(2)}, u32[]{:S(2)}) %all-to-all-start) | async-done | bytes 327712 | tf_op jit(solution)/shard_map/all_to_all | solution.py:15
  41.2 0.2 reduce_sum.92
  41.5 0.7 pad.7
  42.1 0.0 all-gather.8.cloned.1.call-update
  42.2 0.0 all-gather.6.cloned.1.call-start
  42.2 0.7 all-gather.6.cloned.1.call-update
  42.9 0.1 multiply_reduce_fusion.1
  43.1 0.1 multiply_reduce_fusion
  43.2 0.1 concatenate.7
  43.3 16.8 %all_to_all.34 = f32[8,1,1440]{2,1,0:T(1,128)S(1)} all-to-all(f32[8,1,1440]{2,1,0:T(1,128)S(1)} %broadcast_in_dim.7), channel_id=1, replica_groups=mesh['y'=8,'z'=8,'f'=8] {'f'}, dimensions={0} | all-to-all | bytes 92160 | tf_op jit(solution)/shard_map/all_to_all | solution.py:15
  60.1 0.7 broadcast_in_dim.8
  60.8 5.6 %all-to-all-start.2 = ((f32[64,1,160]{2,1,0:T(1,128)}), f32[64,1,160]{2,1,0:T(1,128)S(1)}, u32[]{:S(2)}, u32[]{:S(2)}) async-start(f32[64,1,160]{2,1,0:T(1,128)} %broadcast_in_dim.8), calls=%async_computation.2 | async-start | bytes 131072 | tf_op jit(solution)/shard_map/all_to_all | solution.py:15
  66.4 0.0 all-gather.10.cloned.1.call-start
  66.5 11.1 %all-to-all-done.2 = f32[64,1,160]{2,1,0:T(1,128)S(1)} async-done(((f32[64,1,160]{2,1,0:T(1,128)}), f32[64,1,160]{2,1,0:T(1,128)S(1)}, u32[]{:S(2)}, u32[]{:S(2)}) %all-to-all-start.2) | async-done | bytes 40992 | tf_op jit(solution)/shard_map/all_to_all | solution.py:15
  77.5 0.1 fusion.2
  77.6 0.1 reshape.66
  77.7 0.1 reshape.65
  77.8 0.1 reshape.68
  77.9 0.1 reshape.69
  78.0 0.6 fusion
  79.3 0.1 mul.116
  80.1 0.1 dynamic_slice.10
  80.1 0.1 dynamic-slice_multiply_fusion
  80.2 0.1 slice_multiply_fusion.2
  80.3 0.8 convert_bitcast_fusion
  81.1 0.7 pad.8
  81.7 0.0 all-gather.10.cloned.1.call-update
  81.8 0.0 all-gather.8.cloned.1.call-done
  81.8 1.2 slice.47
  83.0 41.1 %all-gather.6.cloned.1.call-done = f32[640,640]{1,0:T(8,128)} async-done(((f32[80,640]{1,0:T(8,128)}), f32[640,640]{1,0:T(8,128)}) %all-gather.6.cloned.1.call-update) | async-done | bytes 1638416 | tf_op jit(solution)/shard_map/all_gather | solution.py:31
  124.1 1.7 subtract_convert_fusion
  125.8 2.1 fusion.4
  127.8 9.1 %all-to-all-start.3 = ((f32[8,80,640]{2,1,0:T(8,128)}), f32[8,80,640]{2,1,0:T(8,128)S(1)}, u32[]{:S(2)}, u32[]{:S(2)}) async-start(f32[8,80,640]{2,1,0:T(8,128)} %fusion.4), calls=%async_computation.3 | async-start | bytes 3276800 | tf_op jit(solution)/shard_map/all_to_all | solution.py:69
  137.0 29.8 %all-gather.10.cloned.1.call-done = bf16[832,640]{1,0:T(8,128)(2,1)} async-done(((bf16[104,640]{1,0:T(8,128)(2,1)}), bf16[832,640]{1,0:T(8,128)(2,1)}) %all-gather.10.cloned.1.call-update) | async-done | bytes 1064976 | tf_op jit(solution)/shard_map/all_gather | solution.py:21
  166.8 1.2 slice.50
  168.0 0.0 all-to-all-done.3
  168.0 0.1 reduce_sum.97
  168.1 18.7 %all_gather.21 = bf16[640,640]{1,0:T(8,128)(2,1)S(1)} all-gather(bf16[80,640]{1,0:T(8,128)(2,1)S(1)} %reduce_sum.97), channel_id=1, replica_groups=mesh['y'=8,'z'=8,'f'=8] {'f'}, dimensions={0}, use_global_device_ids=true | all-gather | bytes 921600 | tf_op jit(solution)/shard_map/all_gather | solution.py:71
  186.8 2.1 fusion.5
  188.9 6.5 %all-to-all-start.4 = ((f32[8,80,640]{2,1,0:T(8,128)}), f32[8,80,640]{2,1,0:T(8,128)S(1)}, u32[]{:S(2)}, u32[]{:S(2)}) async-start(f32[8,80,640]{2,1,0:T(8,128)} %fusion.5), calls=%async_computation.4 | async-start | bytes 3276800 | tf_op jit(solution)/shard_map/all_to_all | solution.py:74
  195.3 0.8 multiply_subtract_fusion
  196.1 41.1 %all-to-all-done.4 = f32[8,80,640]{2,1,0:T(8,128)S(1)} async-done(((f32[8,80,640]{2,1,0:T(8,128)}), f32[8,80,640]{2,1,0:T(8,128)S(1)}, u32[]{:S(2)}, u32[]{:S(2)}) %all-to-all-start.4) | async-done | bytes 1638432 | tf_op jit(solution)/shard_map/all_to_all | solution.py:74
  237.2 0.7 reduce_sum.99
  (15 shorter events, 0.1 us)
Async XLA Ops:
  7.2 20.3 %copy-start.2 = (bf16[80,640]{1,0:T(8,128)(2,1)S(1)}, bf16[80,640]{1,0:T(8,128)(2,1)}, u32[]{:S(2)}) copy-start(bf16[80,640]{1,0:T(8,128)(2,1)} %param.7) | copy-start | bytes 307204
  7.2 35.8 %copy-start = (f32[80,640]{1,0:T(8,128)S(1)}, f32[80,640]{1,0:T(8,128)}, u32[]{:S(2)}) copy-start(f32[80,640]{1,0:T(8,128)} %param.8) | copy-start | bytes 614404
  9.4 33.7 %copy-start.1 = (f32[640,80]{0,1:T(8,128)S(1)}, f32[640,80]{0,1:T(8,128)}, u32[]{:S(2)}) copy-start(f32[640,80]{0,1:T(8,128)} %param.9) | copy-start | bytes 614404
  10.3 31.0 %all-to-all-start = ((f32[64,1,1280]{2,1,0:T(1,128)}), f32[64,1,1280]{2,1,0:T(1,128)S(1)}, u32[]{:S(2)}, u32[]{:S(2)}) async-start(f32[64,1,1280]{2,1,0:T(1,128)} %broadcast_in_dim.6), calls=%async_computation | async-start | bytes 655360 | tf_op jit(solution)/shard_map/all_to_all | solution.py:15
  27.4 54.4 %all-gather.8.cloned.1.call-start = ((), (), s32[]{:S(2)}) async-start(), calls=%async_computation.6 | async-start | bytes 1198080 | tf_op jit(solution)/shard_map/all_gather | solution.py:21
  27.4 14.0 %collective-permute-start = (bf16[80,640]{1,0:T(8,128)(2,1)S(1)}, bf16[80,640]{1,0:T(8,128)(2,1)S(1)}, u32[]{:S(2)}, u32[]{:S(2)}) collective-permute-start(bf16[80,640]{1,0:T(8,128)(2,1)S(1)} %copy-done.2), channel_id=1, source_target_pairs={{0,0},{1,64},{2,128},{3,192},{4,256},{5,320},{6,384},{7,448},{64,1... | collective-permute-start | bytes 307208 | tf_op jit(solution)/shard_map/ppermute | solution.py:33
  42.2 81.9 %all-gather.6.cloned.1.call-start = ((), (), s32[]{:S(2)}) async-start(), calls=%async_computation.5 | async-start | bytes 1843200 | tf_op jit(solution)/shard_map/all_gather | solution.py:31
  60.8 16.8 %all-to-all-start.2 = ((f32[64,1,160]{2,1,0:T(1,128)}), f32[64,1,160]{2,1,0:T(1,128)S(1)}, u32[]{:S(2)}, u32[]{:S(2)}) async-start(f32[64,1,160]{2,1,0:T(1,128)} %broadcast_in_dim.8), calls=%async_computation.2 | async-start | bytes 131072 | tf_op jit(solution)/shard_map/all_to_all | solution.py:15
  66.4 100.3 %all-gather.10.cloned.1.call-start = ((), (), s32[]{:S(2)}) async-start(), calls=%async_computation.7 | async-start | bytes 1198080 | tf_op jit(solution)/shard_map/all_gather | solution.py:21
  127.8 40.1 %all-to-all-start.3 = ((f32[8,80,640]{2,1,0:T(8,128)}), f32[8,80,640]{2,1,0:T(8,128)S(1)}, u32[]{:S(2)}, u32[]{:S(2)}) async-start(f32[8,80,640]{2,1,0:T(8,128)} %fusion.4), calls=%async_computation.3 | async-start | bytes 3276800 | tf_op jit(solution)/shard_map/all_to_all | solution.py:69
  188.9 48.3 %all-to-all-start.4 = ((f32[8,80,640]{2,1,0:T(8,128)}), f32[8,80,640]{2,1,0:T(8,128)S(1)}, u32[]{:S(2)}, u32[]{:S(2)}) async-start(f32[8,80,640]{2,1,0:T(8,128)} %fusion.5), calls=%async_computation.4 | async-start | bytes 3276800 | tf_op jit(solution)/shard_map/all_to_all | solution.py:74
Sparse Core Ops, SparseCore 0:
  42.3 38.8 all-gather.7
  83.2 40.7 all-gather.5
  126.2 40.5 all-gather.9

commit v2 on v1

v2 whole, which is shorter than its diff:
```python
import jax
import jax.numpy as jnp
from jax import lax
from jax.sharding import Mesh, PartitionSpec as P


decay = 0.9
Y = ("u", "v")
F = ("x", "c")
DP = ("u", "v", "z")


def coefficient(quadratic):
    return (1.0 - decay) / (decay * decay * (1.0 + (1.0 - decay) / decay * quadratic))


def share(vec, axes):
    count = lax.axis_size(axes)
    return lax.all_to_all(jnp.broadcast_to(vec[None], (count,) + vec.shape), axes, 0, 0, tiled=True)


def per_device(layer_inputs, out_grads, weight_grad, left_inv, right_inv):
    ny, nz, nf, nx = lax.axis_size(Y), lax.axis_size("z"), lax.axis_size(F), lax.axis_size("x")
    nu = lax.axis_size("u")
    token_count = layer_inputs.shape[0] * ny * nz
    rows, cols = left_inv.shape
    half = rows // 2
    u, v, z, f = lax.axis_index("u"), lax.axis_index("v"), lax.axis_index("z"), lax.axis_index(F)

    left_wide = lax.all_gather(left_inv, Y, axis=0, tiled=False)
    swap = [(a * nf + b, b * nf + a) for a in range(ny) for b in range(nf)]
    weight_piece = lax.ppermute(weight_grad, Y + F, swap)
    right_rows_own = right_inv.T
    right_other = lax.ppermute(right_rows_own, "v", [(0, 1), (1, 0)])
    right_pair = jnp.concatenate([right_rows_own[None], right_other[None]], axis=0)

    act_local = jnp.sum(layer_inputs, axis=0, dtype=jnp.float32)
    grad_local = jnp.sum(out_grads, axis=0, dtype=jnp.float32)
    sums = share(jnp.concatenate([act_local, grad_local]), DP)
    means = jnp.sum(sums, axis=0) / token_count

    weight_piece, right_pair, means = lax.optimization_barrier((weight_piece, right_pair, means))
    weight_block = share(weight_piece, "z").reshape(nz * rows, cols)
    right_wide = lax.all_gather(right_pair, "z", axis=0, tiled=False)

    left_partial = jnp.sum(left_inv * means[None, :cols], axis=1)
    right_partial = jnp.sum(right_inv * means[cols:, None], axis=0)
    both = share(jnp.concatenate([means, left_partial, right_partial]), F)
    whole_act = both[:, :cols].reshape(nf * cols)
    whole_grad = both[:, cols : 2 * cols].reshape(nf * cols)
    images = jnp.sum(both[:, 2 * cols :], axis=0)
    all_images = share(images, DP)
    left_image = all_images[:, :rows].reshape(ny * nz * rows)
    right_image = all_images[:, rows:].reshape(ny * nz * rows)
    left_coef = coefficient(jnp.sum(whole_act * left_image))
    right_coef = coefficient(jnp.sum(whole_grad * right_image))

    left_cols = lax.dynamic_slice_in_dim(left_image, f * cols, cols)
    right_cols = lax.dynamic_slice_in_dim(right_image, f * cols, cols)

    wide_image = lax.dynamic_slice_in_dim(left_image.reshape(ny, nz, rows), z, 1, 1)
    left_block = left_wide / decay - (left_coef * wide_image.reshape(ny, rows, 1)) * left_cols
    left_half = left_block.astype(jnp.bfloat16).reshape(nx, 2, 2, half, cols)
    left_half = left_half.transpose(0, 2, 1, 3, 4).reshape(ny * rows, cols)
    partial = jnp.dot(left_half, weight_block, preferred_element_type=jnp.float32)
    pieces = lax.all_to_all(partial.reshape(nf, 2, half, cols), F, 0, 0, tiled=True)
    hidden_piece = jnp.sum(pieces, axis=0).astype(jnp.bfloat16)
    hidden_piece = lax.all_to_all(hidden_piece, "v", 0, 0, tiled=True)
    hidden_piece = hidden_piece.transpose(1, 0, 2).reshape(half, 2 * cols)
    hidden = lax.all_gather(hidden_piece, F, axis=0, tiled=True)

    pair_image = lax.dynamic_slice_in_dim(right_image.reshape(nu, 2, nz, rows), u, 1, 0)[0]
    right_sorted = jnp.where(v == 0, right_wide, right_wide[:, ::-1]).transpose(1, 0, 2, 3)
    right_block = right_sorted / decay - (right_coef * pair_image[..., None]) * right_cols
    right_half = right_block.astype(jnp.bfloat16).reshape(2 * nz * rows, cols)
    partial = jnp.dot(hidden, right_half, preferred_element_type=jnp.float32)
    pieces = lax.all_to_all(partial.reshape(nu, rows, cols), "u", 0, 0, tiled=True)
    precond = jnp.sum(pieces, axis=0).astype(jnp.bfloat16)

    new_left = left_inv / decay - left_coef * images[:rows, None] * left_cols[None, :]
    new_right = right_inv / decay - right_coef * right_cols[:, None] * images[None, rows:]
    return (precond, new_left, new_right)


def solution(mesh):
    cube = Mesh(mesh.devices.reshape(4, 2, 8, 4, 2), ("u", "v", "z", "x", "c"))
    rows, cols = P(DP, F), P(F, DP)

    return jax.shard_map(
        per_device,
        mesh=cube,
        in_specs=(rows, rows, rows, rows, cols),
        out_specs=(rows, rows, cols),
        check_vma=False,
    )
```

time: 245 us -> 216 us (0.88)
  waiting for transfers between devices: 134 us -> 89.2 us
  blocking collectives: 35.5 us -> 51 us
  other arithmetic: 7.46 us -> 12.5 us
  local copies, waits for them, and re-layouts: 6 us -> 2.77 us
  starting transfers between devices: 42.5 us -> 39.9 us
    all_gather x3 -> x2, waiting for transfers between devices: 70.9 us -> 0.02 us  [the longest x1 0.02 us: per_device(): left_wide = lax.all_gather(left_inv, Y, axis=0, tiled=False)]
    all_to_all x1 -> x2, blocking collectives: 16.8 us -> 35.6 us  [share(): lax.all_to_all(jnp.broadcast_to(vec[None], (count,) + vec.shape), axes, 0...]
    ppermute x1 -> x2, waiting for transfers between devices: 0.01 us -> 16.8 us  [the longest x1 12.7 us: per_device(): right_other = lax.ppermute(right_rows_own, 'v', [(0, 1), (1, 0)])]
    all_to_all x2, waiting for transfers between devices: 20.8 us -> 28.5 us  [share(): lax.all_to_all(jnp.broadcast_to(vec[None], (count,) + vec.shape), axes, 0...]
    all_gather x1, blocking collectives: 18.7 us -> 15.4 us  [per_device(): hidden = lax.all_gather(hidden_piece, F, axis=0, tiled=True)]
    all_to_all x2 -> x3, starting transfers between devices: 15.6 us -> 12.8 us  [the longest x1 5.92 us: per_device(): lax.all_to_all(partial.reshape(nf, 2, half, cols), F, 0, 0, tiled=True)]
    ppermute x1 -> x2, starting transfers between devices: 4.04 us -> 6.4 us  [the longest x1 3.48 us: per_device(): weight_piece = lax.ppermute(weight_grad, Y + F, swap)]
    all_to_all x2 -> x3, waiting for transfers between devices: 41.1 us -> 43.1 us  [the longest x1 20.5 us: per_device(): lax.all_to_all(partial.reshape(nf, 2, half, cols), F, 0, 0, tiled=True)]
  transfers between devices with their start and end apart: 8 -> 9, of which waited for: 5 -> 6; matrix products, arithmetic and copies ran while one was open for 4% -> 6% of each run, Pallas kernels for 0% -> 0%
where the time goes in v2:
time: 216 us; the launch traced here: 215 us
  waiting for transfers between devices  89.2 us (41%)
  blocking collectives  51 us (24%)
  starting transfers between devices  39.9 us (18%)
  between operations  15.7 us (7%)
  other arithmetic  12.5 us (6%)
  matrix products  3.82 us (2%)
  local copies, waits for them, and re-layouts  2.77 us (1%)
    all_to_all x2, blocking collectives, share(): lax.all_to_all(jnp.broadcast_to(vec[None], (count,) + vec.shape), axes, 0...  35.6 us
    all_to_all x2, waiting for transfers between devices, share(): lax.all_to_all(jnp.broadcast_to(vec[None], (count,) + vec.shape), axes, 0...  28.5 us
    all_to_all x2, starting transfers between devices, share(): lax.all_to_all(jnp.broadcast_to(vec[None], (count,) + vec.shape), axes, 0...  20.7 us
    all_to_all x1, waiting for transfers between devices, per_device(): lax.all_to_all(partial.reshape(nf, 2, half, cols), F, 0, 0, tiled=True)  20.5 us
    all_to_all x1, waiting for transfers between devices, per_device(): lax.all_to_all(partial.reshape(nu, rows, cols), 'u', 0, 0, tiled=True)  19.6 us
    all_gather x1, blocking collectives, per_device(): hidden = lax.all_gather(hidden_piece, F, axis=0, tiled=True)  15.4 us
    ppermute x1, waiting for transfers between devices, per_device(): right_other = lax.ppermute(right_rows_own, 'v', [(0, 1), (1, 0)])  12.7 us
    all_to_all x1, starting transfers between devices, per_device(): lax.all_to_all(partial.reshape(nf, 2, half, cols), F, 0, 0, tiled=True)  5.92 us
  transfers between devices with their start and end apart: 9, of which 6 were waited for; matrix products, arithmetic and copies ran while one was open for 6% of the time, Pallas kernels for 0%

profile of v2, /device:TPU:1, one launch (start us, length us, event | category | flops | bytes accessed | tf_op | source)
XLA Modules:
  0.0 214.8 jit_solution(3452530748583266782)
XLA Ops:
  7.2 0.0 all-gather.5.cloned.1.call-start
  7.2 0.7 all-gather.5.cloned.1.call-update
  7.9 2.2 %convert_reduce_fusion = (f32[640]{0:T(1024)S(1)}, f32[640]{0:T(1024)S(1)}) fusion(bf16[1024,640]{1,0:T(8,128)(2,1)} %param.6, bf16[1024,640]{1,0:T(8,128)(2,1)} %param.5), kind=kLoop, calls=%fused_computation.5 | loop fusion | flops 2620160 | bytes 2626560 | tf_op jit(solution)/shard_map/reduce_sum | solution.py:38
  10.1 0.9 broadcast_in_dim.14
  11.0 17.1 %all-to-all-start = ((f32[64,1,1280]{2,1,0:T(1,128)}), f32[64,1,1280]{2,1,0:T(1,128)S(1)}, u32[]{:S(2)}, u32[]{:S(2)}) async-start(f32[64,1,1280]{2,1,0:T(1,128)} %broadcast_in_dim.14), calls=%async_computation | async-start | bytes 655360 | tf_op jit(solution)/shard_map/all_to_all | solution.py:19
  28.2 0.0 all-gather.7.cloned.1.call-start
  28.2 2.9 %collective-permute-start.1 = (f32[80,640]{1,0:T(8,128)S(1)}, f32[80,640]{1,0:T(8,128)S(1)}, u32[]{:S(2)}, u32[]{:S(2)}) collective-permute-start(f32[80,640]{1,0:T(8,128)S(1)} %bitcast.47), channel_id=1, source_target_pairs={{0,64},{64,0},{1,65},{65,1},{2,66},{66,2},{3,67},{67,3},{4,68},{68... | collective-permute-start | bytes 614408 | tf_op jit(solution)/shard_map/ppermute | solution.py:34
  31.2 3.5 %collective-permute-start = (bf16[80,640]{1,0:T(8,128)(2,1)S(1)}, bf16[80,640]{1,0:T(8,128)(2,1)S(1)}, u32[]{:S(2)}, u32[]{:S(2)}) collective-permute-start(bf16[80,640]{1,0:T(8,128)(2,1)S(1)} %copy-done.2), channel_id=1, source_target_pairs={{0,0},{1,64},{2,128},{3,192},{4,256},{5,320},{6,384},{7,448},{64,1... | collective-permute-start | bytes 307208 | tf_op jit(solution)/shard_map/ppermute | solution.py:32
  34.6 12.7 %collective-permute-done.1 = f32[80,640]{1,0:T(8,128)S(1)} collective-permute-done((f32[80,640]{1,0:T(8,128)S(1)}, f32[80,640]{1,0:T(8,128)S(1)}, u32[]{:S(2)}, u32[]{:S(2)}) %collective-permute-start.1) | collective-permute-done | bytes 204832 | tf_op jit(solution)/shard_map/ppermute | solution.py:34
  47.4 0.8 pad_maximum_fusion
  48.2 0.2 reduce_sum.92
  48.4 4.1 %collective-permute-done = bf16[80,640]{1,0:T(8,128)(2,1)S(1)} collective-permute-done((bf16[80,640]{1,0:T(8,128)(2,1)S(1)}, bf16[80,640]{1,0:T(8,128)(2,1)S(1)}, u32[]{:S(2)}, u32[]{:S(2)}) %collective-permute-start) | collective-permute-done | bytes 102432 | tf_op jit(solution)/shard_map/ppermute | solution.py:32
  52.5 0.1 multiply_reduce_fusion
  52.6 0.1 multiply_reduce_fusion.1
  52.7 0.1 concatenate.11
  52.9 14.9 %all_to_all.44 = f32[8,1,1440]{2,1,0:T(1,128)S(1)} all-to-all(f32[8,1,1440]{2,1,0:T(1,128)S(1)} %broadcast_in_dim.15), channel_id=1, replica_groups=mesh['u'=4,'v'=2,'z'=8,'x'=4,'c'=2] {'x','c'}, dimensions={0} | all-to-all | bytes 92160 | tf_op jit(solution)/shard_map/all_to_all | solution.py:19
  67.8 20.6 %all_to_all.45 = f32[64,1,160]{2,1,0:T(1,128)S(1)} all-to-all(f32[64,1,160]{2,1,0:T(1,128)S(1)} %broadcast_in_dim.16), channel_id=1, replica_groups=mesh['u'=4,'v'=2,'z'=8,'x'=4,'c'=2] {'u','v','z'}, dimensions={0} | all-to-all | bytes 81920 | tf_op jit(solution)/shard_map/all_to_all | solution.py:19
  88.5 1.0 broadcast_in_dim.17
  89.5 3.5 %all-to-all-start.3 = ((bf16[8,80,640]{2,1,0:T(8,128)(2,1)}), bf16[8,80,640]{2,1,0:T(8,128)(2,1)S(1)}, u32[]{:S(2)}, u32[]{:S(2)}) async-start(bf16[8,80,640]{2,1,0:T(8,128)(2,1)} %broadcast_in_dim.17), calls=%async_computation.3 | async-start | bytes 1638400 | tf_op jit(solution)/shard_map/all_to_all | solution.py:19
  93.1 0.1 fusion.6
  93.1 0.1 reshape.86
  93.2 0.1 reshape.87
  93.3 0.1 reshape.91
  93.4 0.6 fusion.4
  94.7 0.1 dynamic_slice.13
  94.8 0.0 all-gather.5.cloned.1.call-done
  94.8 1.6 broadcast_multiply_fusion
  96.4 0.2 subtract_convert_fusion
  96.6 0.1 copy.25
  96.7 28.5 %all-to-all-done.3 = bf16[8,80,640]{2,1,0:T(8,128)(2,1)S(1)} async-done(((bf16[8,80,640]{2,1,0:T(8,128)(2,1)}), bf16[8,80,640]{2,1,0:T(8,128)(2,1)S(1)}, u32[]{:S(2)}, u32[]{:S(2)}) %all-to-all-start.3) | async-done | bytes 819232 | tf_op jit(solution)/shard_map/all_to_all | solution.py:19
  125.2 2.1 fusion.9
  127.3 5.9 %all-to-all-start.4 = ((f32[8,2,40,640]{3,2,1,0:T(8,128)}), f32[8,2,40,640]{3,2,1,0:T(8,128)S(1)}, u32[]{:S(2)}, u32[]{:S(2)}) async-start(f32[8,2,40,640]{3,2,1,0:T(8,128)} %fusion.9), calls=%async_computation.4 | async-start | bytes 3276800 | tf_op jit(solution)/shard_map/all_to_all | solution.py:66
  133.3 0.1 reshape.92
  134.1 20.5 %all-to-all-done.4 = f32[8,2,40,640]{3,2,1,0:T(8,128)S(1)} async-done(((f32[8,2,40,640]{3,2,1,0:T(8,128)}), f32[8,2,40,640]{3,2,1,0:T(8,128)S(1)}, u32[]{:S(2)}, u32[]{:S(2)}) %all-to-all-start.4) | async-done | bytes 1638432 | tf_op jit(solution)/shard_map/all_to_all | solution.py:66
  154.6 0.7 reduce_sum.97
  155.3 3.3 %all-to-all-start.5 = ((bf16[2,40,640]{2,1,0:T(8,128)(2,1)}), bf16[2,40,640]{2,1,0:T(8,128)(2,1)S(1)}, u32[]{:S(2)}, u32[]{:S(2)}) async-start(bf16[2,40,640]{2,1,0:T(8,128)(2,1)} %reduce_sum.97), calls=%async_computation.5 | async-start | bytes 204800 | tf_op jit(solution)/shard_map/all_to_all | solution.py:68
  158.7 0.1 broadcast_multiply_fusion.2
  158.8 3.1 %all-to-all-done.5 = bf16[2,40,640]{2,1,0:T(8,128)(2,1)S(1)} async-done(((bf16[2,40,640]{2,1,0:T(8,128)(2,1)}), bf16[2,40,640]{2,1,0:T(8,128)(2,1)S(1)}, u32[]{:S(2)}, u32[]{:S(2)}) %all-to-all-start.5) | async-done | bytes 102432 | tf_op jit(solution)/shard_map/all_to_all | solution.py:68
  161.8 15.4 %all_gather.17 = bf16[320,1280]{1,0:T(8,128)(2,1)S(1)} all-gather(bf16[40,1280]{1,0:T(8,128)(2,1)S(1)} %bitcast.53), channel_id=1, replica_groups=mesh['u'=4,'v'=2,'z'=8,'x'=4,'c'=2] {'x','c'}, dimensions={0}, use_global_device_ids=true | all-gather | bytes 921600 | tf_op jit(solution)/shard_map/all_gather | solution.py:70
  177.3 3.5 %fusion.3 = bf16[2,8,80,640]{3,2,0,1:T(8,128)(2,1)S(1)} fusion(f32[8,2,80,640]{3,2,1,0:T(8,128)} %bitcast.46, f32[640]{0:T(1024)S(1)} %get-tuple-element.12, f32[2,8,80]{2,0,1:T(2,128)S(1)} %copy.27, pred[]{:T(512)S(6)} %eq.3), kind=kLoop, calls=%fused_computation.4 | loop fusion | flops 4096000 | bytes 4922881 | tf_op jit(solution)/shard_map/convert_element_type | solution.py:75
  180.7 0.1 copy.28
  180.9 1.7 fusion.10
  182.6 3.5 %all-to-all-start.6 = ((f32[4,80,640]{2,1,0:T(8,128)}), f32[4,80,640]{2,1,0:T(8,128)S(1)}, u32[]{:S(2)}, u32[]{:S(2)}) async-start(f32[4,80,640]{2,1,0:T(8,128)} %fusion.10), calls=%async_computation.6 | async-start | bytes 1638400 | tf_op jit(solution)/shard_map/all_to_all | solution.py:77
  186.1 0.1 fusion.8
  186.2 0.8 multiply_subtract_fusion.1
  186.9 0.8 multiply_subtract_fusion
  187.7 19.6 %all-to-all-done.6 = f32[4,80,640]{2,1,0:T(8,128)S(1)} async-done(((f32[4,80,640]{2,1,0:T(8,128)}), f32[4,80,640]{2,1,0:T(8,128)S(1)}, u32[]{:S(2)}, u32[]{:S(2)}) %all-to-all-start.6) | async-done | bytes 819232 | tf_op jit(solution)/shard_map/all_to_all | solution.py:77
  207.3 0.7 reduce_sum.99
  (21 shorter events, 0.2 us)
Async XLA Ops:
  7.2 87.6 %all-gather.5.cloned.1.call-start = ((), (), s32[]{:S(2)}) async-start(), calls=%async_computation.7 | async-start | bytes 1843200 | tf_op jit(solution)/shard_map/all_gather | solution.py:30
  7.9 20.3 %copy-start.1 = (f32[640,80]{0,1:T(8,128)S(1)}, f32[640,80]{0,1:T(8,128)}, u32[]{:S(2)}) copy-start(f32[640,80]{0,1:T(8,128)} %param.9) | copy-start | bytes 614404
  7.9 23.2 %copy-start.2 = (bf16[80,640]{1,0:T(8,128)(2,1)S(1)}, bf16[80,640]{1,0:T(8,128)(2,1)}, u32[]{:S(2)}) copy-start(bf16[80,640]{1,0:T(8,128)(2,1)} %param.7) | copy-start | bytes 307204
  10.1 42.5 %copy-start = (f32[80,640]{1,0:T(8,128)S(1)}, f32[80,640]{1,0:T(8,128)}, u32[]{:S(2)}) copy-start(f32[80,640]{1,0:T(8,128)} %param.8) | copy-start | bytes 614404
  11.0 37.2 %all-to-all-start = ((f32[64,1,1280]{2,1,0:T(1,128)}), f32[64,1,1280]{2,1,0:T(1,128)S(1)}, u32[]{:S(2)}, u32[]{:S(2)}) async-start(f32[64,1,1280]{2,1,0:T(1,128)} %broadcast_in_dim.14), calls=%async_computation | async-start | bytes 655360 | tf_op jit(solution)/shard_map/all_to_all | solution.py:19
  28.2 149.1 %all-gather.7.cloned.1.call-start = ((), (), s32[]{:S(2)}) async-start(), calls=%async_computation.8 | async-start | bytes 3686400 | tf_op jit(solution)/shard_map/all_gather | solution.py:44
  28.2 19.2 %collective-permute-start.1 = (f32[80,640]{1,0:T(8,128)S(1)}, f32[80,640]{1,0:T(8,128)S(1)}, u32[]{:S(2)}, u32[]{:S(2)}) collective-permute-start(f32[80,640]{1,0:T(8,128)S(1)} %bitcast.47), channel_id=1, source_target_pairs={{0,64},{64,0},{1,65},{65,1},{2,66},{66,2},{3,67},{67,3},{4,68},{68... | collective-permute-start | bytes 614408 | tf_op jit(solution)/shard_map/ppermute | solution.py:34
  31.2 21.3 %collective-permute-start = (bf16[80,640]{1,0:T(8,128)(2,1)S(1)}, bf16[80,640]{1,0:T(8,128)(2,1)S(1)}, u32[]{:S(2)}, u32[]{:S(2)}) collective-permute-start(bf16[80,640]{1,0:T(8,128)(2,1)S(1)} %copy-done.2), channel_id=1, source_target_pairs={{0,0},{1,64},{2,128},{3,192},{4,256},{5,320},{6,384},{7,448},{64,1... | collective-permute-start | bytes 307208 | tf_op jit(solution)/shard_map/ppermute | solution.py:32
  89.5 35.8 %all-to-all-start.3 = ((bf16[8,80,640]{2,1,0:T(8,128)(2,1)}), bf16[8,80,640]{2,1,0:T(8,128)(2,1)S(1)}, u32[]{:S(2)}, u32[]{:S(2)}) async-start(bf16[8,80,640]{2,1,0:T(8,128)(2,1)} %broadcast_in_dim.17), calls=%async_computation.3 | async-start | bytes 1638400 | tf_op jit(solution)/shard_map/all_to_all | solution.py:19
  127.3 27.2 %all-to-all-start.4 = ((f32[8,2,40,640]{3,2,1,0:T(8,128)}), f32[8,2,40,640]{3,2,1,0:T(8,128)S(1)}, u32[]{:S(2)}, u32[]{:S(2)}) async-start(f32[8,2,40,640]{3,2,1,0:T(8,128)} %fusion.9), calls=%async_computation.4 | async-start | bytes 3276800 | tf_op jit(solution)/shard_map/all_to_all | solution.py:66
  155.3 6.5 %all-to-all-start.5 = ((bf16[2,40,640]{2,1,0:T(8,128)(2,1)}), bf16[2,40,640]{2,1,0:T(8,128)(2,1)S(1)}, u32[]{:S(2)}, u32[]{:S(2)}) async-start(bf16[2,40,640]{2,1,0:T(8,128)(2,1)} %reduce_sum.97), calls=%async_computation.5 | async-start | bytes 204800 | tf_op jit(solution)/shard_map/all_to_all | solution.py:68
  182.6 24.7 %all-to-all-start.6 = ((f32[4,80,640]{2,1,0:T(8,128)}), f32[4,80,640]{2,1,0:T(8,128)S(1)}, u32[]{:S(2)}, u32[]{:S(2)}) async-start(f32[4,80,640]{2,1,0:T(8,128)} %fusion.10), calls=%async_computation.6 | async-start | bytes 1638400 | tf_op jit(solution)/shard_map/all_to_all | solution.py:77
Sparse Core Ops, SparseCore 0:
  10.1 53.9 all-gather.4
  66.1 68.2 all-gather.6

commit v3 on v2

--- a/solution.py
+++ b/solution.py
@@ -5,6 +5,7 @@
 
 
 decay = 0.9
+PAD = 104
 Y = ("u", "v")
 F = ("x", "c")
 DP = ("u", "v", "z")
@@ -25,23 +26,19 @@
     token_count = layer_inputs.shape[0] * ny * nz
     rows, cols = left_inv.shape
     half = rows // 2
-    u, v, z, f = lax.axis_index("u"), lax.axis_index("v"), lax.axis_index("z"), lax.axis_index(F)
+    v, z, f = lax.axis_index("v"), lax.axis_index("z"), lax.axis_index(F)
 
     left_wide = lax.all_gather(left_inv, Y, axis=0, tiled=False)
     swap = [(a * nf + b, b * nf + a) for a in range(ny) for b in range(nf)]
     weight_piece = lax.ppermute(weight_grad, Y + F, swap)
-    right_rows_own = right_inv.T
-    right_other = lax.ppermute(right_rows_own, "v", [(0, 1), (1, 0)])
-    right_pair = jnp.concatenate([right_rows_own[None], right_other[None]], axis=0)
-
     act_local = jnp.sum(layer_inputs, axis=0, dtype=jnp.float32)
     grad_local = jnp.sum(out_grads, axis=0, dtype=jnp.float32)
     sums = share(jnp.concatenate([act_local, grad_local]), DP)
     means = jnp.sum(sums, axis=0) / token_count
 
-    weight_piece, right_pair, means = lax.optimization_barrier((weight_piece, right_pair, means))
-    weight_block = share(weight_piece, "z").reshape(nz * rows, cols)
-    right_wide = lax.all_gather(right_pair, "z", axis=0, tiled=False)
+    padded = jnp.pad(weight_piece, ((0, PAD - rows), (0, 0)))
+    weight_wide = lax.all_gather(padded, "z", axis=0, tiled=False)
+    weight_block = weight_wide[:, :rows, :].reshape(nz * rows, cols)
 
     left_partial = jnp.sum(left_inv * means[None, :cols], axis=1)
     right_partial = jnp.sum(right_inv * means[cols:, None], axis=0)
@@ -58,6 +55,17 @@
     left_cols = lax.dynamic_slice_in_dim(left_image, f * cols, cols)
     right_cols = lax.dynamic_slice_in_dim(right_image, f * cols, cols)
 
+    new_left = left_inv / decay - left_coef * images[:rows, None] * left_cols[None, :]
+    new_right = right_inv / decay - right_coef * right_cols[:, None] * images[None, rows:]
+
+    right_own = new_right.astype(jnp.bfloat16).T
+    right_other = lax.ppermute(right_own, "v", [(0, 1), (1, 0)])
+    right_pair = jnp.where(
+        v == 0, jnp.stack([right_own, right_other]), jnp.stack([right_other, right_own])
+    )
+    right_wide = lax.all_gather(right_pair, "z", axis=0, tiled=False)
+    right_half = right_wide.transpose(1, 0, 2, 3).reshape(2 * nz * rows, cols)
+
     wide_image = lax.dynamic_slice_in_dim(left_image.reshape(ny, nz, rows), z, 1, 1)
     left_block = left_wide / decay - (left_coef * wide_image.reshape(ny, rows, 1)) * left_cols
     left_half = left_block.astype(jnp.bfloat16).reshape(nx, 2, 2, half, cols)
@@ -69,16 +77,10 @@
     hidden_piece = hidden_piece.transpose(1, 0, 2).reshape(half, 2 * cols)
     hidden = lax.all_gather(hidden_piece, F, axis=0, tiled=True)
 
-    pair_image = lax.dynamic_slice_in_dim(right_image.reshape(nu, 2, nz, rows), u, 1, 0)[0]
-    right_sorted = jnp.where(v == 0, right_wide, right_wide[:, ::-1]).transpose(1, 0, 2, 3)
-    right_block = right_sorted / decay - (right_coef * pair_image[..., None]) * right_cols
-    right_half = right_block.astype(jnp.bfloat16).reshape(2 * nz * rows, cols)
     partial = jnp.dot(hidden, right_half, preferred_element_type=jnp.float32)
     pieces = lax.all_to_all(partial.reshape(nu, rows, cols), "u", 0, 0, tiled=True)
     precond = jnp.sum(pieces, axis=0).astype(jnp.bfloat16)
 
-    new_left = left_inv / decay - left_coef * images[:rows, None] * left_cols[None, :]
-    new_right = right_inv / decay - right_coef * right_cols[:, None] * images[None, rows:]
     return (precond, new_left, new_right)
 
 

time: 216 us -> 214 us (level)
  waiting for transfers between devices: 89.2 us -> 76.4 us
  blocking collectives: 51 us -> 61.3 us
  other arithmetic: 12.5 us -> 8.22 us
  starting transfers between devices: 39.9 us -> 43.4 us
  local copies, waits for them, and re-layouts: 2.77 us -> 5.71 us
    all_to_all x0 -> x1, blocking collectives: none -> 30.5 us  [per_device(): lax.all_to_all(partial.reshape(nf, 2, half, cols), F, 0, 0, tiled=True)]
    all_to_all x2 -> x1, blocking collectives: 35.6 us -> 12.6 us  [share(): lax.all_to_all(jnp.broadcast_to(vec[None], (count,) + vec.shape), axes, 0...]
    all_to_all x1 -> x0, waiting for transfers between devices: 20.5 us -> none  [per_device(): lax.all_to_all(partial.reshape(nf, 2, half, cols), F, 0, 0, tiled=True)]
    all_gather x1, waiting for transfers between devices: 0.02 us -> 15.9 us  [per_device(): left_wide = lax.all_gather(left_inv, Y, axis=0, tiled=False)]
    all_gather x1, waiting for transfers between devices: 0.01 us -> 7.63 us  [per_device(): right_wide = lax.all_gather(right_pair, 'z', axis=0, tiled=False)]
    ppermute x1, waiting for transfers between devices: 12.7 us -> 5.72 us  [per_device(): right_other = lax.ppermute(right_own, 'v', [(0, 1), (1, 0)])]
    all_to_all x1 -> x0, starting transfers between devices: 5.92 us -> none  [per_device(): lax.all_to_all(partial.reshape(nf, 2, half, cols), F, 0, 0, tiled=True)]
    all_to_all x2, starting transfers between devices: 20.7 us -> 26.5 us  [share(): lax.all_to_all(jnp.broadcast_to(vec[None], (count,) + vec.shape), axes, 0...]
  transfers between devices with their start and end apart: 9 -> 9, of which waited for: 6 -> 7; matrix products, arithmetic and copies ran while one was open for 6% -> 6% of each run, Pallas kernels for 0% -> 0%
where the time goes in v3:
time: 214 us; the launch traced here: 213 us
  waiting for transfers between devices  76.4 us (36%)
  blocking collectives  61.3 us (29%)
  starting transfers between devices  43.4 us (20%)
  between operations  15.3 us (7%)
  other arithmetic  8.22 us (4%)
  local copies, waits for them, and re-layouts  5.71 us (3%)
  matrix products  2.64 us (1%)
    all_to_all x1, blocking collectives, per_device(): lax.all_to_all(partial.reshape(nf, 2, half, cols), F, 0, 0, tiled=True)  30.5 us
    all_to_all x2, starting transfers between devices, share(): lax.all_to_all(jnp.broadcast_to(vec[None], (count,) + vec.shape), axes, 0...  26.5 us
    all_to_all x2, waiting for transfers between devices, share(): lax.all_to_all(jnp.broadcast_to(vec[None], (count,) + vec.shape), axes, 0...  23.3 us
    all_to_all x1, waiting for transfers between devices, per_device(): lax.all_to_all(partial.reshape(nu, rows, cols), 'u', 0, 0, tiled=True)  20.5 us
    all_gather x1, blocking collectives, per_device(): hidden = lax.all_gather(hidden_piece, F, axis=0, tiled=True)  18.2 us
    all_gather x1, waiting for transfers between devices, per_device(): left_wide = lax.all_gather(left_inv, Y, axis=0, tiled=False)  15.9 us
    all_to_all x1, blocking collectives, share(): lax.all_to_all(jnp.broadcast_to(vec[None], (count,) + vec.shape), axes, 0...  12.6 us
    all_gather x1, waiting for transfers between devices, per_device(): right_wide = lax.all_gather(right_pair, 'z', axis=0, tiled=False)  7.63 us
  transfers between devices with their start and end apart: 9, of which 7 were waited for; matrix products, arithmetic and copies ran while one was open for 6% of the time, Pallas kernels for 0%

profile of v3, /device:TPU:1, one launch (start us, length us, event | category | flops | bytes accessed | tf_op | source)
XLA Modules:
  0.0 212.9 jit_solution(10705083563953044341)
XLA Ops:
  7.2 4.6 %collective-permute-start = (bf16[80,640]{1,0:T(8,128)(2,1)}, bf16[80,640]{1,0:T(8,128)(2,1)S(1)}, u32[]{:S(2)}, u32[]{:S(2)}) collective-permute-start(bf16[80,640]{1,0:T(8,128)(2,1)} %param.7), channel_id=1, source_target_pairs={{0,0},{1,64},{2,128},{3,192},{4,256},{5,320},{6,384},{7,448},{64,1... | collective-permute-start | bytes 307208 | tf_op jit(solution)/shard_map/ppermute | solution.py:33
  11.8 2.5 %collective-permute-done = bf16[80,640]{1,0:T(8,128)(2,1)S(1)} collective-permute-done((bf16[80,640]{1,0:T(8,128)(2,1)}, bf16[80,640]{1,0:T(8,128)(2,1)S(1)}, u32[]{:S(2)}, u32[]{:S(2)}) %collective-permute-start) | collective-permute-done | bytes 102432 | tf_op jit(solution)/shard_map/ppermute | solution.py:33
  14.3 0.7 pad.4
  15.0 2.2 %convert_reduce_fusion = (f32[640]{0:T(1024)S(1)}, f32[640]{0:T(1024)S(1)}) fusion(bf16[1024,640]{1,0:T(8,128)(2,1)} %param.6, bf16[1024,640]{1,0:T(8,128)(2,1)} %param.5), kind=kLoop, calls=%fused_computation | loop fusion | flops 2620160 | bytes 2626560 | tf_op jit(solution)/shard_map/reduce_sum | solution.py:35
  17.2 0.9 broadcast_in_dim.6
  18.1 21.8 %all-to-all-start = ((f32[64,1,1280]{2,1,0:T(1,128)}), f32[64,1,1280]{2,1,0:T(1,128)S(1)}, u32[]{:S(2)}, u32[]{:S(2)}) async-start(f32[64,1,1280]{2,1,0:T(1,128)} %broadcast_in_dim.6), calls=%async_computation | async-start | bytes 655360 | tf_op jit(solution)/shard_map/all_to_all | solution.py:20
  39.9 0.0 all-gather.8.cloned.1.call-start
  40.0 0.7 all-gather.8.cloned.1.call-update
  40.7 12.2 %all-to-all-done = f32[64,1,1280]{2,1,0:T(1,128)S(1)} async-done(((f32[64,1,1280]{2,1,0:T(1,128)}), f32[64,1,1280]{2,1,0:T(1,128)S(1)}, u32[]{:S(2)}, u32[]{:S(2)}) %all-to-all-start) | async-done | bytes 327712 | tf_op jit(solution)/shard_map/all_to_all | solution.py:20
  52.9 0.2 reduce_sum.92
  53.1 0.1 multiply_reduce_fusion.1
  53.2 0.1 multiply_reduce_fusion
  53.4 0.1 concatenate.21
  53.5 12.6 %all_to_all.39 = f32[8,1,1440]{2,1,0:T(1,128)S(1)} all-to-all(f32[8,1,1440]{2,1,0:T(1,128)S(1)} %broadcast_in_dim.7), channel_id=1, replica_groups=mesh['u'=4,'v'=2,'z'=8,'x'=4,'c'=2] {'x','c'}, dimensions={0} | all-to-all | bytes 92160 | tf_op jit(solution)/shard_map/all_to_all | solution.py:20
  66.1 0.7 broadcast_in_dim.8
  66.8 4.7 %all-to-all-start.2 = ((f32[64,1,160]{2,1,0:T(1,128)}), f32[64,1,160]{2,1,0:T(1,128)S(1)}, u32[]{:S(2)}, u32[]{:S(2)}) async-start(f32[64,1,160]{2,1,0:T(1,128)} %broadcast_in_dim.8), calls=%async_computation.2 | async-start | bytes 131072 | tf_op jit(solution)/shard_map/all_to_all | solution.py:20
  71.5 0.0 all-gather.6.cloned.1.call-start
  71.6 11.1 %all-to-all-done.2 = f32[64,1,160]{2,1,0:T(1,128)S(1)} async-done(((f32[64,1,160]{2,1,0:T(1,128)}), f32[64,1,160]{2,1,0:T(1,128)S(1)}, u32[]{:S(2)}, u32[]{:S(2)}) %all-to-all-start.2) | async-done | bytes 40992 | tf_op jit(solution)/shard_map/all_to_all | solution.py:20
  82.6 0.1 fusion.2
  82.7 0.1 reshape.140
  82.8 0.1 reshape.139
  82.9 0.1 reshape.134
  83.0 0.6 fusion
  85.0 0.1 dynamic-slice_multiply_fusion
  85.0 0.1 slice_multiply_fusion.2
  85.1 0.1 convert_bitcast_fusion
  85.2 2.3 %collective-permute-start.1 = (bf16[80,640]{1,0:T(8,128)(2,1)S(1)}, bf16[80,640]{1,0:T(8,128)(2,1)S(1)}, u32[]{:S(2)}, u32[]{:S(2)}) collective-permute-start(bf16[80,640]{1,0:T(8,128)(2,1)S(1)} %convert_bitcast_fusion.1), channel_id=1, source_target_pairs={{0,64},{64,0},{1,65},{65,1},{2,66},{66,2},{3,67},{67,3},{4,68},{68... | collective-permute-start | bytes 307208 | tf_op jit(solution)/shard_map/ppermute | solution.py:62
  87.6 5.7 %collective-permute-done.1 = bf16[80,640]{1,0:T(8,128)(2,1)S(1)} collective-permute-done((bf16[80,640]{1,0:T(8,128)(2,1)S(1)}, bf16[80,640]{1,0:T(8,128)(2,1)S(1)}, u32[]{:S(2)}, u32[]{:S(2)}) %collective-permute-start.1) | collective-permute-done | bytes 102432 | tf_op jit(solution)/shard_map/ppermute | solution.py:62
  93.3 0.7 maximum_select_fusion
  94.0 0.1 reshape.135
  94.1 0.1 dynamic_slice.10
  94.2 1.2 slice.45
  95.5 15.9 %all-gather.8.cloned.1.call-done = f32[640,640]{1,0:T(8,128)} async-done(((f32[80,640]{1,0:T(8,128)}), f32[640,640]{1,0:T(8,128)}) %all-gather.8.cloned.1.call-update) | async-done | bytes 1638416 | tf_op jit(solution)/shard_map/all_gather | solution.py:31
  111.4 1.6 broadcast_multiply_fusion
  113.0 0.2 subtract_convert_fusion
  113.2 0.1 copy.21
  113.3 0.9 fusion.4
  114.2 30.5 %all_to_all.40 = f32[8,2,40,640]{3,2,1,0:T(8,128)S(1)} all-to-all(f32[8,2,40,640]{3,2,1,0:T(8,128)S(1)} %fusion.4), channel_id=1, replica_groups=mesh['u'=4,'v'=2,'z'=8,'x'=4,'c'=2] {'x','c'}, dimensions={0} | all-to-all | bytes 3276800 | tf_op jit(solution)/shard_map/all_to_all | solution.py:74
  144.7 0.7 reduce_sum.97
  145.4 3.3 %all-to-all-start.4 = ((bf16[2,40,640]{2,1,0:T(8,128)(2,1)}), bf16[2,40,640]{2,1,0:T(8,128)(2,1)S(1)}, u32[]{:S(2)}, u32[]{:S(2)}) async-start(bf16[2,40,640]{2,1,0:T(8,128)(2,1)} %reduce_sum.97), calls=%async_computation.4 | async-start | bytes 204800 | tf_op jit(solution)/shard_map/all_to_all | solution.py:76
  148.8 7.6 %all-gather.6.cloned.1.call-done = bf16[8,2,80,640]{3,2,1,0:T(8,128)(2,1)} async-done(((bf16[1,2,80,640]{3,2,1,0:T(8,128)(2,1)}), bf16[8,2,80,640]{3,2,1,0:T(8,128)(2,1)}) %all-gather.6.cloned.1.call-update) | async-done | bytes 1638416 | tf_op jit(solution)/shard_map/all_gather | solution.py:66
  156.4 1.6 copy.23
  158.0 18.2 %all_gather.23 = bf16[320,1280]{1,0:T(8,128)(2,1)S(1)} all-gather(bf16[40,1280]{1,0:T(8,128)(2,1)S(1)} %bitcast.46), channel_id=1, replica_groups=mesh['u'=4,'v'=2,'z'=8,'x'=4,'c'=2] {'x','c'}, dimensions={0}, use_global_device_ids=true | all-gather | bytes 921600 | tf_op jit(solution)/shard_map/all_gather | solution.py:78
  176.2 1.7 fusion.5
  177.9 6.5 %all-to-all-start.5 = ((f32[4,80,640]{2,1,0:T(8,128)}), f32[4,80,640]{2,1,0:T(8,128)S(1)}, u32[]{:S(2)}, u32[]{:S(2)}) async-start(f32[4,80,640]{2,1,0:T(8,128)} %fusion.5), calls=%async_computation.5 | async-start | bytes 1638400 | tf_op jit(solution)/shard_map/all_to_all | solution.py:81
  184.4 0.8 multiply_subtract_fusion
  185.1 20.5 %all-to-all-done.5 = f32[4,80,640]{2,1,0:T(8,128)S(1)} async-done(((f32[4,80,640]{2,1,0:T(8,128)}), f32[4,80,640]{2,1,0:T(8,128)S(1)}, u32[]{:S(2)}, u32[]{:S(2)}) %all-to-all-start.5) | async-done | bytes 819232 | tf_op jit(solution)/shard_map/all_to_all | solution.py:81
  205.7 0.7 reduce_sum.99
  (21 shorter events, 0.2 us)
Async XLA Ops:
  7.2 87.1 %all-gather.10.cloned.1.call-start = ((), (), s32[]{:S(2)}) async-start(), calls=%async_computation.8 | async-start | bytes 1198080 | tf_op jit(solution)/shard_map/all_gather | solution.py:40
  7.2 7.1 %collective-permute-start = (bf16[80,640]{1,0:T(8,128)(2,1)}, bf16[80,640]{1,0:T(8,128)(2,1)S(1)}, u32[]{:S(2)}, u32[]{:S(2)}) collective-permute-start(bf16[80,640]{1,0:T(8,128)(2,1)} %param.7), channel_id=1, source_target_pairs={{0,0},{1,64},{2,128},{3,192},{4,256},{5,320},{6,384},{7,448},{64,1... | collective-permute-start | bytes 307208 | tf_op jit(solution)/shard_map/ppermute | solution.py:33
  15.0 38.1 %copy-start = (f32[80,640]{1,0:T(8,128)S(1)}, f32[80,640]{1,0:T(8,128)}, u32[]{:S(2)}) copy-start(f32[80,640]{1,0:T(8,128)} %param.8) | copy-start | bytes 614404
  15.0 38.2 %copy-start.1 = (f32[640,80]{0,1:T(8,128)S(1)}, f32[640,80]{0,1:T(8,128)}, u32[]{:S(2)}) copy-start(f32[640,80]{0,1:T(8,128)} %param.9) | copy-start | bytes 614404
  18.1 34.8 %all-to-all-start = ((f32[64,1,1280]{2,1,0:T(1,128)}), f32[64,1,1280]{2,1,0:T(1,128)S(1)}, u32[]{:S(2)}, u32[]{:S(2)}) async-start(f32[64,1,1280]{2,1,0:T(1,128)} %broadcast_in_dim.6), calls=%async_computation | async-start | bytes 655360 | tf_op jit(solution)/shard_map/all_to_all | solution.py:20
  39.9 71.4 %all-gather.8.cloned.1.call-start = ((), (), s32[]{:S(2)}) async-start(), calls=%async_computation.7 | async-start | bytes 1843200 | tf_op jit(solution)/shard_map/all_gather | solution.py:31
  66.8 15.9 %all-to-all-start.2 = ((f32[64,1,160]{2,1,0:T(1,128)}), f32[64,1,160]{2,1,0:T(1,128)S(1)}, u32[]{:S(2)}, u32[]{:S(2)}) async-start(f32[64,1,160]{2,1,0:T(1,128)} %broadcast_in_dim.8), calls=%async_computation.2 | async-start | bytes 131072 | tf_op jit(solution)/shard_map/all_to_all | solution.py:20
  71.5 84.9 %all-gather.6.cloned.1.call-start = ((), (), s32[]{:S(2)}) async-start(), calls=%async_computation.6 | async-start | bytes 1843200 | tf_op jit(solution)/shard_map/all_gather | solution.py:66
  85.2 27.7 %copy-start.2 = (f32[640,80]{0,1:T(8,128)}, f32[640,80]{0,1:T(8,128)S(1)}, u32[]{:S(2)}) copy-start(f32[640,80]{0,1:T(8,128)S(1)} %get-tuple-element.6) | copy-start | bytes 614404
  85.2 8.0 %collective-permute-start.1 = (bf16[80,640]{1,0:T(8,128)(2,1)S(1)}, bf16[80,640]{1,0:T(8,128)(2,1)S(1)}, u32[]{:S(2)}, u32[]{:S(2)}) collective-permute-start(bf16[80,640]{1,0:T(8,128)(2,1)S(1)} %convert_bitcast_fusion.1), channel_id=1, source_target_pairs={{0,64},{64,0},{1,65},{65,1},{2,66},{66,2},{3,67},{67,3},{4,68},{68... | collective-permute-start | bytes 307208 | tf_op jit(solution)/shard_map/ppermute | solution.py:62
  145.4 12.6 %all-to-all-start.4 = ((bf16[2,40,640]{2,1,0:T(8,128)(2,1)}), bf16[2,40,640]{2,1,0:T(8,128)(2,1)S(1)}, u32[]{:S(2)}, u32[]{:S(2)}) async-start(bf16[2,40,640]{2,1,0:T(8,128)(2,1)} %reduce_sum.97), calls=%async_computation.4 | async-start | bytes 204800 | tf_op jit(solution)/shard_map/all_to_all | solution.py:76
  177.9 27.8 %all-to-all-start.5 = ((f32[4,80,640]{2,1,0:T(8,128)}), f32[4,80,640]{2,1,0:T(8,128)S(1)}, u32[]{:S(2)}, u32[]{:S(2)}) async-start(f32[4,80,640]{2,1,0:T(8,128)} %fusion.5), calls=%async_computation.5 | async-start | bytes 1638400 | tf_op jit(solution)/shard_map/all_to_all | solution.py:81
Sparse Core Ops, SparseCore 0:
  15.1 52.7 all-gather.9
  70.0 41.2 all-gather.7
  114.0 42.3 all-gather.5

commit v4 on v3

v4 whole, which is shorter than its diff:
```python
import jax
import jax.numpy as jnp
from jax import lax
from jax.sharding import Mesh, PartitionSpec as P


decay = 0.9
PAD = 104
F = ("x", "c")
DP = ("u", "v", "z")


def coefficient(quadratic):
    return (1.0 - decay) / (decay * decay * (1.0 + (1.0 - decay) / decay * quadratic))


def share(vec, axes):
    count = lax.axis_size(axes)
    return lax.all_to_all(jnp.broadcast_to(vec[None], (count,) + vec.shape), axes, 0, 0, tiled=True)


def swap_u_x(block):
    n = lax.axis_size("u")
    return lax.ppermute(block, ("u", "x"), [(a * n + b, b * n + a) for a in range(n) for b in range(n)])


def swap_v(block):
    return lax.ppermute(block, "v", [(0, 1), (1, 0)])


def block_of(vec, index, size):
    return lax.dynamic_slice_in_dim(vec, index * size, size)


def per_device(layer_inputs, out_grads, weight_grad, left_inv, right_inv):
    nu, nz, nf, ndp = lax.axis_size("u"), lax.axis_size("z"), lax.axis_size(F), lax.axis_size(DP)
    token_count = layer_inputs.shape[0] * ndp
    rows, cols = left_inv.shape
    u, v, z, f = lax.axis_index("u"), lax.axis_index("v"), lax.axis_index("z"), lax.axis_index(F)

    padded = jnp.pad(weight_grad, ((0, PAD - rows), (0, 0)))
    weight_wide = lax.all_gather(padded, "z", axis=0, tiled=False)

    left_piece = swap_u_x(left_inv)
    left_wide = lax.all_gather(left_piece, F, axis=0, tiled=False)

    act_local = jnp.sum(layer_inputs, axis=0, dtype=jnp.float32)
    grad_local = jnp.sum(out_grads, axis=0, dtype=jnp.float32)
    sums = share(jnp.concatenate([act_local, grad_local]), DP)
    means = jnp.sum(sums, axis=0) / token_count

    left_partial = jnp.sum(left_inv * means[None, :cols], axis=1)
    right_partial = jnp.sum(right_inv * means[cols:, None], axis=0)
    both = share(jnp.concatenate([means, left_partial, right_partial]), F)
    whole_act = both[:, :cols].reshape(nf * cols)
    whole_grad = both[:, cols : 2 * cols].reshape(nf * cols)
    images = jnp.sum(both[:, 2 * cols :], axis=0)
    weight_wide, images = lax.optimization_barrier((weight_wide, images))
    weight_own = weight_wide[:, :rows, :].reshape(nz * rows, cols)
    weight_other = swap_v(weight_own)
    all_images = share(images, DP)
    left_image = all_images[:, :rows].reshape(ndp * rows)
    right_image = all_images[:, rows:].reshape(ndp * rows)
    left_coef = coefficient(jnp.sum(whole_act * left_image))
    right_coef = coefficient(jnp.sum(whole_grad * right_image))

    left_cols = block_of(left_image, f, cols)
    right_cols = block_of(right_image, f, cols)
    new_left = left_inv / decay - left_coef * images[:rows, None] * left_cols[None, :]
    new_right = right_inv / decay - right_coef * right_cols[:, None] * images[None, rows:]

    right_own = new_right.astype(jnp.bfloat16).T
    right_other = swap_v(right_own)
    right_pair = jnp.where(
        v == 0, jnp.stack([right_own, right_other]), jnp.stack([right_other, right_own])
    )
    right_wide = lax.all_gather(right_pair, "z", axis=0, tiled=False)

    row_image = lax.dynamic_index_in_dim(
        left_image.reshape(nu, ndp // nu, rows), v * nz + z, 1, keepdims=False
    )
    left_wide = left_wide.reshape(nu, 2, rows, cols)

    def left_half(which):
        old = lax.dynamic_index_in_dim(left_wide, which, 1, keepdims=False)
        col_image = block_of(left_image, 2 * u + which, cols)
        new = old / decay - (left_coef * row_image[:, :, None]) * col_image[None, None, :]
        return new.astype(jnp.bfloat16).reshape(nu * rows, cols)

    partial = jnp.dot(left_half(v), weight_own, preferred_element_type=jnp.float32)
    partial += jnp.dot(left_half(1 - v), weight_other, preferred_element_type=jnp.float32)
    pieces = lax.all_to_all(partial.reshape(nu, rows, cols), "u", 0, 0, tiled=True)
    hidden_piece = jnp.sum(pieces, axis=0).astype(jnp.bfloat16)
    hidden = lax.all_gather(hidden_piece, "u", axis=0, tiled=True)

    right_half = right_wide.transpose(1, 0, 2, 3).reshape(2, nz * rows, cols)
    partial = jnp.einsum(
        "crk,cmk->crm",
        jnp.broadcast_to(hidden[None], (2,) + hidden.shape),
        right_half,
        preferred_element_type=jnp.float32,
    )
    pieces = lax.all_to_all(partial.reshape(nf, rows, cols), ("c", "x"), 0, 0, tiled=True)
    precond = jnp.sum(pieces, axis=0).astype(jnp.bfloat16)
    precond = swap_u_x(precond)
    return (precond, new_left, new_right)


def solution(mesh):
    cube = Mesh(mesh.devices.reshape(4, 2, 8, 4, 2), ("u", "v", "z", "x", "c"))
    rows, cols = P(DP, F), P(F, DP)

    return jax.shard_map(
        per_device,
        mesh=cube,
        in_specs=(rows, rows, rows, rows, cols),
        out_specs=(rows, rows, cols),
        check_vma=False,
    )
```

time: 214 us -> 203 us (0.949)
  the two profiles are of different devices: /device:TPU:1 before, /device:TPU:14 now
where the time goes in v4:
time: 203 us; the launch traced here: 202 us
  blocking collectives  67.4 us (33%)
  waiting for transfers between devices  59.8 us (29%)
  starting transfers between devices  42.6 us (21%)
  between operations  15.4 us (8%)
  other arithmetic  7.51 us (4%)
  local copies, waits for them, and re-layouts  7.3 us (4%)
    all_to_all x2, starting transfers between devices, share(): lax.all_to_all(jnp.broadcast_to(vec[None], (count,) + vec.shape), axes, 0...  27.2 us
    all_to_all x1, blocking collectives, per_device(): lax.all_to_all(partial.reshape(nf, rows, cols), ('c', 'x'), 0, 0, tiled=T...  27.1 us
    all_to_all x2, waiting for transfers between devices, share(): lax.all_to_all(jnp.broadcast_to(vec[None], (count,) + vec.shape), axes, 0...  25.4 us
    ppermute x2, waiting for transfers between devices, swap_v(): return lax.ppermute(block, 'v', [(0, 1), (1, 0)])  18.3 us
    all_to_all x1, blocking collectives, per_device(): lax.all_to_all(partial.reshape(nu, rows, cols), 'u', 0, 0, tiled=True)  17.8 us
    all_gather x1, blocking collectives, per_device(): hidden = lax.all_gather(hidden_piece, 'u', axis=0, tiled=True)  14.7 us
    ppermute x2, waiting for transfers between devices, swap_u_x(): lax.ppermute(block, ('u', 'x'), [(a * n + b, b * n + a) for a in range(n)...  10.8 us
    ppermute x2, starting transfers between devices, swap_u_x(): lax.ppermute(block, ('u', 'x'), [(a * n + b, b * n + a) for a in range(n)...  8.83 us
  transfers between devices with their start and end apart: 9, of which 6 were waited for; matrix products, arithmetic and copies ran while one was open for 6% of the time, Pallas kernels for 0%

profile of v4, /device:TPU:14, one launch (start us, length us, event | category | flops | bytes accessed | tf_op | source)
XLA Modules:
  0.0 201.9 jit_solution(11172980437374977613)
XLA Ops:
  7.2 1.6 pad.4
  8.8 5.3 %collective-permute-start = (f32[80,640]{1,0:T(8,128)}, f32[80,640]{1,0:T(8,128)S(1)}, u32[]{:S(2)}, u32[]{:S(2)}) collective-permute-start(f32[80,640]{1,0:T(8,128)} %param.8), channel_id=1, source_target_pairs={{0,0},{2,128},{4,256},{6,384},{128,2},{130,130},{132,258},{134,386... | collective-permute-start | bytes 614408 | tf_op jit(solution)/shard_map/ppermute | solution.py:24
  14.1 2.1 %convert_reduce_fusion = (f32[640]{0:T(1024)S(1)}, f32[640]{0:T(1024)S(1)}) fusion(bf16[1024,640]{1,0:T(8,128)(2,1)} %param.6, bf16[1024,640]{1,0:T(8,128)(2,1)} %param.5), kind=kLoop, calls=%fused_computation | loop fusion | flops 2620160 | bytes 2626560 | tf_op jit(solution)/shard_map/reduce_sum | solution.py:48
  16.3 0.9 broadcast_in_dim.8
  17.2 15.1 %all-to-all-start = ((f32[64,1,1280]{2,1,0:T(1,128)}), f32[64,1,1280]{2,1,0:T(1,128)S(1)}, u32[]{:S(2)}, u32[]{:S(2)}) async-start(f32[64,1,1280]{2,1,0:T(1,128)} %broadcast_in_dim.8), calls=%async_computation | async-start | bytes 655360 | tf_op jit(solution)/shard_map/all_to_all | solution.py:19
  32.3 0.7 copy-done.4
  33.0 14.0 %all-to-all-done = f32[64,1,1280]{2,1,0:T(1,128)S(1)} async-done(((f32[64,1,1280]{2,1,0:T(1,128)}), f32[64,1,1280]{2,1,0:T(1,128)S(1)}, u32[]{:S(2)}, u32[]{:S(2)}) %all-to-all-start) | async-done | bytes 327712 | tf_op jit(solution)/shard_map/all_to_all | solution.py:19
  47.0 0.2 reduce_sum.92
  47.3 0.1 multiply_reduce_fusion.1
  47.4 0.1 multiply_reduce_fusion
  47.5 0.1 concatenate.21
  47.6 7.8 %all_to_all.34 = f32[8,1,1440]{2,1,0:T(1,128)S(1)} all-to-all(f32[8,1,1440]{2,1,0:T(1,128)S(1)} %broadcast_in_dim.9), channel_id=1, replica_groups=mesh['u'=4,'v'=2,'z'=8,'x'=4,'c'=2] {'x','c'}, dimensions={0} | all-to-all | bytes 92160 | tf_op jit(solution)/shard_map/all_to_all | solution.py:19
  55.5 5.3 %all-gather.10.cloned.1.call-done = bf16[832,640]{1,0:T(8,128)(2,1)} async-done(((bf16[104,640]{1,0:T(8,128)(2,1)}), bf16[832,640]{1,0:T(8,128)(2,1)}) %all-gather.10.cloned.1.call-update) | async-done | bytes 1064976 | tf_op jit(solution)/shard_map/all_gather | solution.py:42
  60.7 0.7 broadcast_in_dim.10
  61.4 12.2 %all-to-all-start.2 = ((f32[64,1,160]{2,1,0:T(1,128)}), f32[64,1,160]{2,1,0:T(1,128)S(1)}, u32[]{:S(2)}, u32[]{:S(2)}) async-start(f32[64,1,160]{2,1,0:T(1,128)} %broadcast_in_dim.10), calls=%async_computation.2 | async-start | bytes 131072 | tf_op jit(solution)/shard_map/all_to_all | solution.py:19
  73.6 11.3 %all-to-all-done.2 = f32[64,1,160]{2,1,0:T(1,128)S(1)} async-done(((f32[64,1,160]{2,1,0:T(1,128)}), f32[64,1,160]{2,1,0:T(1,128)S(1)}, u32[]{:S(2)}, u32[]{:S(2)}) %all-to-all-start.2) | async-done | bytes 40992 | tf_op jit(solution)/shard_map/all_to_all | solution.py:19
  84.9 0.1 fusion.6
  85.0 0.1 reshape.167
  85.1 0.1 reshape.168
  85.2 0.1 reshape.163
  85.3 0.6 fusion.4
  87.3 0.1 dynamic-slice_multiply_fusion.1
  87.4 0.1 convert_bitcast_fusion
  87.5 3.3 %collective-permute-start.2 = (bf16[80,640]{1,0:T(8,128)(2,1)S(1)}, bf16[80,640]{1,0:T(8,128)(2,1)S(1)}, u32[]{:S(2)}, u32[]{:S(2)}) collective-permute-start(bf16[80,640]{1,0:T(8,128)(2,1)S(1)} %convert_bitcast_fusion.1), channel_id=1, source_target_pairs={{0,64},{64,0},{1,65},{65,1},{2,66},{66,2},{3,67},{67,3},{4,68},{68... | collective-permute-start | bytes 307208 | tf_op jit(solution)/shard_map/ppermute | solution.py:28
  90.8 4.4 %collective-permute-done.2 = bf16[80,640]{1,0:T(8,128)(2,1)S(1)} collective-permute-done((bf16[80,640]{1,0:T(8,128)(2,1)S(1)}, bf16[80,640]{1,0:T(8,128)(2,1)S(1)}, u32[]{:S(2)}, u32[]{:S(2)}) %collective-permute-start.2) | collective-permute-done | bytes 102432 | tf_op jit(solution)/shard_map/ppermute | solution.py:28
  95.2 0.7 maximum_select_fusion
  96.0 0.1 slice.35
  96.0 3.2 %collective-permute-start.1 = (bf16[640,640]{1,0:T(8,128)(2,1)S(1)}, bf16[640,640]{1,0:T(8,128)(2,1)S(1)}, u32[]{:S(2)}, u32[]{:S(2)}) collective-permute-start(bf16[640,640]{1,0:T(8,128)(2,1)S(1)} %bitcast.34), channel_id=1, source_target_pairs={{0,64},{64,0},{1,65},{65,1},{2,66},{66,2},{3,67},{67,3},{4,68},{68... | collective-permute-start | bytes 2457608 | tf_op jit(solution)/shard_map/ppermute | solution.py:28
  99.2 0.1 reshape.164
  99.3 0.1 fusion.7
  99.4 0.5 broadcast.81
  99.9 0.7 fusion.5
  100.6 0.1 mul.167
  100.6 1.6 dynamic-slice_multiply_fusion
  102.3 0.1 fusion
  102.4 0.5 fusion.9
  103.0 13.9 %collective-permute-done.1 = bf16[640,640]{1,0:T(8,128)(2,1)S(1)} collective-permute-done((bf16[640,640]{1,0:T(8,128)(2,1)S(1)}, bf16[640,640]{1,0:T(8,128)(2,1)S(1)}, u32[]{:S(2)}, u32[]{:S(2)}) %collective-permute-start.1) | collective-permute-done | bytes 819232 | tf_op jit(solution)/shard_map/ppermute | solution.py:28
  116.9 0.5 convolution_add_fusion
  117.4 17.8 %all_to_all.35 = f32[4,80,640]{2,1,0:T(8,128)S(1)} all-to-all(f32[4,80,640]{2,1,0:T(8,128)S(1)} %bitcast.33), channel_id=1, replica_groups=mesh['u'=4,'v'=2,'z'=8,'x'=4,'c'=2] {'u'}, dimensions={0} | all-to-all | bytes 1638400 | tf_op jit(solution)/shard_map/all_to_all | solution.py:92
  135.3 14.7 %all_gather.23 = bf16[320,640]{1,0:T(8,128)(2,1)S(1)} all-gather(bf16[80,640]{1,0:T(8,128)(2,1)S(1)} %reduce_sum.97), channel_id=1, replica_groups=mesh['u'=4,'v'=2,'z'=8,'x'=4,'c'=2] {'u'}, dimensions={0}, use_global_device_ids=true | all-gather | bytes 512000 | tf_op jit(solution)/shard_map/all_gather | solution.py:94
  150.0 1.6 copy.13
  151.6 0.9 fusion.1
  152.5 27.1 %all_to_all.36 = f32[8,80,640]{2,1,0:T(8,128)S(1)} all-to-all(f32[8,80,640]{2,1,0:T(8,128)S(1)} %bitcast.32), channel_id=1, replica_groups=mesh['u'=4,'v'=2,'z'=8,'x'=4,'c'=2] {'c','x'}, dimensions={0} | all-to-all | bytes 3276800 | tf_op jit(solution)/shard_map/all_to_all | solution.py:103
  179.6 0.1 reduce_sum.99
  179.7 3.5 %collective-permute-start.3 = (bf16[80,640]{1,0:T(8,128)(2,1)S(1)}, bf16[80,640]{1,0:T(8,128)(2,1)S(1)}, u32[]{:S(2)}, u32[]{:S(2)}) collective-permute-start(bf16[80,640]{1,0:T(8,128)(2,1)S(1)} %reduce_sum.99), channel_id=1, source_target_pairs={{0,0},{2,128},{4,256},{6,384},{128,2},{130,130},{132,258},{134,386... | collective-permute-start | bytes 307208 | tf_op jit(solution)/shard_map/ppermute | solution.py:24
  183.2 0.8 multiply_subtract_fusion
  184.0 10.8 %collective-permute-done.3 = bf16[80,640]{1,0:T(8,128)(2,1)S(1)} collective-permute-done((bf16[80,640]{1,0:T(8,128)(2,1)S(1)}, bf16[80,640]{1,0:T(8,128)(2,1)S(1)}, u32[]{:S(2)}, u32[]{:S(2)}) %collective-permute-start.3) | collective-permute-done | bytes 102432 | tf_op jit(solution)/shard_map/ppermute | solution.py:24
  194.8 0.6 copy.22
  (28 shorter events, 0.4 us)
Async XLA Ops:
  7.2 53.6 %all-gather.10.cloned.1.call-start = ((), (), s32[]{:S(2)}) async-start(), calls=%async_computation.7 | async-start | bytes 1198080 | tf_op jit(solution)/shard_map/all_gather | solution.py:42
  8.8 38.5 %copy-start.1 = (f32[80,640]{1,0:T(8,128)S(1)}, f32[80,640]{1,0:T(8,128)}, u32[]{:S(2)}) copy-start(f32[80,640]{1,0:T(8,128)} %param.8) | copy-start | bytes 614404
  8.8 38.6 %copy-start = (f32[640,80]{0,1:T(8,128)S(1)}, f32[640,80]{0,1:T(8,128)}, u32[]{:S(2)}) copy-start(f32[640,80]{0,1:T(8,128)} %param.9) | copy-start | bytes 614404
  8.8 23.5 %collective-permute-start = (f32[80,640]{1,0:T(8,128)}, f32[80,640]{1,0:T(8,128)S(1)}, u32[]{:S(2)}, u32[]{:S(2)}) collective-permute-start(f32[80,640]{1,0:T(8,128)} %param.8), channel_id=1, source_target_pairs={{0,0},{2,128},{4,256},{6,384},{128,2},{130,130},{132,258},{134,386... | collective-permute-start | bytes 614408 | tf_op jit(solution)/shard_map/ppermute | solution.py:24
  17.2 29.9 %all-to-all-start = ((f32[64,1,1280]{2,1,0:T(1,128)}), f32[64,1,1280]{2,1,0:T(1,128)S(1)}, u32[]{:S(2)}, u32[]{:S(2)}) async-start(f32[64,1,1280]{2,1,0:T(1,128)} %broadcast_in_dim.8), calls=%async_computation | async-start | bytes 655360 | tf_op jit(solution)/shard_map/all_to_all | solution.py:19
  32.2 68.4 %all-gather.8.cloned.1.call-start = ((), (), s32[]{:S(2)}) async-start(), calls=%async_computation.6 | async-start | bytes 1843200 | tf_op jit(solution)/shard_map/all_gather | solution.py:45
  32.3 0.7 copy-start.4
  60.7 35.2 %copy-start.3 = (bf16[832,640]{1,0:T(8,128)(2,1)S(1)}, bf16[832,640]{1,0:T(8,128)(2,1)}, u32[]{:S(2)}) copy-start(bf16[832,640]{1,0:T(8,128)(2,1)} %all-gather.10.cloned.1.call-done) | copy-start | bytes 3194884
  61.4 23.5 %all-to-all-start.2 = ((f32[64,1,160]{2,1,0:T(1,128)}), f32[64,1,160]{2,1,0:T(1,128)S(1)}, u32[]{:S(2)}, u32[]{:S(2)}) async-start(f32[64,1,160]{2,1,0:T(1,128)} %broadcast_in_dim.10), calls=%async_computation.2 | async-start | bytes 131072 | tf_op jit(solution)/shard_map/all_to_all | solution.py:19
  73.6 76.4 %all-gather.6.cloned.1.call-start = ((), (), s32[]{:S(2)}) async-start(), calls=%async_computation.5 | async-start | bytes 1843200 | tf_op jit(solution)/shard_map/all_gather | solution.py:77
  87.5 14.8 %copy-start.2 = (f32[640,80]{0,1:T(8,128)}, f32[640,80]{0,1:T(8,128)S(1)}, u32[]{:S(2)}) copy-start(f32[640,80]{0,1:T(8,128)S(1)} %get-tuple-element.31) | copy-start | bytes 614404
  87.5 7.6 %collective-permute-start.2 = (bf16[80,640]{1,0:T(8,128)(2,1)S(1)}, bf16[80,640]{1,0:T(8,128)(2,1)S(1)}, u32[]{:S(2)}, u32[]{:S(2)}) collective-permute-start(bf16[80,640]{1,0:T(8,128)(2,1)S(1)} %convert_bitcast_fusion.1), channel_id=1, source_target_pairs={{0,64},{64,0},{1,65},{65,1},{2,66},{66,2},{3,67},{67,3},{4,68},{68... | collective-permute-start | bytes 307208 | tf_op jit(solution)/shard_map/ppermute | solution.py:28
  96.0 20.9 %collective-permute-start.1 = (bf16[640,640]{1,0:T(8,128)(2,1)S(1)}, bf16[640,640]{1,0:T(8,128)(2,1)S(1)}, u32[]{:S(2)}, u32[]{:S(2)}) collective-permute-start(bf16[640,640]{1,0:T(8,128)(2,1)S(1)} %bitcast.34), channel_id=1, source_target_pairs={{0,64},{64,0},{1,65},{65,1},{2,66},{66,2},{3,67},{67,3},{4,68},{68... | collective-permute-start | bytes 2457608 | tf_op jit(solution)/shard_map/ppermute | solution.py:28
  179.7 15.1 %collective-permute-start.3 = (bf16[80,640]{1,0:T(8,128)(2,1)S(1)}, bf16[80,640]{1,0:T(8,128)(2,1)S(1)}, u32[]{:S(2)}, u32[]{:S(2)}) collective-permute-start(bf16[80,640]{1,0:T(8,128)(2,1)S(1)} %reduce_sum.99), channel_id=1, source_target_pairs={{0,0},{2,128},{4,256},{6,384},{128,2},{130,130},{132,258},{134,386... | collective-permute-start | bytes 307208 | tf_op jit(solution)/shard_map/ppermute | solution.py:24
Sparse Core Ops, SparseCore 0:
  10.6 50.0 all-gather.9
  62.8 27.9 all-gather.7
  96.1 42.5 all-gather.5

commit v5 on v4

v5 whole, which is shorter than its diff:
```python
import jax
import jax.numpy as jnp
from jax import lax
from jax.sharding import Mesh, PartitionSpec as P


decay = 0.9
F = ("x", "c")
DP = ("u", "v", "z")


def coefficient(quadratic):
    return (1.0 - decay) / (decay * decay * (1.0 + (1.0 - decay) / decay * quadratic))


def share(vec, axes):
    count = lax.axis_size(axes)
    return lax.all_to_all(jnp.broadcast_to(vec[None], (count,) + vec.shape), axes, 0, 0, tiled=True)


def swap_u_x(block, flip):
    n, m = lax.axis_size("u"), lax.axis_size("v")
    moves = [
        ((a * m + w) * n + b, (b * m + (w + flip) % m) * n + a)
        for a in range(n)
        for w in range(m)
        for b in range(n)
    ]
    return lax.ppermute(block, ("u", "v", "x"), moves)


def in_order(own, other):
    return jnp.where(lax.axis_index("v") == 0, jnp.stack([own, other]), jnp.stack([other, own]))


def block_of(vec, index, size):
    return lax.dynamic_slice_in_dim(vec, index * size, size)


def per_device(layer_inputs, out_grads, weight_grad, left_inv, right_inv):
    nu, nv, nz = lax.axis_size("u"), lax.axis_size("v"), lax.axis_size("z")
    nf, ndp = lax.axis_size(F), lax.axis_size(DP)
    token_count = layer_inputs.shape[0] * ndp
    rows, cols = left_inv.shape
    _, z, x, f = (lax.axis_index(axes) for axes in ("u", "z", "x", F))

    weight_pieces = [swap_u_x(weight_grad, flip) for flip in range(2)]
    right_pieces = [swap_u_x(right_inv.T, flip) for flip in range(2)]

    act_local = jnp.sum(layer_inputs, axis=0, dtype=jnp.float32)
    grad_local = jnp.sum(out_grads, axis=0, dtype=jnp.float32)
    sums = share(jnp.concatenate([act_local, grad_local]), DP)
    means = jnp.sum(sums, axis=0) / token_count

    weight_pieces, _ = lax.optimization_barrier((weight_pieces, means))
    weight_wide = lax.all_gather(in_order(*weight_pieces), "z", axis=0, tiled=False)
    weight_wide = weight_wide.transpose(1, 0, 2, 3).reshape(nv * nz * rows, cols)

    left_partial = jnp.sum(left_inv * means[None, :cols], axis=1)
    right_partial = jnp.sum(right_inv * means[cols:, None], axis=0)
    both = share(jnp.concatenate([means, left_partial, right_partial]), F)
    whole_act = both[:, :cols].reshape(nf * cols)
    whole_grad = both[:, cols : 2 * cols].reshape(nf * cols)
    images = jnp.sum(both[:, 2 * cols :], axis=0)
    all_images = share(images, DP)
    left_image = all_images[:, :rows].reshape(ndp * rows)
    right_image = all_images[:, rows:].reshape(ndp * rows)
    left_coef = coefficient(jnp.sum(whole_act * left_image))
    right_coef = coefficient(jnp.sum(whole_grad * right_image))

    left_cols = block_of(left_image, f, cols)
    right_cols = block_of(right_image, f, cols)
    new_left = left_inv / decay - left_coef * images[:rows, None] * left_cols[None, :]
    new_right = right_inv / decay - right_coef * right_cols[:, None] * images[None, rows:]

    row_image = right_image.reshape(nu, nv, nz, rows)[x, :, z]
    col_image = block_of(right_image, lax.axis_index(("u", "c")), cols)
    right_pair = in_order(*right_pieces) / decay - (right_coef * col_image) * row_image[:, :, None]
    right_wide = lax.all_gather(right_pair.astype(jnp.bfloat16), "z", axis=0, tiled=False)

    left_wide = lax.all_gather(new_left.astype(jnp.bfloat16), ("c", "u"), axis=0, tiled=True)
    left_wide = left_wide.reshape(2, nu * rows, cols).transpose(1, 0, 2).reshape(nu * rows, 2 * cols)
    partial = jnp.dot(left_wide, weight_wide, preferred_element_type=jnp.float32)
    pieces = lax.all_to_all(partial.reshape(nu, rows, cols), "x", 0, 0, tiled=True)
    hidden_piece = jnp.sum(pieces, axis=0).astype(jnp.bfloat16)
    hidden = lax.all_gather(hidden_piece, "x", axis=0, tiled=True)

    right_half = right_wide.transpose(1, 0, 2, 3).reshape(nv, nz * rows, cols)
    partial = jnp.einsum(
        "crk,cmk->crm",
        jnp.broadcast_to(hidden[None], (nv,) + hidden.shape),
        right_half,
        preferred_element_type=jnp.float32,
    )
    pieces = lax.all_to_all(partial, "c", 0, 0, tiled=True)
    partial = jnp.sum(pieces, axis=0)
    pieces = lax.all_to_all(partial.reshape(nu, rows, cols), "u", 0, 0, tiled=True)
    precond = jnp.sum(pieces, axis=0).astype(jnp.bfloat16)
    return (precond, new_left, new_right)


def solution(mesh):
    cube = Mesh(mesh.devices.reshape(4, 2, 8, 4, 2), ("u", "v", "z", "x", "c"))
    rows, cols = P(DP, F), P(F, DP)

    return jax.shard_map(
        per_device,
        mesh=cube,
        in_specs=(rows, rows, rows, rows, cols),
        out_specs=(rows, rows, cols),
        check_vma=False,
    )
```

time: 203 us -> 216 us (1.064)
  the two profiles are of different devices: /device:TPU:14 before, /device:TPU:8 now
where the time goes in v5:
time: 216 us
  blocking collectives  100 us (46%)
  waiting for transfers between devices  42.4 us (20%)
  starting transfers between devices  41.1 us (19%)
  between operations  15.6 us (7%)
  other arithmetic  8.24 us (4%)
  matrix products  4.6 us (2%)
  local copies, waits for them, and re-layouts  3.53 us (2%)
    all_gather x1, blocking collectives, per_device(): lax.all_gather(new_left.astype(jnp.bfloat16), ('c', 'u'), axis=0, tiled=T...  51.7 us
    all_to_all x2, starting transfers between devices, share(): lax.all_to_all(jnp.broadcast_to(vec[None], (count,) + vec.shape), axes, 0...  29.1 us
    all_to_all x1, waiting for transfers between devices, per_device(): lax.all_to_all(partial.reshape(nu, rows, cols), 'u', 0, 0, tiled=True)  21.6 us
    all_to_all x2, waiting for transfers between devices, share(): lax.all_to_all(jnp.broadcast_to(vec[None], (count,) + vec.shape), axes, 0...  20.7 us
    all_to_all x1, blocking collectives, per_device(): lax.all_to_all(partial.reshape(nu, rows, cols), 'x', 0, 0, tiled=True)  16 us
    all_to_all x1, blocking collectives, share(): lax.all_to_all(jnp.broadcast_to(vec[None], (count,) + vec.shape), axes, 0...  14.7 us
    all_gather x1, blocking collectives, per_device(): hidden = lax.all_gather(hidden_piece, 'x', axis=0, tiled=True)  12.9 us
    ppermute x4, starting transfers between devices, swap_u_x(): return lax.ppermute(block, ('u', 'v', 'x'), moves)  6.06 us
  transfers between devices with their start and end apart: 9, of which 3 were waited for; matrix products, arithmetic and copies ran while one was open for 4% of the time, Pallas kernels for 0%

profile of v5, /device:TPU:8, one launch (start us, length us, event | category | flops | bytes accessed | tf_op | source)
XLA Modules:
  0.0 215.8 jit_solution(8611723459334347175)
XLA Ops:
  7.2 2.2 %convert_reduce_fusion = (f32[640]{0:T(1024)S(1)}, f32[640]{0:T(1024)S(1)}) fusion(bf16[1024,640]{1,0:T(8,128)(2,1)} %param.6, bf16[1024,640]{1,0:T(8,128)(2,1)} %param.5), kind=kLoop, calls=%fused_computation | loop fusion | flops 2620160 | bytes 2626560 | tf_op jit(solution)/shard_map/reduce_sum | solution.py:51
  9.3 0.0 copy-start
  9.4 0.9 broadcast_in_dim.8
  10.2 16.6 %all-to-all-start = ((f32[64,1,1280]{2,1,0:T(1,128)}), f32[64,1,1280]{2,1,0:T(1,128)S(1)}, u32[]{:S(2)}, u32[]{:S(2)}) async-start(f32[64,1,1280]{2,1,0:T(1,128)} %broadcast_in_dim.8), calls=%async_computation | async-start | bytes 655360 | tf_op jit(solution)/shard_map/all_to_all | solution.py:18
  26.8 0.0 all-gather.3.cloned.1.call-start
  26.9 0.7 collective-permute-start
  27.6 2.4 %collective-permute-start.1 = (bf16[80,640]{1,0:T(8,128)(2,1)S(1)}, bf16[80,640]{1,0:T(8,128)(2,1)S(1)}, u32[]{:S(2)}, u32[]{:S(2)}) collective-permute-start(bf16[80,640]{1,0:T(8,128)(2,1)S(1)} %copy-done.2), channel_id=1, source_target_pairs={{0,64},{2,192},{4,320},{6,448},{64,0},{66,128},{68,256},{70,384},{... | collective-permute-start | bytes 307208 | tf_op jit(solution)/shard_map/ppermute | solution.py:29
  29.9 12.5 %all-to-all-done = f32[64,1,1280]{2,1,0:T(1,128)S(1)} async-done(((f32[64,1,1280]{2,1,0:T(1,128)}), f32[64,1,1280]{2,1,0:T(1,128)S(1)}, u32[]{:S(2)}, u32[]{:S(2)}) %all-to-all-start) | async-done | bytes 327712 | tf_op jit(solution)/shard_map/all_to_all | solution.py:18
  42.4 0.2 reduce_sum.101
  42.6 0.7 maximum_select_fusion.1
  43.4 0.0 all-gather.3.cloned.1.call-update
  43.4 0.1 multiply_reduce_fusion
  43.5 0.1 multiply_reduce_fusion.1
  43.6 0.1 concatenate.35
  43.8 14.7 %all_to_all.39 = f32[8,1,1440]{2,1,0:T(1,128)S(1)} all-to-all(f32[8,1,1440]{2,1,0:T(1,128)S(1)} %broadcast_in_dim.9), channel_id=1, replica_groups=mesh['u'=4,'v'=2,'z'=8,'x'=4,'c'=2] {'x','c'}, dimensions={0} | all-to-all | bytes 92160 | tf_op jit(solution)/shard_map/all_to_all | solution.py:18
  58.5 0.7 broadcast_in_dim.10
  59.1 12.5 %all-to-all-start.2 = ((f32[64,1,160]{2,1,0:T(1,128)}), f32[64,1,160]{2,1,0:T(1,128)S(1)}, u32[]{:S(2)}, u32[]{:S(2)}) async-start(f32[64,1,160]{2,1,0:T(1,128)} %broadcast_in_dim.10), calls=%async_computation.2 | async-start | bytes 131072 | tf_op jit(solution)/shard_map/all_to_all | solution.py:18
  71.7 0.0 all-gather.5.cloned.1.call-start
  71.7 0.7 collective-permute-start.2
  72.4 2.4 %collective-permute-start.3 = (f32[80,640]{1,0:T(8,128)S(1)}, f32[80,640]{1,0:T(8,128)S(1)}, u32[]{:S(2)}, u32[]{:S(2)}) collective-permute-start(f32[80,640]{1,0:T(8,128)S(1)} %bitcast.33), channel_id=1, source_target_pairs={{0,64},{2,192},{4,320},{6,448},{64,0},{66,128},{68,256},{70,384},{... | collective-permute-start | bytes 614408 | tf_op jit(solution)/shard_map/ppermute | solution.py:29
  74.8 8.3 %all-to-all-done.2 = f32[64,1,160]{2,1,0:T(1,128)S(1)} async-done(((f32[64,1,160]{2,1,0:T(1,128)}), f32[64,1,160]{2,1,0:T(1,128)S(1)}, u32[]{:S(2)}, u32[]{:S(2)}) %all-to-all-start.2) | async-done | bytes 40992 | tf_op jit(solution)/shard_map/all_to_all | solution.py:18
  83.1 0.1 fusion.8
  83.1 0.1 reshape.199
  83.2 0.1 reshape.200
  83.3 0.1 reshape.195
  83.4 0.6 fusion.6
  84.7 0.1 dynamic-slice_multiply_fusion
  84.8 0.0 collective-permute-done.3
  84.8 0.8 fusion.2
  85.6 0.0 all-gather.5.cloned.1.call-update
  85.6 0.1 reshape.196
  86.4 0.1 dynamic_slice.12
  86.5 0.1 fusion.10
  86.6 0.8 fusion.7
  87.3 51.7 %all_gather.14 = bf16[640,640]{1,0:T(8,128)(2,1)S(1)} all-gather(bf16[80,640]{1,0:T(8,128)(2,1)S(1)} %get-tuple-element.9), channel_id=1, replica_groups=mesh['u'=4,'v'=2,'z'=8,'x'=4,'c'=2] {'c','u'}, dimensions={0}, use_global_device_ids=true | all-gather | bytes 921600 | tf_op jit(solution)/shard_map/all_gather | solution.py:81
  139.1 0.8 copy.20
  139.9 0.5 dot_general.8
  140.4 0.0 all-gather.3.cloned.1.call-done
  140.5 2.2 %fusion.11 = f32[4,80,640]{2,1,0:T(8,128)S(1)} fusion(bf16[4,80,1280]{2,1,0:T(8,128)(2,1)S(1)} %dot_general.8, bf16[1280,640,1]{1,0,2:T(8,128)(2,1)} %bitcast.43), kind=kOutput, calls=%fused_computation.31 | convolution fusion | flops 524288000 | bytes 3276800 | tf_op jit(solution)/shard_map/dot_general | solution.py:83
  142.7 16.0 %all_to_all.40 = f32[4,80,640]{2,1,0:T(8,128)S(1)} all-to-all(f32[4,80,640]{2,1,0:T(8,128)S(1)} %fusion.11), channel_id=1, replica_groups=mesh['u'=4,'v'=2,'z'=8,'x'=4,'c'=2] {'x'}, dimensions={0} | all-to-all | bytes 1638400 | tf_op jit(solution)/shard_map/all_to_all | solution.py:84
  158.7 12.9 %all_gather.16 = bf16[320,640]{1,0:T(8,128)(2,1)S(1)} all-gather(bf16[80,640]{1,0:T(8,128)(2,1)S(1)} %reduce_sum.106), channel_id=1, replica_groups=mesh['u'=4,'v'=2,'z'=8,'x'=4,'c'=2] {'x'}, dimensions={0}, use_global_device_ids=true | all-gather | bytes 512000 | tf_op jit(solution)/shard_map/all_gather | solution.py:86
  171.7 2.4 %fusion.3 = f32[2,320,640]{2,1,0:T(8,128)S(1)} fusion(bf16[2,640,640]{2,1,0:T(8,128)(2,1)} %bitcast.31, bf16[320,640]{1,0:T(8,128)(2,1)S(1)} %all_gather.16), kind=kOutput, calls=%fused_computation.7 | convolution fusion | flops 524288000 | bytes 3686400 | tf_op jit(solution)/shard_map/crk,cmk->crm/dot_general | solution.py:89
  174.0 5.0 %all_to_all.41 = f32[2,320,640]{2,1,0:T(8,128)S(1)} all-to-all(f32[2,320,640]{2,1,0:T(8,128)S(1)} %fusion.3), channel_id=1, replica_groups=mesh['u'=4,'v'=2,'z'=8,'x'=4,'c'=2] {'c'}, dimensions={0} | all-to-all | bytes 3276800 | tf_op jit(solution)/shard_map/all_to_all | solution.py:95
  179.1 1.1 reduce_sum.108
  180.1 5.8 %all-to-all-start.5 = ((f32[4,80,640]{2,1,0:T(8,128)}), f32[4,80,640]{2,1,0:T(8,128)S(1)}, u32[]{:S(2)}, u32[]{:S(2)}) async-start(f32[4,80,640]{2,1,0:T(8,128)} %bitcast.14), calls=%async_computation.5 | async-start | bytes 1638400 | tf_op jit(solution)/shard_map/all_to_all | solution.py:97
  185.9 0.8 multiply_subtract_fusion
  186.7 21.6 %all-to-all-done.5 = f32[4,80,640]{2,1,0:T(8,128)S(1)} async-done(((f32[4,80,640]{2,1,0:T(8,128)}), f32[4,80,640]{2,1,0:T(8,128)S(1)}, u32[]{:S(2)}, u32[]{:S(2)}) %all-to-all-start.5) | async-done | bytes 819232 | tf_op jit(solution)/shard_map/all_to_all | solution.py:97
  208.3 0.7 reduce_sum.109
  (18 shorter events, 0.2 us)
Async XLA Ops:
  7.2 19.7 %copy-start.2 = (bf16[80,640]{1,0:T(8,128)(2,1)S(1)}, bf16[80,640]{1,0:T(8,128)(2,1)}, u32[]{:S(2)}) copy-start(bf16[80,640]{1,0:T(8,128)(2,1)} %param.7) | copy-start | bytes 307204
  9.3 34.1 %copy-start.1 = (f32[640,80]{0,1:T(8,128)S(1)}, f32[640,80]{0,1:T(8,128)}, u32[]{:S(2)}) copy-start(f32[640,80]{0,1:T(8,128)} %param.9) | copy-start | bytes 614404
  9.3 34.2 %copy-start = (f32[80,640]{1,0:T(8,128)S(1)}, f32[80,640]{1,0:T(8,128)}, u32[]{:S(2)}) copy-start(f32[80,640]{1,0:T(8,128)} %param.8) | copy-start | bytes 614404
  10.2 32.2 %all-to-all-start = ((f32[64,1,1280]{2,1,0:T(1,128)}), f32[64,1,1280]{2,1,0:T(1,128)S(1)}, u32[]{:S(2)}, u32[]{:S(2)}) async-start(f32[64,1,1280]{2,1,0:T(1,128)} %broadcast_in_dim.8), calls=%async_computation | async-start | bytes 655360 | tf_op jit(solution)/shard_map/all_to_all | solution.py:18
  26.8 113.6 %all-gather.3.cloned.1.call-start = ((), (), s32[]{:S(2)}) async-start(), calls=%async_computation.6 | async-start | bytes 1843200 | tf_op jit(solution)/shard_map/all_gather | solution.py:56
  26.9 15.7 %collective-permute-start = (bf16[80,640]{1,0:T(8,128)(2,1)S(1)}, bf16[80,640]{1,0:T(8,128)(2,1)S(1)}, u32[]{:S(2)}, u32[]{:S(2)}) collective-permute-start(bf16[80,640]{1,0:T(8,128)(2,1)S(1)} %copy-done.2), channel_id=1, source_target_pairs={{0,0},{2,128},{4,256},{6,384},{64,64},{66,192},{68,320},{70,448},{... | collective-permute-start | bytes 307208 | tf_op jit(solution)/shard_map/ppermute | solution.py:29
  27.6 15.1 %collective-permute-start.1 = (bf16[80,640]{1,0:T(8,128)(2,1)S(1)}, bf16[80,640]{1,0:T(8,128)(2,1)S(1)}, u32[]{:S(2)}, u32[]{:S(2)}) collective-permute-start(bf16[80,640]{1,0:T(8,128)(2,1)S(1)} %copy-done.2), channel_id=1, source_target_pairs={{0,64},{2,192},{4,320},{6,448},{64,0},{66,128},{68,256},{70,384},{... | collective-permute-start | bytes 307208 | tf_op jit(solution)/shard_map/ppermute | solution.py:29
  59.1 23.9 %all-to-all-start.2 = ((f32[64,1,160]{2,1,0:T(1,128)}), f32[64,1,160]{2,1,0:T(1,128)S(1)}, u32[]{:S(2)}, u32[]{:S(2)}) async-start(f32[64,1,160]{2,1,0:T(1,128)} %broadcast_in_dim.10), calls=%async_computation.2 | async-start | bytes 131072 | tf_op jit(solution)/shard_map/all_to_all | solution.py:18
  71.7 100.0 %all-gather.5.cloned.1.call-start = ((), (), s32[]{:S(2)}) async-start(), calls=%async_computation.7 | async-start | bytes 1843200 | tf_op jit(solution)/shard_map/all_gather | solution.py:79
  71.7 13.1 %collective-permute-start.2 = (f32[80,640]{1,0:T(8,128)S(1)}, f32[80,640]{1,0:T(8,128)S(1)}, u32[]{:S(2)}, u32[]{:S(2)}) collective-permute-start(f32[80,640]{1,0:T(8,128)S(1)} %bitcast.32), channel_id=1, source_target_pairs={{0,0},{2,128},{4,256},{6,384},{64,64},{66,192},{68,320},{70,448},{... | collective-permute-start | bytes 614408 | tf_op jit(solution)/shard_map/ppermute | solution.py:29
  72.4 12.4 %collective-permute-start.3 = (f32[80,640]{1,0:T(8,128)S(1)}, f32[80,640]{1,0:T(8,128)S(1)}, u32[]{:S(2)}, u32[]{:S(2)}) collective-permute-start(f32[80,640]{1,0:T(8,128)S(1)} %bitcast.33), channel_id=1, source_target_pairs={{0,64},{2,192},{4,320},{6,448},{64,0},{66,128},{68,256},{70,384},{... | collective-permute-start | bytes 614408 | tf_op jit(solution)/shard_map/ppermute | solution.py:29
  180.1 28.1 %all-to-all-start.5 = ((f32[4,80,640]{2,1,0:T(8,128)}), f32[4,80,640]{2,1,0:T(8,128)S(1)}, u32[]{:S(2)}, u32[]{:S(2)}) async-start(f32[4,80,640]{2,1,0:T(8,128)} %bitcast.14), calls=%async_computation.5 | async-start | bytes 1638400 | tf_op jit(solution)/shard_map/all_to_all | solution.py:97
Sparse Core Ops, SparseCore 0:
  43.5 48.9 all-gather.2
  95.1 51.2 all-gather.4

commit v6 on v5

--- a/solution.py
+++ b/solution.py
@@ -42,7 +42,9 @@
     nf, ndp = lax.axis_size(F), lax.axis_size(DP)
     token_count = layer_inputs.shape[0] * ndp
     rows, cols = left_inv.shape
-    _, z, x, f = (lax.axis_index(axes) for axes in ("u", "z", "x", F))
+    v, z, x, f = (lax.axis_index(axes) for axes in ("v", "z", "x", F))
+
+    left_wide = lax.all_gather(left_inv, ("c", "u"), axis=0, tiled=False)
 
     weight_pieces = [swap_u_x(weight_grad, flip) for flip in range(2)]
     right_pieces = [swap_u_x(right_inv.T, flip) for flip in range(2)]
@@ -78,9 +80,14 @@
     right_pair = in_order(*right_pieces) / decay - (right_coef * col_image) * row_image[:, :, None]
     right_wide = lax.all_gather(right_pair.astype(jnp.bfloat16), "z", axis=0, tiled=False)
 
-    left_wide = lax.all_gather(new_left.astype(jnp.bfloat16), ("c", "u"), axis=0, tiled=True)
-    left_wide = left_wide.reshape(2, nu * rows, cols).transpose(1, 0, 2).reshape(nu * rows, 2 * cols)
-    partial = jnp.dot(left_wide, weight_wide, preferred_element_type=jnp.float32)
+    row_image = lax.dynamic_index_in_dim(
+        left_image.reshape(nu, nv * nz, rows), v * nz + z, 1, keepdims=False
+    )
+    col_image = left_image.reshape(nu, 2, cols)[x]
+    left_wide = left_wide.reshape(2, nu, rows, cols)
+    left_wide = left_wide / decay - (left_coef * row_image[:, :, None]) * col_image[:, None, None, :]
+    left_half = left_wide.astype(jnp.bfloat16).transpose(1, 2, 0, 3).reshape(nu * rows, 2 * cols)
+    partial = jnp.dot(left_half, weight_wide, preferred_element_type=jnp.float32)
     pieces = lax.all_to_all(partial.reshape(nu, rows, cols), "x", 0, 0, tiled=True)
     hidden_piece = jnp.sum(pieces, axis=0).astype(jnp.bfloat16)
     hidden = lax.all_gather(hidden_piece, "x", axis=0, tiled=True)

time: 216 us -> 205 us (0.949)
  the two profiles are of different devices: /device:TPU:8 before, /device:TPU:1 now
where the time goes in v6:
time: 205 us; the launch traced here: 204 us
  blocking collectives  82.9 us (40%)
  waiting for transfers between devices  46.8 us (23%)
  starting transfers between devices  40.8 us (20%)
  between operations  15.4 us (8%)
  other arithmetic  11.1 us (5%)
  matrix products  4.62 us (2%)
  local copies, waits for them, and re-layouts  2.8 us (1%)
    all_to_all x1, blocking collectives, per_device(): lax.all_to_all(partial.reshape(nu, rows, cols), 'x', 0, 0, tiled=True)  32.1 us
    all_to_all x1, blocking collectives, share(): lax.all_to_all(jnp.broadcast_to(vec[None], (count,) + vec.shape), axes, 0...  30.4 us
    all_to_all x2, starting transfers between devices, share(): lax.all_to_all(jnp.broadcast_to(vec[None], (count,) + vec.shape), axes, 0...  27 us
    all_to_all x1, waiting for transfers between devices, per_device(): lax.all_to_all(partial.reshape(nu, rows, cols), 'u', 0, 0, tiled=True)  19.5 us
    all_to_all x2, waiting for transfers between devices, share(): lax.all_to_all(jnp.broadcast_to(vec[None], (count,) + vec.shape), axes, 0...  17.6 us
    all_gather x1, blocking collectives, per_device(): hidden = lax.all_gather(hidden_piece, 'x', axis=0, tiled=True)  11.1 us
    all_to_all x1, blocking collectives, per_device(): pieces = lax.all_to_all(partial, 'c', 0, 0, tiled=True)  9.3 us
    ppermute x4, starting transfers between devices, swap_u_x(): return lax.ppermute(block, ('u', 'v', 'x'), moves)  7.19 us
  transfers between devices with their start and end apart: 10, of which 6 were waited for; matrix products, arithmetic and copies ran while one was open for 7% of the time, Pallas kernels for 0%

profile of v6, /device:TPU:1, one launch (start us, length us, event | category | flops | bytes accessed | tf_op | source)
XLA Modules:
  0.0 204.3 jit_solution(10723866048978764190)
XLA Ops:
  7.2 0.7 all-gather.9.cloned.1.call-update
  7.9 2.2 %convert_reduce_fusion = (f32[640]{0:T(1024)S(1)}, f32[640]{0:T(1024)S(1)}) fusion(bf16[1024,640]{1,0:T(8,128)(2,1)} %param.6, bf16[1024,640]{1,0:T(8,128)(2,1)} %param.5), kind=kLoop, calls=%fused_computation | loop fusion | flops 2620160 | bytes 2626560 | tf_op jit(solution)/shard_map/reduce_sum | solution.py:53
  10.1 0.9 broadcast_in_dim.8
  11.0 17.1 %all-to-all-start = ((f32[64,1,1280]{2,1,0:T(1,128)}), f32[64,1,1280]{2,1,0:T(1,128)S(1)}, u32[]{:S(2)}, u32[]{:S(2)}) async-start(f32[64,1,1280]{2,1,0:T(1,128)} %broadcast_in_dim.8), calls=%async_computation | async-start | bytes 655360 | tf_op jit(solution)/shard_map/all_to_all | solution.py:18
  28.1 0.0 all-gather.5.cloned.1.call-start
  28.2 0.7 collective-permute-start
  28.9 2.9 %collective-permute-start.1 = (bf16[80,640]{1,0:T(8,128)(2,1)S(1)}, bf16[80,640]{1,0:T(8,128)(2,1)S(1)}, u32[]{:S(2)}, u32[]{:S(2)}) collective-permute-start(bf16[80,640]{1,0:T(8,128)(2,1)S(1)} %copy-done.2), channel_id=1, source_target_pairs={{0,64},{2,192},{4,320},{6,448},{64,0},{66,128},{68,256},{70,384},{... | collective-permute-start | bytes 307208 | tf_op jit(solution)/shard_map/ppermute | solution.py:29
  31.8 10.2 %all-to-all-done = f32[64,1,1280]{2,1,0:T(1,128)S(1)} async-done(((f32[64,1,1280]{2,1,0:T(1,128)}), f32[64,1,1280]{2,1,0:T(1,128)S(1)}, u32[]{:S(2)}, u32[]{:S(2)}) %all-to-all-start) | async-done | bytes 327712 | tf_op jit(solution)/shard_map/all_to_all | solution.py:18
  42.0 0.2 reduce_sum.101
  42.2 1.2 collective-permute-done.1
  43.4 0.7 maximum_select_fusion.1
  44.2 0.1 multiply_reduce_fusion.1
  44.3 0.1 multiply_reduce_fusion
  44.4 0.1 concatenate.35
  44.5 30.4 %all_to_all.39 = f32[8,1,1440]{2,1,0:T(1,128)S(1)} all-to-all(f32[8,1,1440]{2,1,0:T(1,128)S(1)} %broadcast_in_dim.9), channel_id=1, replica_groups=mesh['u'=4,'v'=2,'z'=8,'x'=4,'c'=2] {'x','c'}, dimensions={0} | all-to-all | bytes 92160 | tf_op jit(solution)/shard_map/all_to_all | solution.py:18
  74.9 0.7 broadcast_in_dim.10
  75.6 9.9 %all-to-all-start.2 = ((f32[64,1,160]{2,1,0:T(1,128)}), f32[64,1,160]{2,1,0:T(1,128)S(1)}, u32[]{:S(2)}, u32[]{:S(2)}) async-start(f32[64,1,160]{2,1,0:T(1,128)} %broadcast_in_dim.10), calls=%async_computation.2 | async-start | bytes 131072 | tf_op jit(solution)/shard_map/all_to_all | solution.py:18
  85.5 0.0 all-gather.7.cloned.1.call-start
  85.6 0.7 collective-permute-start.2
  86.2 2.9 %collective-permute-start.3 = (f32[80,640]{1,0:T(8,128)S(1)}, f32[80,640]{1,0:T(8,128)S(1)}, u32[]{:S(2)}, u32[]{:S(2)}) collective-permute-start(f32[80,640]{1,0:T(8,128)S(1)} %bitcast.35), channel_id=1, source_target_pairs={{0,64},{2,192},{4,320},{6,448},{64,0},{66,128},{68,256},{70,384},{... | collective-permute-start | bytes 614408 | tf_op jit(solution)/shard_map/ppermute | solution.py:29
  89.2 7.5 %all-to-all-done.2 = f32[64,1,160]{2,1,0:T(1,128)S(1)} async-done(((f32[64,1,160]{2,1,0:T(1,128)}), f32[64,1,160]{2,1,0:T(1,128)S(1)}, u32[]{:S(2)}, u32[]{:S(2)}) %all-to-all-start.2) | async-done | bytes 40992 | tf_op jit(solution)/shard_map/all_to_all | solution.py:18
  96.6 0.1 fusion.9
  96.7 0.1 reshape.209
  96.8 0.1 reshape.210
  96.9 0.1 reshape.207
  97.0 0.6 fusion.8
  98.3 0.1 dynamic-slice_multiply_fusion
  98.4 0.8 fusion.4
  99.2 0.1 reshape_reshape.10
  100.1 1.6 broadcast_multiply_fusion
  101.7 1.3 fusion.1
  102.9 0.5 dot_general.8
  103.5 3.4 %all-gather.5.cloned.1.call-done = bf16[8,2,80,640]{3,2,0,1:T(8,128)(2,1)} async-done(((bf16[1,2,80,640]{3,2,0,1:T(8,128)(2,1)}), bf16[8,2,80,640]{3,2,0,1:T(8,128)(2,1)}) %all-gather.5.cloned.1.call-update) | async-done | bytes 1638416 | tf_op jit(solution)/shard_map/all_gather | solution.py:58
  106.9 2.2 %fusion.12 = f32[4,80,640]{2,1,0:T(8,128)S(1)} fusion(bf16[4,80,1280]{2,1,0:T(8,128)(2,1)S(1)} %dot_general.8, bf16[1280,640,1]{1,0,2:T(8,128)(2,1)} %bitcast.47), kind=kOutput, calls=%fused_computation.35 | convolution fusion | flops 524288000 | bytes 3276800 | tf_op jit(solution)/shard_map/dot_general | solution.py:90
  109.1 32.1 %all_to_all.40 = f32[4,80,640]{2,1,0:T(8,128)S(1)} all-to-all(f32[4,80,640]{2,1,0:T(8,128)S(1)} %fusion.12), channel_id=1, replica_groups=mesh['u'=4,'v'=2,'z'=8,'x'=4,'c'=2] {'x'}, dimensions={0} | all-to-all | bytes 1638400 | tf_op jit(solution)/shard_map/all_to_all | solution.py:91
  141.3 11.1 %all_gather.20 = bf16[320,640]{1,0:T(8,128)(2,1)S(1)} all-gather(bf16[80,640]{1,0:T(8,128)(2,1)S(1)} %reduce_sum.106), channel_id=1, replica_groups=mesh['u'=4,'v'=2,'z'=8,'x'=4,'c'=2] {'x'}, dimensions={0}, use_global_device_ids=true | all-gather | bytes 512000 | tf_op jit(solution)/shard_map/all_gather | solution.py:93
  152.4 4.3 %all-gather.7.cloned.1.call-done = bf16[8,2,80,640]{3,2,0,1:T(8,128)(2,1)} async-done(((bf16[1,2,80,640]{3,2,0,1:T(8,128)(2,1)}), bf16[8,2,80,640]{3,2,0,1:T(8,128)(2,1)}) %all-gather.7.cloned.1.call-update) | async-done | bytes 1638416 | tf_op jit(solution)/shard_map/all_gather | solution.py:81
  156.7 2.4 %fusion.5 = f32[2,320,640]{2,1,0:T(8,128)S(1)} fusion(bf16[2,640,640]{2,1,0:T(8,128)(2,1)} %bitcast.33, bf16[320,640]{1,0:T(8,128)(2,1)S(1)} %all_gather.20), kind=kOutput, calls=%fused_computation.10 | convolution fusion | flops 524288000 | bytes 3686400 | tf_op jit(solution)/shard_map/crk,cmk->crm/dot_general | solution.py:96
  159.1 9.3 %all_to_all.41 = f32[2,320,640]{2,1,0:T(8,128)S(1)} all-to-all(f32[2,320,640]{2,1,0:T(8,128)S(1)} %fusion.5), channel_id=1, replica_groups=mesh['u'=4,'v'=2,'z'=8,'x'=4,'c'=2] {'c'}, dimensions={0} | all-to-all | bytes 3276800 | tf_op jit(solution)/shard_map/all_to_all | solution.py:102
  168.4 1.1 reduce_sum.108
  169.4 6.4 %all-to-all-start.5 = ((f32[4,80,640]{2,1,0:T(8,128)}), f32[4,80,640]{2,1,0:T(8,128)S(1)}, u32[]{:S(2)}, u32[]{:S(2)}) async-start(f32[4,80,640]{2,1,0:T(8,128)} %bitcast.17), calls=%async_computation.5 | async-start | bytes 1638400 | tf_op jit(solution)/shard_map/all_to_all | solution.py:104
  175.9 0.1 reshape.213
  176.0 0.1 dynamic_slice.23
  176.1 0.1 fusion.11
  176.1 0.8 multiply_subtract_fusion
  176.9 0.8 multiply_subtract_fusion.1
  177.7 19.5 %all-to-all-done.5 = f32[4,80,640]{2,1,0:T(8,128)S(1)} async-done(((f32[4,80,640]{2,1,0:T(8,128)}), f32[4,80,640]{2,1,0:T(8,128)S(1)}, u32[]{:S(2)}, u32[]{:S(2)}) %all-to-all-start.5) | async-done | bytes 819232 | tf_op jit(solution)/shard_map/all_to_all | solution.py:104
  197.1 0.7 reduce_sum.109
  (24 shorter events, 0.3 us)
Async XLA Ops:
  7.2 92.9 %all-gather.9.cloned.1.call-start = ((), (), s32[]{:S(2)}) async-start(), calls=%async_computation.8 | async-start | bytes 1843200 | tf_op jit(solution)/shard_map/all_gather | solution.py:47
  7.9 20.3 %copy-start.2 = (bf16[80,640]{1,0:T(8,128)(2,1)S(1)}, bf16[80,640]{1,0:T(8,128)(2,1)}, u32[]{:S(2)}) copy-start(bf16[80,640]{1,0:T(8,128)(2,1)} %param.7) | copy-start | bytes 307204
  10.1 34.1 %copy-start = (f32[80,640]{1,0:T(8,128)S(1)}, f32[80,640]{1,0:T(8,128)}, u32[]{:S(2)}) copy-start(f32[80,640]{1,0:T(8,128)} %param.8) | copy-start | bytes 614404
  10.1 34.2 %copy-start.1 = (f32[640,80]{0,1:T(8,128)S(1)}, f32[640,80]{0,1:T(8,128)}, u32[]{:S(2)}) copy-start(f32[640,80]{0,1:T(8,128)} %param.9) | copy-start | bytes 614404
  11.0 31.0 %all-to-all-start = ((f32[64,1,1280]{2,1,0:T(1,128)}), f32[64,1,1280]{2,1,0:T(1,128)S(1)}, u32[]{:S(2)}, u32[]{:S(2)}) async-start(f32[64,1,1280]{2,1,0:T(1,128)} %broadcast_in_dim.8), calls=%async_computation | async-start | bytes 655360 | tf_op jit(solution)/shard_map/all_to_all | solution.py:18
  28.1 78.8 %all-gather.5.cloned.1.call-start = ((), (), s32[]{:S(2)}) async-start(), calls=%async_computation.6 | async-start | bytes 1843200 | tf_op jit(solution)/shard_map/all_gather | solution.py:58
  28.2 14.0 %collective-permute-start = (bf16[80,640]{1,0:T(8,128)(2,1)S(1)}, bf16[80,640]{1,0:T(8,128)(2,1)S(1)}, u32[]{:S(2)}, u32[]{:S(2)}) collective-permute-start(bf16[80,640]{1,0:T(8,128)(2,1)S(1)} %copy-done.2), channel_id=1, source_target_pairs={{0,0},{2,128},{4,256},{6,384},{64,64},{66,192},{68,320},{70,448},{... | collective-permute-start | bytes 307208 | tf_op jit(solution)/shard_map/ppermute | solution.py:29
  28.9 14.6 %collective-permute-start.1 = (bf16[80,640]{1,0:T(8,128)(2,1)S(1)}, bf16[80,640]{1,0:T(8,128)(2,1)S(1)}, u32[]{:S(2)}, u32[]{:S(2)}) collective-permute-start(bf16[80,640]{1,0:T(8,128)(2,1)S(1)} %copy-done.2), channel_id=1, source_target_pairs={{0,64},{2,192},{4,320},{6,448},{64,0},{66,128},{68,256},{70,384},{... | collective-permute-start | bytes 307208 | tf_op jit(solution)/shard_map/ppermute | solution.py:29
  75.6 21.0 %all-to-all-start.2 = ((f32[64,1,160]{2,1,0:T(1,128)}), f32[64,1,160]{2,1,0:T(1,128)S(1)}, u32[]{:S(2)}, u32[]{:S(2)}) async-start(f32[64,1,160]{2,1,0:T(1,128)} %broadcast_in_dim.10), calls=%async_computation.2 | async-start | bytes 131072 | tf_op jit(solution)/shard_map/all_to_all | solution.py:18
  85.5 71.2 %all-gather.7.cloned.1.call-start = ((), (), s32[]{:S(2)}) async-start(), calls=%async_computation.7 | async-start | bytes 1843200 | tf_op jit(solution)/shard_map/all_gather | solution.py:81
  85.6 12.8 %collective-permute-start.2 = (f32[80,640]{1,0:T(8,128)S(1)}, f32[80,640]{1,0:T(8,128)S(1)}, u32[]{:S(2)}, u32[]{:S(2)}) collective-permute-start(f32[80,640]{1,0:T(8,128)S(1)} %bitcast.34), channel_id=1, source_target_pairs={{0,0},{2,128},{4,256},{6,384},{64,64},{66,192},{68,320},{70,448},{... | collective-permute-start | bytes 614408 | tf_op jit(solution)/shard_map/ppermute | solution.py:29
  86.2 12.2 %collective-permute-start.3 = (f32[80,640]{1,0:T(8,128)S(1)}, f32[80,640]{1,0:T(8,128)S(1)}, u32[]{:S(2)}, u32[]{:S(2)}) collective-permute-start(f32[80,640]{1,0:T(8,128)S(1)} %bitcast.35), channel_id=1, source_target_pairs={{0,64},{2,192},{4,320},{6,448},{64,0},{66,128},{68,256},{70,384},{... | collective-permute-start | bytes 614408 | tf_op jit(solution)/shard_map/ppermute | solution.py:29
  169.4 27.7 %all-to-all-start.5 = ((f32[4,80,640]{2,1,0:T(8,128)}), f32[4,80,640]{2,1,0:T(8,128)S(1)}, u32[]{:S(2)}, u32[]{:S(2)}) async-start(f32[4,80,640]{2,1,0:T(8,128)} %bitcast.17), calls=%async_computation.5 | async-start | bytes 1638400 | tf_op jit(solution)/shard_map/all_to_all | solution.py:104
Sparse Core Ops, SparseCore 0:
  10.1 55.9 all-gather.8
  68.8 38.0 all-gather.4
  109.5 47.0 all-gather.6

commit v7 on v6

--- a/solution.py
+++ b/solution.py
@@ -29,6 +29,11 @@
     return lax.ppermute(block, ("u", "v", "x"), moves)
 
 
+def swap_v_c(block, flip):
+    moves = [(2 * a + b, 2 * ((b + flip) % 2) + a) for a in range(2) for b in range(2)]
+    return lax.ppermute(block, ("v", "c"), moves)
+
+
 def in_order(own, other):
     return jnp.where(lax.axis_index("v") == 0, jnp.stack([own, other]), jnp.stack([other, own]))
 
@@ -47,16 +52,10 @@
     left_wide = lax.all_gather(left_inv, ("c", "u"), axis=0, tiled=False)
 
     weight_pieces = [swap_u_x(weight_grad, flip) for flip in range(2)]
-    right_pieces = [swap_u_x(right_inv.T, flip) for flip in range(2)]
-
     act_local = jnp.sum(layer_inputs, axis=0, dtype=jnp.float32)
     grad_local = jnp.sum(out_grads, axis=0, dtype=jnp.float32)
     sums = share(jnp.concatenate([act_local, grad_local]), DP)
     means = jnp.sum(sums, axis=0) / token_count
-
-    weight_pieces, _ = lax.optimization_barrier((weight_pieces, means))
-    weight_wide = lax.all_gather(in_order(*weight_pieces), "z", axis=0, tiled=False)
-    weight_wide = weight_wide.transpose(1, 0, 2, 3).reshape(nv * nz * rows, cols)
 
     left_partial = jnp.sum(left_inv * means[None, :cols], axis=1)
     right_partial = jnp.sum(right_inv * means[cols:, None], axis=0)
@@ -64,6 +63,9 @@
     whole_act = both[:, :cols].reshape(nf * cols)
     whole_grad = both[:, cols : 2 * cols].reshape(nf * cols)
     images = jnp.sum(both[:, 2 * cols :], axis=0)
+    weight_pieces, _ = lax.optimization_barrier((weight_pieces, images))
+    weight_wide = lax.all_gather(in_order(*weight_pieces), "z", axis=0, tiled=False)
+    weight_wide = weight_wide.transpose(1, 0, 2, 3).reshape(nv * nz * rows, cols)
     all_images = share(images, DP)
     left_image = all_images[:, :rows].reshape(ndp * rows)
     right_image = all_images[:, rows:].reshape(ndp * rows)
@@ -75,10 +77,9 @@
     new_left = left_inv / decay - left_coef * images[:rows, None] * left_cols[None, :]
     new_right = right_inv / decay - right_coef * right_cols[:, None] * images[None, rows:]
 
-    row_image = right_image.reshape(nu, nv, nz, rows)[x, :, z]
-    col_image = block_of(right_image, lax.axis_index(("u", "c")), cols)
-    right_pair = in_order(*right_pieces) / decay - (right_coef * col_image) * row_image[:, :, None]
-    right_wide = lax.all_gather(right_pair.astype(jnp.bfloat16), "z", axis=0, tiled=False)
+    right_own = new_right.astype(jnp.bfloat16).T
+    right_pieces = [swap_v_c(right_own, flip) for flip in range(2)]
+    right_wide = lax.all_gather(in_order(*right_pieces), "z", axis=0, tiled=False)
 
     row_image = lax.dynamic_index_in_dim(
         left_image.reshape(nu, nv * nz, rows), v * nz + z, 1, keepdims=False
@@ -94,7 +95,7 @@
 
     right_half = right_wide.transpose(1, 0, 2, 3).reshape(nv, nz * rows, cols)
     partial = jnp.einsum(
-        "crk,cmk->crm",
+        "crk,ckm->crm",
         jnp.broadcast_to(hidden[None], (nv,) + hidden.shape),
         right_half,
         preferred_element_type=jnp.float32,

time: 205 us -> 199 us (0.971)
  blocking collectives: 82.9 us -> 63.8 us
  waiting for transfers between devices: 46.8 us -> 57.2 us
  starting transfers between devices: 40.8 us -> 43.4 us
    all_to_all x1, blocking collectives: 32.1 us -> 13.2 us  [per_device(): lax.all_to_all(partial.reshape(nu, rows, cols), 'x', 0, 0, tiled=True)]
    all_gather x1, waiting for transfers between devices: 4.29 us -> 16.1 us  [per_device(): lax.all_gather(in_order(*right_pieces), 'z', axis=0, tiled=False)]
    all_to_all x2, waiting for transfers between devices: 17.6 us -> 11.1 us  [share(): lax.all_to_all(jnp.broadcast_to(vec[None], (count,) + vec.shape), axes, 0...]
    ppermute x0 -> x2, starting transfers between devices: none -> 6.32 us  [swap_v_c(): return lax.ppermute(block, ('v', 'c'), moves)]
    ppermute x0 -> x2, waiting for transfers between devices: none -> 3.88 us  [swap_v_c(): return lax.ppermute(block, ('v', 'c'), moves)]
    ppermute x4 -> x2, waiting for transfers between devices: 1.23 us -> 5.05 us  [swap_u_x(): return lax.ppermute(block, ('u', 'v', 'x'), moves)]
    all_gather x1, waiting for transfers between devices: 3.41 us -> 0.02 us  [per_device(): lax.all_gather(in_order(*weight_pieces), 'z', axis=0, tiled=False)]
    ppermute x4 -> x2, starting transfers between devices: 7.19 us -> 4.73 us  [swap_u_x(): return lax.ppermute(block, ('u', 'v', 'x'), moves)]
where the time goes in v7:
time: 199 us; the launch traced here: 198 us
  blocking collectives  63.8 us (32%)
  waiting for transfers between devices  57.2 us (29%)
  starting transfers between devices  43.4 us (22%)
  between operations  15.3 us (8%)
  other arithmetic  11.1 us (6%)
  matrix products  4.57 us (2%)
  local copies, waits for them, and re-layouts  2.7 us (1%)
    all_to_all x1, blocking collectives, share(): lax.all_to_all(jnp.broadcast_to(vec[None], (count,) + vec.shape), axes, 0...  30.8 us
    all_to_all x2, starting transfers between devices, share(): lax.all_to_all(jnp.broadcast_to(vec[None], (count,) + vec.shape), axes, 0...  25.8 us
    all_to_all x1, waiting for transfers between devices, per_device(): lax.all_to_all(partial.reshape(nu, rows, cols), 'u', 0, 0, tiled=True)  20.3 us
    all_gather x1, waiting for transfers between devices, per_device(): lax.all_gather(in_order(*right_pieces), 'z', axis=0, tiled=False)  16.1 us
    all_to_all x1, blocking collectives, per_device(): lax.all_to_all(partial.reshape(nu, rows, cols), 'x', 0, 0, tiled=True)  13.2 us
    all_to_all x2, waiting for transfers between devices, share(): lax.all_to_all(jnp.broadcast_to(vec[None], (count,) + vec.shape), axes, 0...  11.1 us
    all_gather x1, blocking collectives, per_device(): hidden = lax.all_gather(hidden_piece, 'x', axis=0, tiled=True)  10.5 us
    all_to_all x1, blocking collectives, per_device(): pieces = lax.all_to_all(partial, 'c', 0, 0, tiled=True)  9.35 us
  transfers between devices with their start and end apart: 10, of which 6 were waited for; matrix products, arithmetic and copies ran while one was open for 7% of the time, Pallas kernels for 0%

profile of v7, /device:TPU:1, one launch (start us, length us, event | category | flops | bytes accessed | tf_op | source)
XLA Modules:
  0.0 198.1 jit_solution(10349015807059609508)
XLA Ops:
  7.2 0.7 all-gather.9.cloned.1.call-update
  7.9 2.2 %convert_reduce_fusion = (f32[640]{0:T(1024)S(1)}, f32[640]{0:T(1024)S(1)}) fusion(bf16[1024,640]{1,0:T(8,128)(2,1)} %param.6, bf16[1024,640]{1,0:T(8,128)(2,1)} %param.5), kind=kLoop, calls=%fused_computation | loop fusion | flops 2620160 | bytes 2626560 | tf_op jit(solution)/shard_map/reduce_sum | solution.py:56
  10.1 0.2 broadcast_in_dim.8
  10.3 30.8 %all_to_all.39 = f32[64,1,1280]{2,1,0:T(1,128)S(1)} all-to-all(f32[64,1,1280]{2,1,0:T(1,128)S(1)} %broadcast_in_dim.8), channel_id=1, replica_groups=mesh['u'=4,'v'=2,'z'=8,'x'=4,'c'=2] {'u','v','z'}, dimensions={0} | all-to-all | bytes 655360 | tf_op jit(solution)/shard_map/all_to_all | solution.py:18
  41.1 0.2 reduce_sum.101
  41.3 0.1 multiply_reduce_fusion.1
  41.4 0.1 multiply_reduce_fusion
  41.5 0.1 concatenate.35
  41.6 0.7 broadcast_in_dim.9
  42.3 8.0 %all-to-all-start.1 = ((f32[8,1,1440]{2,1,0:T(1,128)}), f32[8,1,1440]{2,1,0:T(1,128)S(1)}, u32[]{:S(2)}, u32[]{:S(2)}) async-start(f32[8,1,1440]{2,1,0:T(1,128)} %broadcast_in_dim.9), calls=%async_computation.1 | async-start | bytes 98304 | tf_op jit(solution)/shard_map/all_to_all | solution.py:18
  50.3 0.7 collective-permute-start
  51.0 4.1 %collective-permute-start.1 = (bf16[80,640]{1,0:T(8,128)(2,1)S(1)}, bf16[80,640]{1,0:T(8,128)(2,1)S(1)}, u32[]{:S(2)}, u32[]{:S(2)}) collective-permute-start(bf16[80,640]{1,0:T(8,128)(2,1)S(1)} %copy-done.2), channel_id=1, source_target_pairs={{0,64},{2,192},{4,320},{6,448},{64,0},{66,128},{68,256},{70,384},{... | collective-permute-start | bytes 307208 | tf_op jit(solution)/shard_map/ppermute | solution.py:29
  55.1 5.0 %collective-permute-done.1 = bf16[80,640]{1,0:T(8,128)(2,1)S(1)} collective-permute-done((bf16[80,640]{1,0:T(8,128)(2,1)S(1)}, bf16[80,640]{1,0:T(8,128)(2,1)S(1)}, u32[]{:S(2)}, u32[]{:S(2)}) %collective-permute-start.1) | collective-permute-done | bytes 102432 | tf_op jit(solution)/shard_map/ppermute | solution.py:29
  60.1 0.7 maximum_select_fusion
  60.9 0.7 broadcast_in_dim.10
  61.6 17.8 %all-to-all-start.2 = ((f32[64,1,160]{2,1,0:T(1,128)}), f32[64,1,160]{2,1,0:T(1,128)S(1)}, u32[]{:S(2)}, u32[]{:S(2)}) async-start(f32[64,1,160]{2,1,0:T(1,128)} %broadcast_in_dim.10), calls=%async_computation.2 | async-start | bytes 131072 | tf_op jit(solution)/shard_map/all_to_all | solution.py:18
  79.4 0.0 all-gather.7.cloned.1.call-start
  79.5 11.1 %all-to-all-done.2 = f32[64,1,160]{2,1,0:T(1,128)S(1)} async-done(((f32[64,1,160]{2,1,0:T(1,128)}), f32[64,1,160]{2,1,0:T(1,128)S(1)}, u32[]{:S(2)}, u32[]{:S(2)}) %all-to-all-start.2) | async-done | bytes 40992 | tf_op jit(solution)/shard_map/all_to_all | solution.py:18
  90.5 0.1 fusion.6
  90.6 0.1 reshape.195
  90.7 0.1 reshape.196
  90.8 0.1 reshape.193
  90.9 0.6 fusion.5
  92.9 0.1 dynamic-slice_multiply_fusion
  92.9 0.1 slice_multiply_fusion.2
  93.0 0.8 convert_bitcast_fusion
  93.8 4.4 %collective-permute-start.2 = (bf16[80,640]{1,0:T(8,128)(2,1)S(1)}, bf16[80,640]{1,0:T(8,128)(2,1)S(1)}, u32[]{:S(2)}, u32[]{:S(2)}) collective-permute-start(bf16[80,640]{1,0:T(8,128)(2,1)S(1)} %get-tuple-element.9), channel_id=1, source_target_pairs={{0,0},{1,64},{64,1},{65,65},{2,2},{3,66},{66,3},{67,67},{4,4},{5,6... | collective-permute-start | bytes 307208 | tf_op jit(solution)/shard_map/ppermute | solution.py:34
  98.2 1.9 collective-permute-start.3
  100.1 0.8 collective-permute-done.2
  100.9 3.1 %collective-permute-done.3 = bf16[80,640]{1,0:T(8,128)(2,1)S(1)} collective-permute-done((bf16[80,640]{1,0:T(8,128)(2,1)S(1)}, bf16[80,640]{1,0:T(8,128)(2,1)S(1)}, u32[]{:S(2)}, u32[]{:S(2)}) %collective-permute-start.3) | collective-permute-done | bytes 102432 | tf_op jit(solution)/shard_map/ppermute | solution.py:34
  104.0 0.7 maximum_select_fusion.1
  104.8 0.1 reshape_reshape.7
  104.9 1.6 broadcast_multiply_fusion
  106.5 1.3 fusion.1
  107.8 0.5 dot_general.8
  108.3 2.2 %fusion.8 = f32[4,80,640]{2,1,0:T(8,128)S(1)} fusion(bf16[4,80,1280]{2,1,0:T(8,128)(2,1)S(1)} %dot_general.8, bf16[1280,640,1]{1,0,2:T(8,128)(2,1)} %bitcast.42), kind=kOutput, calls=%fused_computation.30 | convolution fusion | flops 524288000 | bytes 3276800 | tf_op jit(solution)/shard_map/dot_general | solution.py:91
  110.6 13.2 %all_to_all.40 = f32[4,80,640]{2,1,0:T(8,128)S(1)} all-to-all(f32[4,80,640]{2,1,0:T(8,128)S(1)} %fusion.8), channel_id=1, replica_groups=mesh['u'=4,'v'=2,'z'=8,'x'=4,'c'=2] {'x'}, dimensions={0} | all-to-all | bytes 1638400 | tf_op jit(solution)/shard_map/all_to_all | solution.py:92
  123.8 10.5 %all_gather.20 = bf16[320,640]{1,0:T(8,128)(2,1)S(1)} all-gather(bf16[80,640]{1,0:T(8,128)(2,1)S(1)} %reduce_sum.106), channel_id=1, replica_groups=mesh['u'=4,'v'=2,'z'=8,'x'=4,'c'=2] {'x'}, dimensions={0}, use_global_device_ids=true | all-gather | bytes 512000 | tf_op jit(solution)/shard_map/all_gather | solution.py:94
  134.3 16.1 %all-gather.7.cloned.1.call-done = bf16[8,2,80,640]{3,2,0,1:T(8,128)(2,1)} async-done(((bf16[1,2,80,640]{3,2,0,1:T(8,128)(2,1)}), bf16[8,2,80,640]{3,2,0,1:T(8,128)(2,1)}) %all-gather.7.cloned.1.call-update) | async-done | bytes 1638416 | tf_op jit(solution)/shard_map/all_gather | solution.py:82
  150.4 2.3 %fusion.2 = f32[2,320,640]{2,1,0:T(8,128)S(1)} fusion(bf16[2,640,640]{2,1,0:T(8,128)(2,1)} %bitcast.32, bf16[320,640]{1,0:T(8,128)(2,1)S(1)} %all_gather.20), kind=kOutput, calls=%fused_computation.6 | convolution fusion | flops 524288000 | bytes 3686400 | tf_op jit(solution)/shard_map/crk,ckm->crm/dot_general | solution.py:97
  152.8 9.4 %all_to_all.41 = f32[2,320,640]{2,1,0:T(8,128)S(1)} all-to-all(f32[2,320,640]{2,1,0:T(8,128)S(1)} %fusion.2), channel_id=1, replica_groups=mesh['u'=4,'v'=2,'z'=8,'x'=4,'c'=2] {'c'}, dimensions={0} | all-to-all | bytes 3276800 | tf_op jit(solution)/shard_map/all_to_all | solution.py:103
  162.1 1.1 reduce_sum.108
  163.2 6.4 %all-to-all-start.5 = ((f32[4,80,640]{2,1,0:T(8,128)}), f32[4,80,640]{2,1,0:T(8,128)S(1)}, u32[]{:S(2)}, u32[]{:S(2)}) async-start(f32[4,80,640]{2,1,0:T(8,128)} %bitcast.15), calls=%async_computation.5 | async-start | bytes 1638400 | tf_op jit(solution)/shard_map/all_to_all | solution.py:105
  169.6 0.1 reshape.199
  169.7 0.1 dynamic_slice.16
  169.8 0.8 multiply_subtract_fusion
  170.6 20.3 %all-to-all-done.5 = f32[4,80,640]{2,1,0:T(8,128)S(1)} async-done(((f32[4,80,640]{2,1,0:T(8,128)}), f32[4,80,640]{2,1,0:T(8,128)S(1)}, u32[]{:S(2)}, u32[]{:S(2)}) %all-to-all-start.5) | async-done | bytes 819232 | tf_op jit(solution)/shard_map/all_to_all | solution.py:105
  190.9 0.7 reduce_sum.109
  (23 shorter events, 0.3 us)
Async XLA Ops:
  7.2 97.7 %all-gather.9.cloned.1.call-start = ((), (), s32[]{:S(2)}) async-start(), calls=%async_computation.8 | async-start | bytes 1843200 | tf_op jit(solution)/shard_map/all_gather | solution.py:52
  7.9 33.4 %copy-start = (f32[80,640]{1,0:T(8,128)S(1)}, f32[80,640]{1,0:T(8,128)}, u32[]{:S(2)}) copy-start(f32[80,640]{1,0:T(8,128)} %param.8) | copy-start | bytes 614404
  7.9 33.5 %copy-start.1 = (f32[640,80]{0,1:T(8,128)S(1)}, f32[640,80]{0,1:T(8,128)}, u32[]{:S(2)}) copy-start(f32[640,80]{0,1:T(8,128)} %param.9) | copy-start | bytes 614404
  10.1 40.2 %copy-start.2 = (bf16[80,640]{1,0:T(8,128)(2,1)S(1)}, bf16[80,640]{1,0:T(8,128)(2,1)}, u32[]{:S(2)}) copy-start(bf16[80,640]{1,0:T(8,128)(2,1)} %param.7) | copy-start | bytes 307204
  42.3 12.8 %all-to-all-start.1 = ((f32[8,1,1440]{2,1,0:T(1,128)}), f32[8,1,1440]{2,1,0:T(1,128)S(1)}, u32[]{:S(2)}, u32[]{:S(2)}) async-start(f32[8,1,1440]{2,1,0:T(1,128)} %broadcast_in_dim.9), calls=%async_computation.1 | async-start | bytes 98304 | tf_op jit(solution)/shard_map/all_to_all | solution.py:18
  50.3 58.0 %all-gather.5.cloned.1.call-start = ((), (), s32[]{:S(2)}) async-start(), calls=%async_computation.6 | async-start | bytes 1843200 | tf_op jit(solution)/shard_map/all_gather | solution.py:67
  50.3 4.8 %collective-permute-start = (bf16[80,640]{1,0:T(8,128)(2,1)S(1)}, bf16[80,640]{1,0:T(8,128)(2,1)S(1)}, u32[]{:S(2)}, u32[]{:S(2)}) collective-permute-start(bf16[80,640]{1,0:T(8,128)(2,1)S(1)} %copy-done.2), channel_id=1, source_target_pairs={{0,0},{2,128},{4,256},{6,384},{64,64},{66,192},{68,320},{70,448},{... | collective-permute-start | bytes 307208 | tf_op jit(solution)/shard_map/ppermute | solution.py:29
  51.0 9.2 %collective-permute-start.1 = (bf16[80,640]{1,0:T(8,128)(2,1)S(1)}, bf16[80,640]{1,0:T(8,128)(2,1)S(1)}, u32[]{:S(2)}, u32[]{:S(2)}) collective-permute-start(bf16[80,640]{1,0:T(8,128)(2,1)S(1)} %copy-done.2), channel_id=1, source_target_pairs={{0,64},{2,192},{4,320},{6,448},{64,0},{66,128},{68,256},{70,384},{... | collective-permute-start | bytes 307208 | tf_op jit(solution)/shard_map/ppermute | solution.py:29
  61.6 29.0 %all-to-all-start.2 = ((f32[64,1,160]{2,1,0:T(1,128)}), f32[64,1,160]{2,1,0:T(1,128)S(1)}, u32[]{:S(2)}, u32[]{:S(2)}) async-start(f32[64,1,160]{2,1,0:T(1,128)} %broadcast_in_dim.10), calls=%async_computation.2 | async-start | bytes 131072 | tf_op jit(solution)/shard_map/all_to_all | solution.py:18
  79.4 71.0 %all-gather.7.cloned.1.call-start = ((), (), s32[]{:S(2)}) async-start(), calls=%async_computation.7 | async-start | bytes 1843200 | tf_op jit(solution)/shard_map/all_gather | solution.py:82
  93.8 7.1 %collective-permute-start.2 = (bf16[80,640]{1,0:T(8,128)(2,1)S(1)}, bf16[80,640]{1,0:T(8,128)(2,1)S(1)}, u32[]{:S(2)}, u32[]{:S(2)}) collective-permute-start(bf16[80,640]{1,0:T(8,128)(2,1)S(1)} %get-tuple-element.9), channel_id=1, source_target_pairs={{0,0},{1,64},{64,1},{65,65},{2,2},{3,66},{66,3},{67,67},{4,4},{5,6... | collective-permute-start | bytes 307208 | tf_op jit(solution)/shard_map/ppermute | solution.py:34
  98.2 5.8 %collective-permute-start.3 = (bf16[80,640]{1,0:T(8,128)(2,1)S(1)}, bf16[80,640]{1,0:T(8,128)(2,1)S(1)}, u32[]{:S(2)}, u32[]{:S(2)}) collective-permute-start(bf16[80,640]{1,0:T(8,128)(2,1)S(1)} %get-tuple-element.9), channel_id=1, source_target_pairs={{0,64},{1,0},{64,65},{65,1},{2,66},{3,2},{66,67},{67,3},{4,68},{5,... | collective-permute-start | bytes 307208 | tf_op jit(solution)/shard_map/ppermute | solution.py:34
  163.2 27.7 %all-to-all-start.5 = ((f32[4,80,640]{2,1,0:T(8,128)}), f32[4,80,640]{2,1,0:T(8,128)S(1)}, u32[]{:S(2)}, u32[]{:S(2)}) async-start(f32[4,80,640]{2,1,0:T(8,128)} %bitcast.15), calls=%async_computation.5 | async-start | bytes 1638400 | tf_op jit(solution)/shard_map/all_to_all | solution.py:105
Sparse Core Ops, SparseCore 0:
  10.1 43.4 all-gather.8
  61.0 44.9 all-gather.4
  108.6 41.7 all-gather.6

commit v8 on v4

--- a/solution.py
+++ b/solution.py
@@ -42,7 +42,6 @@
     weight_wide = lax.all_gather(padded, "z", axis=0, tiled=False)
 
     left_piece = swap_u_x(left_inv)
-    left_wide = lax.all_gather(left_piece, F, axis=0, tiled=False)
 
     act_local = jnp.sum(layer_inputs, axis=0, dtype=jnp.float32)
     grad_local = jnp.sum(out_grads, axis=0, dtype=jnp.float32)
@@ -55,6 +54,8 @@
     whole_act = both[:, :cols].reshape(nf * cols)
     whole_grad = both[:, cols : 2 * cols].reshape(nf * cols)
     images = jnp.sum(both[:, 2 * cols :], axis=0)
+    left_piece, _ = lax.optimization_barrier((left_piece, images))
+    left_wide = lax.all_gather(left_piece, F, axis=0, tiled=False)
     weight_wide, images = lax.optimization_barrier((weight_wide, images))
     weight_own = weight_wide[:, :rows, :].reshape(nz * rows, cols)
     weight_other = swap_v(weight_own)
@@ -74,7 +75,7 @@
     right_pair = jnp.where(
         v == 0, jnp.stack([right_own, right_other]), jnp.stack([right_other, right_own])
     )
-    right_wide = lax.all_gather(right_pair, "z", axis=0, tiled=False)
+    right_half = lax.all_gather(right_pair, "z", axis=1, tiled=True)
 
     row_image = lax.dynamic_index_in_dim(
         left_image.reshape(nu, ndp // nu, rows), v * nz + z, 1, keepdims=False
@@ -93,14 +94,15 @@
     hidden_piece = jnp.sum(pieces, axis=0).astype(jnp.bfloat16)
     hidden = lax.all_gather(hidden_piece, "u", axis=0, tiled=True)
 
-    right_half = right_wide.transpose(1, 0, 2, 3).reshape(2, nz * rows, cols)
     partial = jnp.einsum(
         "crk,cmk->crm",
         jnp.broadcast_to(hidden[None], (2,) + hidden.shape),
         right_half,
         preferred_element_type=jnp.float32,
     )
-    pieces = lax.all_to_all(partial.reshape(nf, rows, cols), ("c", "x"), 0, 0, tiled=True)
+    pieces = lax.all_to_all(partial, "c", 0, 0, tiled=True)
+    partial = jnp.sum(pieces, axis=0)
+    pieces = lax.all_to_all(partial.reshape(nu, rows, cols), "x", 0, 0, tiled=True)
     precond = jnp.sum(pieces, axis=0).astype(jnp.bfloat16)
     precond = swap_u_x(precond)
     return (precond, new_left, new_right)

time: 203 us -> 198 us (0.975)
  the two profiles are of different devices: /device:TPU:14 before, /device:TPU:4 now
where the time goes in v8:
time: 198 us; the launch traced here: 197 us
  blocking collectives  71 us (36%)
  waiting for transfers between devices  49.3 us (25%)
  starting transfers between devices  44.6 us (23%)
  between operations  15.4 us (8%)
  other arithmetic  7.69 us (4%)
  local copies, waits for them, and re-layouts  5.73 us (3%)
  matrix products  3.43 us (2%)
    all_to_all x2, starting transfers between devices, share(): lax.all_to_all(jnp.broadcast_to(vec[None], (count,) + vec.shape), axes, 0...  25.9 us
    ppermute x2, waiting for transfers between devices, swap_v(): return lax.ppermute(block, 'v', [(0, 1), (1, 0)])  21.5 us
    all_to_all x2, waiting for transfers between devices, share(): lax.all_to_all(jnp.broadcast_to(vec[None], (count,) + vec.shape), axes, 0...  20.6 us
    all_to_all x1, blocking collectives, per_device(): lax.all_to_all(partial.reshape(nu, rows, cols), 'u', 0, 0, tiled=True)  19.2 us
    all_to_all x1, blocking collectives, share(): lax.all_to_all(jnp.broadcast_to(vec[None], (count,) + vec.shape), axes, 0...  16.9 us
    all_to_all x1, blocking collectives, per_device(): lax.all_to_all(partial.reshape(nu, rows, cols), 'x', 0, 0, tiled=True)  15.1 us
    all_gather x1, blocking collectives, per_device(): hidden = lax.all_gather(hidden_piece, 'u', axis=0, tiled=True)  14.8 us
    ppermute x2, starting transfers between devices, swap_u_x(): lax.ppermute(block, ('u', 'x'), [(a * n + b, b * n + a) for a in range(n)...  13.4 us
  transfers between devices with their start and end apart: 9, of which 5 were waited for; matrix products, arithmetic and copies ran while one was open for 6% of the time, Pallas kernels for 0%

profile of v8, /device:TPU:4, one launch (start us, length us, event | category | flops | bytes accessed | tf_op | source)
XLA Modules:
  0.0 197.2 jit_solution(14894579586042761062)
XLA Ops:
  7.2 1.6 pad.4
  8.8 2.2 %convert_reduce_fusion = (f32[640]{0:T(1024)S(1)}, f32[640]{0:T(1024)S(1)}) fusion(bf16[1024,640]{1,0:T(8,128)(2,1)} %param.6, bf16[1024,640]{1,0:T(8,128)(2,1)} %param.5), kind=kLoop, calls=%fused_computation | loop fusion | flops 2620160 | bytes 2626560 | tf_op jit(solution)/shard_map/reduce_sum | solution.py:47
  11.0 0.9 broadcast_in_dim.8
  11.9 16.6 %all-to-all-start = ((f32[64,1,1280]{2,1,0:T(1,128)}), f32[64,1,1280]{2,1,0:T(1,128)S(1)}, u32[]{:S(2)}, u32[]{:S(2)}) async-start(f32[64,1,1280]{2,1,0:T(1,128)} %broadcast_in_dim.8), calls=%async_computation | async-start | bytes 655360 | tf_op jit(solution)/shard_map/all_to_all | solution.py:19
  28.5 7.4 %collective-permute-start = (f32[80,640]{1,0:T(8,128)S(1)}, f32[80,640]{1,0:T(8,128)S(1)}, u32[]{:S(2)}, u32[]{:S(2)}) collective-permute-start(f32[80,640]{1,0:T(8,128)S(1)} %copy-done.1), channel_id=1, source_target_pairs={{0,0},{2,128},{4,256},{6,384},{128,2},{130,130},{132,258},{134,386... | collective-permute-start | bytes 614408 | tf_op jit(solution)/shard_map/ppermute | solution.py:24
  36.0 8.4 %all-to-all-done = f32[64,1,1280]{2,1,0:T(1,128)S(1)} async-done(((f32[64,1,1280]{2,1,0:T(1,128)}), f32[64,1,1280]{2,1,0:T(1,128)S(1)}, u32[]{:S(2)}, u32[]{:S(2)}) %all-to-all-start) | async-done | bytes 327712 | tf_op jit(solution)/shard_map/all_to_all | solution.py:19
  44.4 0.2 reduce_sum.101
  44.6 0.1 multiply_reduce_fusion.1
  44.8 0.1 multiply_reduce_fusion
  44.9 0.1 concatenate.7
  45.0 16.9 %all_to_all.39 = f32[8,1,1440]{2,1,0:T(1,128)S(1)} all-to-all(f32[8,1,1440]{2,1,0:T(1,128)S(1)} %broadcast_in_dim.9), channel_id=1, replica_groups=mesh['u'=4,'v'=2,'z'=8,'x'=4,'c'=2] {'x','c'}, dimensions={0} | all-to-all | bytes 92160 | tf_op jit(solution)/shard_map/all_to_all | solution.py:19
  62.0 0.7 copy-done.4
  62.7 0.7 broadcast_in_dim.10
  63.4 9.4 %all-to-all-start.2 = ((f32[64,1,160]{2,1,0:T(1,128)}), f32[64,1,160]{2,1,0:T(1,128)S(1)}, u32[]{:S(2)}, u32[]{:S(2)}) async-start(f32[64,1,160]{2,1,0:T(1,128)} %broadcast_in_dim.10), calls=%async_computation.2 | async-start | bytes 131072 | tf_op jit(solution)/shard_map/all_to_all | solution.py:19
  72.8 12.2 %all-to-all-done.2 = f32[64,1,160]{2,1,0:T(1,128)S(1)} async-done(((f32[64,1,160]{2,1,0:T(1,128)}), f32[64,1,160]{2,1,0:T(1,128)S(1)}, u32[]{:S(2)}, u32[]{:S(2)}) %all-to-all-start.2) | async-done | bytes 40992 | tf_op jit(solution)/shard_map/all_to_all | solution.py:19
  85.0 0.1 fusion.6
  85.1 0.1 reshape.105
  85.2 0.1 reshape.106
  85.2 0.1 reshape.101
  85.3 0.6 fusion.4
  87.3 0.1 dynamic-slice_multiply_fusion.1
  87.4 0.1 slice_multiply_fusion.2
  87.5 0.1 convert_bitcast_fusion
  87.6 2.6 %collective-permute-start.2 = (bf16[80,640]{1,0:T(8,128)(2,1)S(1)}, bf16[80,640]{1,0:T(8,128)(2,1)S(1)}, u32[]{:S(2)}, u32[]{:S(2)}) collective-permute-start(bf16[80,640]{1,0:T(8,128)(2,1)S(1)} %convert_bitcast_fusion.1), channel_id=1, source_target_pairs={{0,64},{64,0},{1,65},{65,1},{2,66},{66,2},{3,67},{67,3},{4,68},{68... | collective-permute-start | bytes 307208 | tf_op jit(solution)/shard_map/ppermute | solution.py:28
  90.2 5.1 %collective-permute-done.2 = bf16[80,640]{1,0:T(8,128)(2,1)S(1)} collective-permute-done((bf16[80,640]{1,0:T(8,128)(2,1)S(1)}, bf16[80,640]{1,0:T(8,128)(2,1)S(1)}, u32[]{:S(2)}, u32[]{:S(2)}) %collective-permute-start.2) | collective-permute-done | bytes 102432 | tf_op jit(solution)/shard_map/ppermute | solution.py:28
  95.2 0.7 maximum_select_fusion
  96.0 0.1 slice.35
  96.1 2.6 %collective-permute-start.1 = (bf16[640,640]{1,0:T(8,128)(2,1)S(1)}, bf16[640,640]{1,0:T(8,128)(2,1)S(1)}, u32[]{:S(2)}, u32[]{:S(2)}) collective-permute-start(bf16[640,640]{1,0:T(8,128)(2,1)S(1)} %bitcast.30), channel_id=1, source_target_pairs={{0,64},{64,0},{1,65},{65,1},{2,66},{66,2},{3,67},{67,3},{4,68},{68... | collective-permute-start | bytes 2457608 | tf_op jit(solution)/shard_map/ppermute | solution.py:28
  98.7 0.1 reshape.102
  98.8 0.1 fusion.7
  98.9 0.5 broadcast.74
  99.4 0.7 fusion.5
  100.0 0.1 mul.167
  100.1 1.6 dynamic-slice_multiply_fusion
  101.8 0.1 fusion
  101.9 0.5 fusion.9
  102.4 16.4 %collective-permute-done.1 = bf16[640,640]{1,0:T(8,128)(2,1)S(1)} collective-permute-done((bf16[640,640]{1,0:T(8,128)(2,1)S(1)}, bf16[640,640]{1,0:T(8,128)(2,1)S(1)}, u32[]{:S(2)}, u32[]{:S(2)}) %collective-permute-start.1) | collective-permute-done | bytes 819232 | tf_op jit(solution)/shard_map/ppermute | solution.py:28
  118.9 0.5 convolution_add_fusion
  119.4 19.2 %all_to_all.40 = f32[4,80,640]{2,1,0:T(8,128)S(1)} all-to-all(f32[4,80,640]{2,1,0:T(8,128)S(1)} %bitcast.29), channel_id=1, replica_groups=mesh['u'=4,'v'=2,'z'=8,'x'=4,'c'=2] {'u'}, dimensions={0} | all-to-all | bytes 1638400 | tf_op jit(solution)/shard_map/all_to_all | solution.py:93
  138.6 14.8 %all_gather.22 = bf16[320,640]{1,0:T(8,128)(2,1)S(1)} all-gather(bf16[80,640]{1,0:T(8,128)(2,1)S(1)} %reduce_sum.106), channel_id=1, replica_groups=mesh['u'=4,'v'=2,'z'=8,'x'=4,'c'=2] {'u'}, dimensions={0}, use_global_device_ids=true | all-gather | bytes 512000 | tf_op jit(solution)/shard_map/all_gather | solution.py:95
  153.4 2.4 %fusion.1 = f32[2,320,640]{2,1,0:T(8,128)S(1)} fusion(bf16[2,640,640]{2,1,0:T(8,128)(2,1)} %all-gather.6.cloned.1.call-done, bf16[320,640]{1,0:T(8,128)(2,1)S(1)} %all_gather.22), kind=kOutput, calls=%fused_computation.7 | convolution fusion | flops 524288000 | bytes 3686400 | tf_op jit(solution)/shard_map/crk,cmk->crm/dot_general | solution.py:97
  155.8 5.0 %all_to_all.41 = f32[2,320,640]{2,1,0:T(8,128)S(1)} all-to-all(f32[2,320,640]{2,1,0:T(8,128)S(1)} %fusion.1), channel_id=1, replica_groups=mesh['u'=4,'v'=2,'z'=8,'x'=4,'c'=2] {'c'}, dimensions={0} | all-to-all | bytes 3276800 | tf_op jit(solution)/shard_map/all_to_all | solution.py:103
  160.9 0.2 reduce_sum.108
  161.0 15.1 %all_to_all.42 = f32[4,80,640]{2,1,0:T(8,128)S(1)} all-to-all(f32[4,80,640]{2,1,0:T(8,128)S(1)} %bitcast.32), channel_id=1, replica_groups=mesh['u'=4,'v'=2,'z'=8,'x'=4,'c'=2] {'x'}, dimensions={0} | all-to-all | bytes 1638400 | tf_op jit(solution)/shard_map/all_to_all | solution.py:105
  176.2 5.9 %collective-permute-start.3 = (bf16[80,640]{1,0:T(8,128)(2,1)S(1)}, bf16[80,640]{1,0:T(8,128)(2,1)S(1)}, u32[]{:S(2)}, u32[]{:S(2)}) collective-permute-start(bf16[80,640]{1,0:T(8,128)(2,1)S(1)} %reduce_sum.109), channel_id=1, source_target_pairs={{0,0},{2,128},{4,256},{6,384},{128,2},{130,130},{132,258},{134,386... | collective-permute-start | bytes 307208 | tf_op jit(solution)/shard_map/ppermute | solution.py:24
  182.1 0.8 multiply_subtract_fusion
  182.9 7.1 %collective-permute-done.3 = bf16[80,640]{1,0:T(8,128)(2,1)S(1)} collective-permute-done((bf16[80,640]{1,0:T(8,128)(2,1)S(1)}, bf16[80,640]{1,0:T(8,128)(2,1)S(1)}, u32[]{:S(2)}, u32[]{:S(2)}) %collective-permute-start.3) | collective-permute-done | bytes 102432 | tf_op jit(solution)/shard_map/ppermute | solution.py:24
  190.0 0.6 copy.17
  (29 shorter events, 0.4 us)
Async XLA Ops:
  7.2 55.5 %all-gather.10.cloned.1.call-start = ((), (), s32[]{:S(2)}) async-start(), calls=%async_computation.8 | async-start | bytes 1198080 | tf_op jit(solution)/shard_map/all_gather | solution.py:42
  8.8 19.7 %copy-start.1 = (f32[80,640]{1,0:T(8,128)S(1)}, f32[80,640]{1,0:T(8,128)}, u32[]{:S(2)}) copy-start(f32[80,640]{1,0:T(8,128)} %param.8) | copy-start | bytes 614404
  8.8 35.9 %copy-start = (f32[640,80]{0,1:T(8,128)S(1)}, f32[640,80]{0,1:T(8,128)}, u32[]{:S(2)}) copy-start(f32[640,80]{0,1:T(8,128)} %param.9) | copy-start | bytes 614404
  11.9 32.5 %all-to-all-start = ((f32[64,1,1280]{2,1,0:T(1,128)}), f32[64,1,1280]{2,1,0:T(1,128)S(1)}, u32[]{:S(2)}, u32[]{:S(2)}) async-start(f32[64,1,1280]{2,1,0:T(1,128)} %broadcast_in_dim.8), calls=%async_computation | async-start | bytes 655360 | tf_op jit(solution)/shard_map/all_to_all | solution.py:19
  28.5 71.6 %all-gather.8.cloned.1.call-start = ((), (), s32[]{:S(2)}) async-start(), calls=%async_computation.7 | async-start | bytes 1843200 | tf_op jit(solution)/shard_map/all_gather | solution.py:58
  28.5 33.4 %collective-permute-start = (f32[80,640]{1,0:T(8,128)S(1)}, f32[80,640]{1,0:T(8,128)S(1)}, u32[]{:S(2)}, u32[]{:S(2)}) collective-permute-start(f32[80,640]{1,0:T(8,128)S(1)} %copy-done.1), channel_id=1, source_target_pairs={{0,0},{2,128},{4,256},{6,384},{128,2},{130,130},{132,258},{134,386... | collective-permute-start | bytes 614408 | tf_op jit(solution)/shard_map/ppermute | solution.py:24
  61.9 0.7 copy-start.4
  62.7 33.3 %copy-start.3 = (bf16[832,640]{1,0:T(8,128)(2,1)S(1)}, bf16[832,640]{1,0:T(8,128)(2,1)}, u32[]{:S(2)}) copy-start(bf16[832,640]{1,0:T(8,128)(2,1)} %all-gather.10.cloned.1.call-done) | copy-start | bytes 3194884
  63.4 21.6 %all-to-all-start.2 = ((f32[64,1,160]{2,1,0:T(1,128)}), f32[64,1,160]{2,1,0:T(1,128)S(1)}, u32[]{:S(2)}, u32[]{:S(2)}) async-start(f32[64,1,160]{2,1,0:T(1,128)} %broadcast_in_dim.10), calls=%async_computation.2 | async-start | bytes 131072 | tf_op jit(solution)/shard_map/all_to_all | solution.py:19
  72.7 80.7 %all-gather.6.cloned.1.call-start = ((), (), s32[]{:S(2)}) async-start(), calls=%async_computation.6 | async-start | bytes 1843200 | tf_op jit(solution)/shard_map/all_gather | solution.py:78
  87.6 14.2 %copy-start.2 = (f32[640,80]{0,1:T(8,128)}, f32[640,80]{0,1:T(8,128)S(1)}, u32[]{:S(2)}) copy-start(f32[640,80]{0,1:T(8,128)S(1)} %get-tuple-element.33) | copy-start | bytes 614404
  87.6 7.6 %collective-permute-start.2 = (bf16[80,640]{1,0:T(8,128)(2,1)S(1)}, bf16[80,640]{1,0:T(8,128)(2,1)S(1)}, u32[]{:S(2)}, u32[]{:S(2)}) collective-permute-start(bf16[80,640]{1,0:T(8,128)(2,1)S(1)} %convert_bitcast_fusion.1), channel_id=1, source_target_pairs={{0,64},{64,0},{1,65},{65,1},{2,66},{66,2},{3,67},{67,3},{4,68},{68... | collective-permute-start | bytes 307208 | tf_op jit(solution)/shard_map/ppermute | solution.py:28
  96.1 22.8 %collective-permute-start.1 = (bf16[640,640]{1,0:T(8,128)(2,1)S(1)}, bf16[640,640]{1,0:T(8,128)(2,1)S(1)}, u32[]{:S(2)}, u32[]{:S(2)}) collective-permute-start(bf16[640,640]{1,0:T(8,128)(2,1)S(1)} %bitcast.30), channel_id=1, source_target_pairs={{0,64},{64,0},{1,65},{65,1},{2,66},{66,2},{3,67},{67,3},{4,68},{68... | collective-permute-start | bytes 2457608 | tf_op jit(solution)/shard_map/ppermute | solution.py:28
  176.2 13.8 %collective-permute-start.3 = (bf16[80,640]{1,0:T(8,128)(2,1)S(1)}, bf16[80,640]{1,0:T(8,128)(2,1)S(1)}, u32[]{:S(2)}, u32[]{:S(2)}) collective-permute-start(bf16[80,640]{1,0:T(8,128)(2,1)S(1)} %reduce_sum.109), channel_id=1, source_target_pairs={{0,0},{2,128},{4,256},{6,384},{128,2},{130,130},{132,258},{134,386... | collective-permute-start | bytes 307208 | tf_op jit(solution)/shard_map/ppermute | solution.py:24
Sparse Core Ops, SparseCore 0:
  10.6 49.7 all-gather.9
  62.8 28.1 all-gather.7
  96.1 42.0 all-gather.5

commit v9 on v8

--- a/solution.py
+++ b/solution.py
@@ -43,6 +43,12 @@
 
     left_piece = swap_u_x(left_inv)
 
+    right_own = right_inv.T
+    right_other = swap_v(right_own)
+    right_pair = jnp.where(
+        v == 0, jnp.stack([right_own, right_other]), jnp.stack([right_other, right_own])
+    )
+
     act_local = jnp.sum(layer_inputs, axis=0, dtype=jnp.float32)
     grad_local = jnp.sum(out_grads, axis=0, dtype=jnp.float32)
     sums = share(jnp.concatenate([act_local, grad_local]), DP)
@@ -70,11 +76,12 @@
     new_left = left_inv / decay - left_coef * images[:rows, None] * left_cols[None, :]
     new_right = right_inv / decay - right_coef * right_cols[:, None] * images[None, rows:]
 
-    right_own = new_right.astype(jnp.bfloat16).T
-    right_other = swap_v(right_own)
-    right_pair = jnp.where(
-        v == 0, jnp.stack([right_own, right_other]), jnp.stack([right_other, right_own])
-    )
+    pair_image = lax.dynamic_slice_in_dim(
+        right_image.reshape(nu, 2, nz, rows), u, 1, 0
+    )[0]
+    pair_image = lax.dynamic_index_in_dim(pair_image, z, 1, keepdims=False)
+    right_pair = right_pair / decay - (right_coef * right_cols) * pair_image[:, :, None]
+    right_pair = right_pair.astype(jnp.bfloat16)
     right_half = lax.all_gather(right_pair, "z", axis=1, tiled=True)
 
     row_image = lax.dynamic_index_in_dim(

time: 198 us -> 188 us (0.949)
  the two profiles are of different devices: /device:TPU:4 before, /device:TPU:15 now
where the time goes in v9:
time: 188 us; the launch traced here: 187 us
  blocking collectives  56.8 us (30%)
  waiting for transfers between devices  49.2 us (26%)
  starting transfers between devices  47.4 us (25%)
  between operations  15.4 us (8%)
  other arithmetic  9.35 us (5%)
  local copies, waits for them, and re-layouts  5.73 us (3%)
  matrix products  3.43 us (2%)
    all_to_all x2, starting transfers between devices, share(): lax.all_to_all(jnp.broadcast_to(vec[None], (count,) + vec.shape), axes, 0...  25.9 us
    all_to_all x1, blocking collectives, per_device(): lax.all_to_all(partial.reshape(nu, rows, cols), 'u', 0, 0, tiled=True)  17.7 us
    all_gather x1, blocking collectives, per_device(): hidden = lax.all_gather(hidden_piece, 'u', axis=0, tiled=True)  17.4 us
    all_to_all x2, waiting for transfers between devices, share(): lax.all_to_all(jnp.broadcast_to(vec[None], (count,) + vec.shape), axes, 0...  16.2 us
    all_to_all x1, blocking collectives, share(): lax.all_to_all(jnp.broadcast_to(vec[None], (count,) + vec.shape), axes, 0...  12.4 us
    all_to_all x1, waiting for transfers between devices, per_device(): lax.all_to_all(partial.reshape(nu, rows, cols), 'x', 0, 0, tiled=True)  9.73 us
    ppermute x2, waiting for transfers between devices, swap_u_x(): lax.ppermute(block, ('u', 'x'), [(a * n + b, b * n + a) for a in range(n)...  9.62 us
    all_to_all x1, blocking collectives, per_device(): pieces = lax.all_to_all(partial, 'c', 0, 0, tiled=True)  9.31 us
  transfers between devices with their start and end apart: 10, of which 8 were waited for; matrix products, arithmetic and copies ran while one was open for 6% of the time, Pallas kernels for 0%

profile of v9, /device:TPU:15, one launch (start us, length us, event | category | flops | bytes accessed | tf_op | source)
XLA Modules:
  0.0 187.2 jit_solution(14905491327349828327)
XLA Ops:
  7.2 1.6 pad.4
  8.8 2.2 %convert_reduce_fusion = (f32[640]{0:T(1024)S(1)}, f32[640]{0:T(1024)S(1)}) fusion(bf16[1024,640]{1,0:T(8,128)(2,1)} %param.6, bf16[1024,640]{1,0:T(8,128)(2,1)} %param.5), kind=kLoop, calls=%fused_computation | loop fusion | flops 2620160 | bytes 2626560 | tf_op jit(solution)/shard_map/reduce_sum | solution.py:53
  11.0 0.9 broadcast_in_dim.8
  11.9 16.0 %all-to-all-start = ((f32[64,1,1280]{2,1,0:T(1,128)}), f32[64,1,1280]{2,1,0:T(1,128)S(1)}, u32[]{:S(2)}, u32[]{:S(2)}) async-start(f32[64,1,1280]{2,1,0:T(1,128)} %broadcast_in_dim.8), calls=%async_computation | async-start | bytes 655360 | tf_op jit(solution)/shard_map/all_to_all | solution.py:19
  28.0 4.5 %collective-permute-start = (f32[80,640]{1,0:T(8,128)S(1)}, f32[80,640]{1,0:T(8,128)S(1)}, u32[]{:S(2)}, u32[]{:S(2)}) collective-permute-start(f32[80,640]{1,0:T(8,128)S(1)} %copy-done.1), channel_id=1, source_target_pairs={{0,0},{2,128},{4,256},{6,384},{128,2},{130,130},{132,258},{134,386... | collective-permute-start | bytes 614408 | tf_op jit(solution)/shard_map/ppermute | solution.py:24
  32.5 8.1 %all-to-all-done = f32[64,1,1280]{2,1,0:T(1,128)S(1)} async-done(((f32[64,1,1280]{2,1,0:T(1,128)}), f32[64,1,1280]{2,1,0:T(1,128)S(1)}, u32[]{:S(2)}, u32[]{:S(2)}) %all-to-all-start) | async-done | bytes 327712 | tf_op jit(solution)/shard_map/all_to_all | solution.py:19
  40.5 0.2 reduce_sum.101
  40.8 0.1 multiply_reduce_fusion.1
  40.9 0.1 multiply_reduce_fusion
  41.0 0.1 concatenate.7
  41.1 12.4 %all_to_all.39 = f32[8,1,1440]{2,1,0:T(1,128)S(1)} all-to-all(f32[8,1,1440]{2,1,0:T(1,128)S(1)} %broadcast_in_dim.9), channel_id=1, replica_groups=mesh['u'=4,'v'=2,'z'=8,'x'=4,'c'=2] {'x','c'}, dimensions={0} | all-to-all | bytes 92160 | tf_op jit(solution)/shard_map/all_to_all | solution.py:19
  53.6 0.7 copy-done.3
  54.3 3.1 %all-gather.10.cloned.1.call-done = bf16[832,640]{1,0:T(8,128)(2,1)} async-done(((bf16[104,640]{1,0:T(8,128)(2,1)}), bf16[832,640]{1,0:T(8,128)(2,1)}) %all-gather.10.cloned.1.call-update) | async-done | bytes 1064976 | tf_op jit(solution)/shard_map/all_gather | solution.py:42
  57.4 0.7 broadcast_in_dim.10
  58.1 9.9 %all-to-all-start.2 = ((f32[64,1,160]{2,1,0:T(1,128)}), f32[64,1,160]{2,1,0:T(1,128)S(1)}, u32[]{:S(2)}, u32[]{:S(2)}) async-start(f32[64,1,160]{2,1,0:T(1,128)} %broadcast_in_dim.10), calls=%async_computation.2 | async-start | bytes 131072 | tf_op jit(solution)/shard_map/all_to_all | solution.py:19
  68.0 2.4 %collective-permute-start.2 = (f32[80,640]{1,0:T(8,128)S(1)}, f32[80,640]{1,0:T(8,128)S(1)}, u32[]{:S(2)}, u32[]{:S(2)}) collective-permute-start(f32[80,640]{1,0:T(8,128)S(1)} %bitcast.32), channel_id=1, source_target_pairs={{0,64},{64,0},{1,65},{65,1},{2,66},{66,2},{3,67},{67,3},{4,68},{68... | collective-permute-start | bytes 614408 | tf_op jit(solution)/shard_map/ppermute | solution.py:28
  70.4 8.1 %all-to-all-done.2 = f32[64,1,160]{2,1,0:T(1,128)S(1)} async-done(((f32[64,1,160]{2,1,0:T(1,128)}), f32[64,1,160]{2,1,0:T(1,128)S(1)}, u32[]{:S(2)}, u32[]{:S(2)}) %all-to-all-start.2) | async-done | bytes 40992 | tf_op jit(solution)/shard_map/all_to_all | solution.py:19
  78.5 0.1 fusion.9
  78.6 0.1 reshape.110
  78.7 0.1 reshape.111
  78.9 0.6 fusion.7
  80.2 0.1 dynamic-slice_multiply_fusion.1
  80.3 0.8 fusion.3
  81.2 2.9 %collective-permute-start.1 = (bf16[640,640]{1,0:T(8,128)(2,1)S(1)}, bf16[640,640]{1,0:T(8,128)(2,1)S(1)}, u32[]{:S(2)}, u32[]{:S(2)}) collective-permute-start(bf16[640,640]{1,0:T(8,128)(2,1)S(1)} %bitcast.30), channel_id=1, source_target_pairs={{0,64},{64,0},{1,65},{65,1},{2,66},{66,2},{3,67},{67,3},{4,68},{68... | collective-permute-start | bytes 2457608 | tf_op jit(solution)/shard_map/ppermute | solution.py:28
  84.1 0.1 reshape.107
  84.9 0.1 fusion.10
  85.0 0.5 broadcast.76
  85.5 0.7 fusion.8
  86.2 0.1 mul.184
  86.3 4.9 %all-gather.8.cloned.1.call-done = f32[640,640]{1,0:T(8,128)} async-done(((f32[80,640]{1,0:T(8,128)}), f32[640,640]{1,0:T(8,128)}) %all-gather.8.cloned.1.call-update) | async-done | bytes 1638416 | tf_op jit(solution)/shard_map/all_gather | solution.py:64
  91.2 1.6 dynamic-slice_multiply_fusion
  92.9 0.1 fusion
  93.0 0.5 fusion.13
  93.5 3.0 %collective-permute-done.1 = bf16[640,640]{1,0:T(8,128)(2,1)S(1)} collective-permute-done((bf16[640,640]{1,0:T(8,128)(2,1)S(1)}, bf16[640,640]{1,0:T(8,128)(2,1)S(1)}, u32[]{:S(2)}, u32[]{:S(2)}) %collective-permute-start.1) | collective-permute-done | bytes 819232 | tf_op jit(solution)/shard_map/ppermute | solution.py:28
  96.5 0.5 convolution_add_fusion
  97.0 17.7 %all_to_all.40 = f32[4,80,640]{2,1,0:T(8,128)S(1)} all-to-all(f32[4,80,640]{2,1,0:T(8,128)S(1)} %bitcast.29), channel_id=1, replica_groups=mesh['u'=4,'v'=2,'z'=8,'x'=4,'c'=2] {'u'}, dimensions={0} | all-to-all | bytes 1638400 | tf_op jit(solution)/shard_map/all_to_all | solution.py:100
  114.8 17.4 %all_gather.22 = bf16[320,640]{1,0:T(8,128)(2,1)S(1)} all-gather(bf16[80,640]{1,0:T(8,128)(2,1)S(1)} %reduce_sum.106), channel_id=1, replica_groups=mesh['u'=4,'v'=2,'z'=8,'x'=4,'c'=2] {'u'}, dimensions={0}, use_global_device_ids=true | all-gather | bytes 512000 | tf_op jit(solution)/shard_map/all_gather | solution.py:102
  132.1 2.6 %all-gather.6.cloned.1.call-done = bf16[2,640,640]{2,1,0:T(8,128)(2,1)} async-done(((bf16[2,80,640]{2,1,0:T(8,128)(2,1)}), bf16[2,640,640]{2,1,0:T(8,128)(2,1)}) %all-gather.6.cloned.1.call-update) | async-done | bytes 1638416 | tf_op jit(solution)/shard_map/all_gather | solution.py:85
  134.7 2.4 %fusion.4 = f32[2,320,640]{2,1,0:T(8,128)S(1)} fusion(bf16[2,640,640]{2,1,0:T(8,128)(2,1)} %all-gather.6.cloned.1.call-done, bf16[320,640]{1,0:T(8,128)(2,1)S(1)} %all_gather.22), kind=kOutput, calls=%fused_computation.11 | convolution fusion | flops 524288000 | bytes 3686400 | tf_op jit(solution)/shard_map/crk,cmk->crm/dot_general | solution.py:104
  137.1 9.3 %all_to_all.41 = f32[2,320,640]{2,1,0:T(8,128)S(1)} all-to-all(f32[2,320,640]{2,1,0:T(8,128)S(1)} %fusion.4), channel_id=1, replica_groups=mesh['u'=4,'v'=2,'z'=8,'x'=4,'c'=2] {'c'}, dimensions={0} | all-to-all | bytes 3276800 | tf_op jit(solution)/shard_map/all_to_all | solution.py:110
  146.4 1.1 reduce_sum.108
  147.5 7.2 %all-to-all-start.5 = ((f32[4,80,640]{2,1,0:T(8,128)}), f32[4,80,640]{2,1,0:T(8,128)S(1)}, u32[]{:S(2)}, u32[]{:S(2)}) async-start(f32[4,80,640]{2,1,0:T(8,128)} %bitcast.14), calls=%async_computation.5 | async-start | bytes 1638400 | tf_op jit(solution)/shard_map/all_to_all | solution.py:112
  154.8 0.8 multiply_subtract_fusion
  155.5 9.7 %all-to-all-done.5 = f32[4,80,640]{2,1,0:T(8,128)S(1)} async-done(((f32[4,80,640]{2,1,0:T(8,128)}), f32[4,80,640]{2,1,0:T(8,128)S(1)}, u32[]{:S(2)}, u32[]{:S(2)}) %all-to-all-start.5) | async-done | bytes 819232 | tf_op jit(solution)/shard_map/all_to_all | solution.py:112
  165.3 4.3 %collective-permute-start.3 = (bf16[80,640]{1,0:T(8,128)(2,1)S(1)}, bf16[80,640]{1,0:T(8,128)(2,1)S(1)}, u32[]{:S(2)}, u32[]{:S(2)}) collective-permute-start(bf16[80,640]{1,0:T(8,128)(2,1)S(1)} %reduce_sum.109), channel_id=1, source_target_pairs={{0,0},{2,128},{4,256},{6,384},{128,2},{130,130},{132,258},{134,386... | collective-permute-start | bytes 307208 | tf_op jit(solution)/shard_map/ppermute | solution.py:24
  169.6 0.8 multiply_subtract_fusion.1
  170.4 9.6 %collective-permute-done.3 = bf16[80,640]{1,0:T(8,128)(2,1)S(1)} collective-permute-done((bf16[80,640]{1,0:T(8,128)(2,1)S(1)}, bf16[80,640]{1,0:T(8,128)(2,1)S(1)}, u32[]{:S(2)}, u32[]{:S(2)}) %collective-permute-start.3) | collective-permute-done | bytes 102432 | tf_op jit(solution)/shard_map/ppermute | solution.py:24
  180.0 0.6 copy.17
  (28 shorter events, 0.6 us)
Async XLA Ops:
  7.2 50.2 %all-gather.10.cloned.1.call-start = ((), (), s32[]{:S(2)}) async-start(), calls=%async_computation.8 | async-start | bytes 1198080 | tf_op jit(solution)/shard_map/all_gather | solution.py:42
  8.8 19.2 %copy-start.1 = (f32[80,640]{1,0:T(8,128)S(1)}, f32[80,640]{1,0:T(8,128)}, u32[]{:S(2)}) copy-start(f32[80,640]{1,0:T(8,128)} %param.8) | copy-start | bytes 614404
  8.8 32.1 %copy-start = (f32[640,80]{0,1:T(8,128)S(1)}, f32[640,80]{0,1:T(8,128)}, u32[]{:S(2)}) copy-start(f32[640,80]{0,1:T(8,128)} %param.9) | copy-start | bytes 614404
  11.9 28.6 %all-to-all-start = ((f32[64,1,1280]{2,1,0:T(1,128)}), f32[64,1,1280]{2,1,0:T(1,128)S(1)}, u32[]{:S(2)}, u32[]{:S(2)}) async-start(f32[64,1,1280]{2,1,0:T(1,128)} %broadcast_in_dim.8), calls=%async_computation | async-start | bytes 655360 | tf_op jit(solution)/shard_map/all_to_all | solution.py:19
  27.9 63.3 %all-gather.8.cloned.1.call-start = ((), (), s32[]{:S(2)}) async-start(), calls=%async_computation.7 | async-start | bytes 1843200 | tf_op jit(solution)/shard_map/all_gather | solution.py:64
  28.0 25.6 %collective-permute-start = (f32[80,640]{1,0:T(8,128)S(1)}, f32[80,640]{1,0:T(8,128)S(1)}, u32[]{:S(2)}, u32[]{:S(2)}) collective-permute-start(f32[80,640]{1,0:T(8,128)S(1)} %copy-done.1), channel_id=1, source_target_pairs={{0,0},{2,128},{4,256},{6,384},{128,2},{130,130},{132,258},{134,386... | collective-permute-start | bytes 614408 | tf_op jit(solution)/shard_map/ppermute | solution.py:24
  53.6 0.7 copy-start.3
  57.4 23.7 %copy-start.2 = (bf16[832,640]{1,0:T(8,128)(2,1)S(1)}, bf16[832,640]{1,0:T(8,128)(2,1)}, u32[]{:S(2)}) copy-start(bf16[832,640]{1,0:T(8,128)(2,1)} %all-gather.10.cloned.1.call-done) | copy-start | bytes 3194884
  58.1 20.5 %all-to-all-start.2 = ((f32[64,1,160]{2,1,0:T(1,128)}), f32[64,1,160]{2,1,0:T(1,128)S(1)}, u32[]{:S(2)}, u32[]{:S(2)}) async-start(f32[64,1,160]{2,1,0:T(1,128)} %broadcast_in_dim.10), calls=%async_computation.2 | async-start | bytes 131072 | tf_op jit(solution)/shard_map/all_to_all | solution.py:19
  67.9 66.7 %all-gather.6.cloned.1.call-start = ((), (), s32[]{:S(2)}) async-start(), calls=%async_computation.6 | async-start | bytes 1843200 | tf_op jit(solution)/shard_map/all_gather | solution.py:85
  68.0 12.3 %collective-permute-start.2 = (f32[80,640]{1,0:T(8,128)S(1)}, f32[80,640]{1,0:T(8,128)S(1)}, u32[]{:S(2)}, u32[]{:S(2)}) collective-permute-start(f32[80,640]{1,0:T(8,128)S(1)} %bitcast.32), channel_id=1, source_target_pairs={{0,64},{64,0},{1,65},{65,1},{2,66},{66,2},{3,67},{67,3},{4,68},{68... | collective-permute-start | bytes 614408 | tf_op jit(solution)/shard_map/ppermute | solution.py:28
  81.2 15.3 %collective-permute-start.1 = (bf16[640,640]{1,0:T(8,128)(2,1)S(1)}, bf16[640,640]{1,0:T(8,128)(2,1)S(1)}, u32[]{:S(2)}, u32[]{:S(2)}) collective-permute-start(bf16[640,640]{1,0:T(8,128)(2,1)S(1)} %bitcast.30), channel_id=1, source_target_pairs={{0,64},{64,0},{1,65},{65,1},{2,66},{66,2},{3,67},{67,3},{4,68},{68... | collective-permute-start | bytes 2457608 | tf_op jit(solution)/shard_map/ppermute | solution.py:28
  147.5 17.8 %all-to-all-start.5 = ((f32[4,80,640]{2,1,0:T(8,128)}), f32[4,80,640]{2,1,0:T(8,128)S(1)}, u32[]{:S(2)}, u32[]{:S(2)}) async-start(f32[4,80,640]{2,1,0:T(8,128)} %bitcast.14), calls=%async_computation.5 | async-start | bytes 1638400 | tf_op jit(solution)/shard_map/all_to_all | solution.py:112
  165.3 14.7 %collective-permute-start.3 = (bf16[80,640]{1,0:T(8,128)(2,1)S(1)}, bf16[80,640]{1,0:T(8,128)(2,1)S(1)}, u32[]{:S(2)}, u32[]{:S(2)}) collective-permute-start(bf16[80,640]{1,0:T(8,128)(2,1)S(1)} %reduce_sum.109), channel_id=1, source_target_pairs={{0,0},{2,128},{4,256},{6,384},{128,2},{130,130},{132,258},{134,386... | collective-permute-start | bytes 307208 | tf_op jit(solution)/shard_map/ppermute | solution.py:24
Sparse Core Ops, SparseCore 0:
  10.6 46.7 all-gather.9
  60.1 31.0 all-gather.7
  93.9 40.7 all-gather.5
